TPU v7x, 32 devices: a whole 2x2x4 slice. The times are simulated.
32 devices in a mesh: ctx: 8 (over y, x, core), exp: 4 (over z).
Axes of the slice: x: 2, y: 2, z: 4, core: 2. Of those that a mesh axis runs over, the one named last changes fastest.
Arguments:
- conv_input: bfloat16 [1024, 4096], P('ctx', 'exp'), may hold values from -6 to 6
- conv_weight: float32 [4, 4096], P(None, 'exp'), may hold values from -3 to 3
- b_proj: bfloat16 [1024, 128], P('ctx'), may hold values from -0.5 to 0.5
- c_proj: bfloat16 [1024, 128], P('ctx'), may hold values from -0.29882812 to 0.29882812
- log_decay: float32 [64, 1024], P('exp', 'ctx'), may hold values from -1 to 0
- skip_gain: float32 [64], P('exp'), may hold values from 0.5 to 1.5
- grad_in: bfloat16 [1024, 4096], P('ctx', 'exp'), may hold values from -6 to 6
- norm_gain: float32 [4096], replicated, may hold values from 0.1 to 1.9
- expert_ids: int32 [1024, 2], P('ctx'), may hold values from 0 to 3, all different within a row; in each aligned block of 32 rows (0 to 31, 32 to 63, ...) at most 24 rows name the same one
- expert_weights: float32 [1024, 2], P('ctx'), may hold values from 0.1 to 1
- up_weight: bfloat16 [4, 4096, 12288], P('exp', None, 'ctx'), may hold values from -0.09375 to 0.09375
- down_weight: bfloat16 [4, 12288, 4096], P('exp', 'ctx'), may hold values from -0.0546875 to 0.0546875
Outputs:
- moe_out: bfloat16 [1024, 4096], P('ctx', 'exp')
- grad_conv: float32 [1024, 4096], P('ctx', 'exp')
Inputs may be any that keep to these rules, and one draw needn't show every extreme that they name: `expert_ids`: each token names 2 different experts; in each aligned block of 32 tokens no expert is named more than 24 times.
All inputs are finite; a program needn't handle non-finite values.
Results may differ from a plain program's by a relative error of at most 0.018.
Values may be sent and summed in bfloat16 or wider, within the bound.
No kernel may reach another device: no remote copies, remote signals or barrier semaphores. Data moves between devices by JAX's collectives and lax.ppermute only.
A program may use at most 128 MiB of HBM per device.

v0:
```python
import jax
import jax.numpy as jnp
from jax import lax
from jax.sharding import PartitionSpec as P

CONV = 4
TOPK = 2


HIGHEST = lax.Precision.HIGHEST
EPSILON = 1e-06


def passed_along(block, axis, distance):
    devices = range(lax.axis_size(axis))
    route = [(i - distance, i) for i in devices if i - distance in devices]
    return lax.ppermute(block, axis, route)


def prefix(x, axis, combine, identity, reverse):
    size, mine = (lax.axis_size(axis), lax.axis_index(axis))
    everything = jax.tree.map(
        lambda part, kind: lax.all_gather(part.astype(kind), axis), x, (jnp.bfloat16, jnp.bfloat16)
    )
    start = jax.tree.map(
        lambda part, zero: jnp.broadcast_to(jnp.asarray(zero, part.dtype), part.shape), x, identity
    )

    def turn(k, before):
        at = size - 1 - k if reverse else k
        reached = at > mine if reverse else at < mine
        new = combine(
            before, jax.tree.map(lambda part, own: part[at].astype(own.dtype), everything, x)
        )
        return jax.tree.map(lambda a, b: jnp.where(reached, a, b), new, before)

    return lax.fori_loop(0, size, turn, start)


def combine_state(earlier, later):
    return (earlier[0] * later[0], later[0][:, None, None] * earlier[1] + later[1])


def conv_mix(extended, conv_weight):
    rows_out = extended.shape[0] - conv_weight.shape[0] + 1
    total = jnp.zeros((rows_out, extended.shape[1]), jnp.float32)
    for offset in range(conv_weight.shape[0]):
        total = total + conv_weight[offset][None, :] * extended[offset : offset + rows_out]
    return jax.nn.silu(total).astype(jnp.bfloat16)


def block_terms(decay_block, b_raw, c_raw):
    totals = jnp.cumsum(decay_block, axis=1)
    rows_here = totals.shape[1]
    causal = jnp.arange(rows_here)[:, None] >= jnp.arange(rows_here)[None, :]
    spread = jnp.where(causal[None], totals[:, :, None] - totals[:, None, :], 0.0)
    kernel = (
        jnp.where(causal[None], jnp.exp(spread), 0.0)
        * jnp.dot(c_raw, b_raw.T, preferred_element_type=jnp.float32)[None]
    )
    to_end = jnp.exp(totals[:, -1:] - totals)
    return (totals, kernel, to_end)


def normalize(rows_in, norm_gain):
    values = rows_in.astype(jnp.float32)
    scale = lax.rsqrt(jnp.mean(values * values, axis=1, keepdims=True) + EPSILON)
    return (values * scale * norm_gain[None, :]).astype(jnp.bfloat16)


def route_matrix(chosen_ids, slots_each, experts):
    pairs = chosen_ids.reshape(-1)
    onehot = (pairs[:, None] == jnp.arange(experts, dtype=jnp.int32)[None, :]).astype(jnp.int32)
    ranks = jnp.sum((jnp.cumsum(onehot, axis=0) - 1) * onehot, axis=1)
    target = pairs * slots_each + ranks
    return (jnp.arange(experts * slots_each, dtype=jnp.int32)[:, None] == target[None, :]).astype(
        jnp.bfloat16
    )


def gather_back(dispatch, returned, weights):
    values = jnp.einsum("sp,sc->pc", dispatch, returned, preferred_element_type=jnp.float32)
    values = values.reshape(weights.shape[0], weights.shape[1], returned.shape[1])
    return jnp.sum(weights[:, :, None] * values, axis=1).astype(jnp.bfloat16)


def expert_block(rows_in, up_weight, down_weight):
    up_local = up_weight[0]
    down_local = down_weight[0]
    hidden = jax.nn.silu(
        jnp.dot(
            lax.all_gather(rows_in, "ctx", axis=0, tiled=True),
            up_local,
            preferred_element_type=jnp.float32,
        )
    ).astype(jnp.bfloat16)
    summed = lax.psum_scatter(
        jnp.dot(hidden, down_local, preferred_element_type=jnp.float32).astype(jnp.bfloat16),
        "ctx",
        scatter_dimension=0,
        tiled=True,
    )
    return summed


def shards(
    conv_input,
    conv_weight,
    b_proj,
    c_proj,
    log_decay,
    skip_gain,
    grad_in,
    norm_gain,
    expert_ids,
    expert_weights,
    up_weight,
    down_weight,
):
    tok_rows = conv_input.shape[0]
    heads_here = log_decay.shape[0]
    head_size = conv_input.shape[1] // heads_here
    rim_rows = passed_along(conv_input[tok_rows - (CONV - 1) :], "ctx", 1)
    extended = jnp.concatenate(
        [rim_rows.astype(jnp.float32), conv_input.astype(jnp.float32)], axis=0
    )
    mixed_in = conv_mix(extended, conv_weight)
    inputs_block = mixed_in.astype(jnp.float32).reshape(tok_rows, heads_here, head_size)
    b_block = b_proj.astype(jnp.float32)
    c_block = c_proj.astype(jnp.float32)
    grad_block = grad_in.astype(jnp.float32).reshape(tok_rows, heads_here, head_size)
    totals, kernel, to_end = block_terms(log_decay, b_proj, c_proj)
    through = jnp.exp(totals[:, -1])
    local_state = jnp.einsum("hs,shp,sn->hpn", to_end, inputs_block, b_block, precision=HIGHEST)
    local_grad = jnp.einsum(
        "ht,thp,tn->hpn", jnp.exp(totals), grad_block, c_block, precision=HIGHEST
    )
    zero_state = jnp.zeros_like(local_state)
    ones_heads = jnp.ones_like(through)
    carry_state = prefix(
        (through, local_state), "ctx", combine_state, (ones_heads, zero_state), False
    )[1]
    carry_grad = prefix(
        (through, local_grad), "ctx", combine_state, (ones_heads, zero_state), True
    )[1]
    inner = jnp.einsum("hts,shp->thp", kernel, inputs_block, precision=HIGHEST)
    carried = jnp.exp(totals).T[:, :, None] * jnp.einsum(
        "hpn,tn->thp", carry_state, c_block, precision=HIGHEST
    )
    output = inner + carried + skip_gain[None, :, None] * inputs_block
    ssd_out = output.reshape(tok_rows, heads_here * head_size).astype(jnp.bfloat16)
    grad_inner = jnp.einsum("hts,thp->shp", kernel, grad_block, precision=HIGHEST)
    grad_carried = to_end.T[:, :, None] * jnp.einsum(
        "hpn,sn->shp", carry_grad, b_block, precision=HIGHEST
    )
    grad_conv = (grad_inner + grad_carried + skip_gain[None, :, None] * grad_block).reshape(
        tok_rows, heads_here * head_size
    )
    experts = lax.axis_size("exp")
    most_rows = 3 * TOPK * tok_rows // (2 * experts * experts)
    share = tok_rows // experts
    token_view = lax.all_to_all(ssd_out, "exp", split_axis=0, concat_axis=1, tiled=True)
    normed = normalize(token_view, norm_gain)
    first_row = lax.axis_index("exp") * share
    my_ids = lax.dynamic_slice_in_dim(expert_ids, first_row, share, 0)
    my_weights = lax.dynamic_slice_in_dim(expert_weights, first_row, share, 0)
    dispatch = route_matrix(my_ids, most_rows, experts)
    outgoing = jnp.dot(
        dispatch, jnp.repeat(normed, TOPK, axis=0), preferred_element_type=jnp.float32
    ).astype(jnp.bfloat16)
    incoming = lax.all_to_all(
        outgoing.reshape(experts, most_rows, normed.shape[1]),
        "exp",
        split_axis=0,
        concat_axis=0,
        tiled=True,
    )
    results = expert_block(
        incoming.reshape(experts * most_rows, normed.shape[1]), up_weight, down_weight
    )
    returned = lax.all_to_all(
        results.reshape(experts, most_rows, normed.shape[1]),
        "exp",
        split_axis=0,
        concat_axis=0,
        tiled=True,
    )
    combined = gather_back(
        dispatch, returned.reshape(experts * most_rows, normed.shape[1]), my_weights
    )
    moe_out = lax.all_to_all(combined, "exp", split_axis=1, concat_axis=0, tiled=True)
    return (moe_out, grad_conv)


def solution(mesh):
    placed = (
        P("ctx", "exp"),
        P(None, "exp"),
        P("ctx", None),
        P("ctx", None),
        P("exp", "ctx"),
        P("exp"),
        P("ctx", "exp"),
        P(),
        P("ctx", None),
        P("ctx", None),
        P("exp", None, "ctx"),
        P("exp", "ctx", None),
    )
    return jax.shard_map(
        shards,
        mesh=mesh,
        in_specs=placed,
        out_specs=(P("ctx", "exp"), P("ctx", "exp")),
        check_vma=False,
    )
```

profile of v0, /device:TPU:0, one launch (start us, length us, event | category | flops | bytes accessed | tf_op | source)
XLA Modules:
  0.0 299.9 jit_solution(15138509072731504501)
XLA Ops:
  7.2 0.7 slice.29
  8.0 2.3 collective-permute-start
  10.3 0.9 fusion.53
  11.2 1.0 reduce_window_sum.23
  12.5 1.0 convert_element_type.132
  14.0 1.9 convolution_convert_fusion.2
  15.9 1.2 dynamic-slice
  18.3 14.5 %all-reduce = bf16[128]{0:T(256)(128)(2,1)S(1)} all-reduce(bf16[128]{0:T(256)(128)(2,1)S(1)} %dynamic-update-slice), channel_id=2, replica_groups=mesh['ctx'=8,'exp'=4] {'ctx'}, use_global_device_ids=true, to_apply=%add | all-reduce | flops 128 | bytes 512
  32.8 0.8 constant_dynamic-slice_fusion
  33.8 0.9 fusion.54
  34.8 11.8 %all-gather.9.cloned.1.call-done = bf16[128,64,128]{2,1,0:T(8,128)(2,1)} async-done(((bf16[16,64,128]{2,1,0:T(8,128)(2,1)}), bf16[128,64,128]{2,1,0:T(8,128)(2,1)}) %all-gather.9.cloned.1.call-update) | async-done | bytes 2097168 | tf_op jit(solution)/shard_map/all_gather | solution.py:23
  46.6 9.1 %while.30 = (s32[]{:T(128)}, f32[16,64,128]{2,1,0:T(8,128)S(1)}, s32[]{:T(128)}, bf16[8,16]{1,0:T(8,128)(2,1)S(1)}, bf16[8,16,64,128]{3,2,1,0:T(8,128)(2,1)}, /*index=5*/s32[]{:T(128)}, s32[]{:T(128)}) while((s32[]{:T(128)}, f32[16,64,128]{2,1,0:T(8,128)S(1)}, s32[]{:T(128)}, bf16[8,16]{1,0:T(8,128)(2,1)S(1)}, ...), condition=%wide.region_4.5_spmd.clone, body=%wide.region_3.4_spmd.clone.sunk | while | flops 655380 | bytes 1310985 | solution.py:37
  46.6 1.1 fusion.66
  47.7 1.1 fusion.66
  48.8 1.1 fusion.66
  50.0 1.1 fusion.66
  51.1 1.1 fusion.66
  52.3 1.1 fusion.66
  53.4 1.1 fusion.66
  54.5 1.1 fusion.66
  56.0 1.3 fusion.20
  57.8 1.1 convert_element_type.138
  58.8 4.6 %all-to-all-start = ((bf16[4,32,1024]{2,1,0:T(8,128)(2,1)}), bf16[4,32,1024]{2,1,0:T(8,128)(2,1)S(1)}, u32[]{:S(2)}, u32[]{:S(2)}) async-start(bf16[4,32,1024]{2,1,0:T(8,128)(2,1)} %convert_element_type.138), calls=%async_computation | async-start | bytes 524288 | tf_op jit(solution)/shard_map/all_to_all | solution.py:162
  63.8 8.9 %all-to-all-done = bf16[4,32,1024]{2,1,0:T(8,128)(2,1)S(1)} async-done(((bf16[4,32,1024]{2,1,0:T(8,128)(2,1)}), bf16[4,32,1024]{2,1,0:T(8,128)(2,1)S(1)}, u32[]{:S(2)}, u32[]{:S(2)}) %all-to-all-start) | async-done | bytes 262176 | tf_op jit(solution)/shard_map/all_to_all | solution.py:162
  74.2 22.0 %all_to_all.36 = bf16[4,24,4096]{2,1,0:T(8,128)(2,1)} all-to-all(bf16[4,24,4096]{2,1,0:T(8,128)(2,1)S(1)} %bitcast.106), channel_id=1, replica_groups=mesh['ctx'=8,'exp'=4] {'exp'}, dimensions={0} | all-to-all | bytes 1572864 | tf_op jit(solution)/shard_map/all_to_all | solution.py:171
  96.5 43.6 %all-gather.7.cloned.1.call-done = bf16[768,4096]{1,0:T(8,128)(2,1)} async-done(((bf16[96,4096]{1,0:T(8,128)(2,1)}), bf16[768,4096]{1,0:T(8,128)(2,1)}) %all-gather.7.cloned.1.call-update) | async-done | bytes 6291472 | tf_op jit(solution)/shard_map/all_gather | solution.py:92
  140.1 30.9 %fusion.6 = bf16[768,4096]{1,0:T(8,128)(2,1)} fusion(bf16[1,1536,4096]{2,1,0:T(8,128)(2,1)} %param.27, bf16[768,4096]{1,0:T(8,128)(2,1)} %all-gather.7.cloned.1.call-done, bf16[1,4096,1536]{2,1,0:T(8,128)(2,1)} %param.26), kind=kOutput, calls=%fused_computation.10 | convolution fusion | flops 19336396800 | bytes 37748736 | tf_op jit(solution)/shard_map/dot_general | solution.py:98
  171.1 0.8 copy-done.2
  172.2 1.1 convolution_convert_fusion.1
  173.5 59.4 %reduce-scatter.2.cloned.1.call-done = bf16[96,4096]{1,0:T(8,128)(2,1)} async-done(((bf16[768,4096]{1,0:T(8,128)(2,1)}), bf16[96,4096]{1,0:T(8,128)(2,1)}) %reduce-scatter.2.cloned.1.call-update) | async-done | bytes 786448 | tf_op jit(solution)/shard_map/reduce_scatter | solution.py:97
  232.9 4.6 %all-to-all-start.2 = ((bf16[4,24,4096]{2,1,0:T(8,128)(2,1)}), bf16[4,24,4096]{2,1,0:T(8,128)(2,1)S(1)}, u32[]{:S(2)}, u32[]{:S(2)}) async-start(bf16[4,24,4096]{2,1,0:T(8,128)(2,1)} %bitcast.116), calls=%async_computation.3 | async-start | bytes 1572864 | tf_op jit(solution)/shard_map/all_to_all | solution.py:181
  237.5 25.8 %all-gather.11.cloned.1.call-done = bf16[128,64,128]{2,1,0:T(8,128)(2,1)} async-done(((bf16[16,64,128]{2,1,0:T(8,128)(2,1)}), bf16[128,64,128]{2,1,0:T(8,128)(2,1)}) %all-gather.11.cloned.1.call-update) | async-done | bytes 2097168 | tf_op jit(solution)/shard_map/all_gather | solution.py:23
  263.3 14.4 %while.31 = (s32[]{:T(128)}, f32[16,64,128]{2,1,0:T(8,128)S(1)}, s32[]{:T(128)}, bf16[8,16]{1,0:T(8,128)(2,1)}, bf16[8,16,64,128]{3,2,1,0:T(8,128)(2,1)}, /*index=5*/s32[]{:T(128)}, s32[]{:T(128)}, s32[]{:T(128)}, s32[]{:T(128)}) while((s32[]{:T(128)}, f32[16,64,128]{2,1,0:T(8,128)S(1)}, s32[]{:T(128)}, bf16[8,16]{1,0:T(8,128)(2,1)}, ...), condition=%wide.region_9.10_spmd.clone, body=%wide.region_8.9_spmd.clone.sunk | while | flops 655384 | bytes 1311047 | solution.py:37
  264.0 1.1 fusion.67
  265.1 0.7 bitcast_convert_fusion.5
  265.8 1.1 fusion.67
  267.6 1.1 fusion.67
  269.4 1.1 fusion.67
  271.2 1.1 fusion.67
  273.0 1.1 fusion.67
  274.8 1.1 fusion.67
  276.6 1.1 fusion.67
  278.0 0.7 copy.46
  278.7 4.6 %all-to-all-start.3 = ((bf16[32,4,1024]{2,0,1:T(8,128)(2,1)}), bf16[32,4,1024]{2,0,1:T(8,128)(2,1)S(1)}, u32[]{:S(2)}, u32[]{:S(2)}) async-start(bf16[32,4,1024]{2,0,1:T(8,128)(2,1)} %bitcast.95), calls=%async_computation.4 | async-start | bytes 524288 | tf_op jit(solution)/shard_map/all_to_all | solution.py:191
  283.7 0.9 fusion.15
  284.6 1.0 copy.40
  285.6 7.0 %all-to-all-done.3 = bf16[32,4,1024]{2,0,1:T(8,128)(2,1)S(1)} async-done(((bf16[32,4,1024]{2,0,1:T(8,128)(2,1)}), bf16[32,4,1024]{2,0,1:T(8,128)(2,1)S(1)}, u32[]{:S(2)}, u32[]{:S(2)}) %all-to-all-start.3) | async-done | bytes 262176 | tf_op jit(solution)/shard_map/all_to_all | solution.py:191
  292.6 0.7 copy.61
  (98 shorter events, 10.4 us)
Async XLA Ops:
  7.2 26.7 %copy-start = (bf16[128,128]{1,0:T(8,128)(2,1)S(1)}, bf16[128,128]{1,0:T(8,128)(2,1)}, u32[]{:S(2)}) copy-start(bf16[128,128]{1,0:T(8,128)(2,1)} %param.19) | copy-start | bytes 98308
  7.2 48.9 %copy-start.18 = (f32[16]{0:T(128)S(1)}, f32[16]{0:T(128)}, u32[]{:S(2)}) copy-start(f32[16]{0:T(128)} %param.21) | copy-start | bytes 196
  7.2 39.4 %all-gather.9.cloned.1.call-start = ((), (), s32[]{:S(2)}) async-start(), calls=%async_computation.7 | async-start | bytes 2359296 | tf_op jit(solution)/shard_map/all_gather | solution.py:23
  8.0 5.5 %collective-permute-start = (bf16[3,1024]{1,0:T(4,128)(2,1)S(1)}, bf16[3,1024]{1,0:T(4,128)(2,1)S(1)}, u32[]{:S(2)}, u32[]{:S(2)}) collective-permute-start(bf16[3,1024]{1,0:T(4,128)(2,1)S(1)} %slice.29), channel_id=1, source_target_pairs={{0,4},{4,8},{8,12},{12,16},{16,20},{20,24},{24,28},{1,5},{5,9},{9,... | collective-permute-start | bytes 18440 | tf_op jit(solution)/shard_map/ppermute | solution.py:17
  12.2 45.1 %copy-start.3 = (f32[16,128]{1,0:T(8,128)}, f32[16,128]{1,0:T(8,128)S(1)}, u32[]{:S(2)}) copy-start(f32[16,128]{1,0:T(8,128)S(1)} %reduce_window_sum.23) | copy-start | bytes 24580
  12.4 3.5 %copy-start.5 = (f32[128,16]{0,1:T(8,128)}, f32[128,16]{0,1:T(8,128)S(1)}, u32[]{:S(2)}) copy-start(f32[128,16]{0,1:T(8,128)S(1)} %get-tuple-element.299) | copy-start | bytes 24580
  12.4 44.9 %copy-start.7 = (f32[128,16]{0,1:T(8,128)}, f32[128,16]{0,1:T(8,128)S(1)}, u32[]{:S(2)}) copy-start(f32[128,16]{0,1:T(8,128)S(1)} %get-tuple-element.298) | copy-start | bytes 24580
  33.8 29.8 %copy-start.12 = (pred[128,128]{1,0:T(8,128)(4,1)}, pred[128,128]{1,0:T(8,128)(4,1)S(1)}, u32[]{:S(2)}) copy-start(pred[128,128]{1,0:T(8,128)(4,1)S(1)} %iota_compare_fusion) | copy-start | bytes 49156
  34.8 38.1 %copy-start.9 = (f32[128,128]{1,0:T(8,128)}, f32[128,128]{1,0:T(8,128)S(1)}, u32[]{:S(2)}) copy-start(f32[128,128]{1,0:T(8,128)S(1)} %fusion.54) | copy-start | bytes 196612
  46.6 26.5 %copy-start.11 = (f32[4096]{0:T(1024)S(1)}, f32[4096]{0:T(1024)}, u32[]{:S(2)}) copy-start(f32[4096]{0:T(1024)} %param.23) | copy-start | bytes 49156
  55.6 17.4 %copy-start.16 = (bf16[8,16]{1,0:T(8,128)(2,1)}, bf16[8,16]{1,0:T(8,128)(2,1)S(1)}, u32[]{:S(2)}) copy-start(bf16[8,16]{1,0:T(8,128)(2,1)S(1)} %get-tuple-element.436) | copy-start | bytes 772
  58.8 13.9 %all-to-all-start = ((bf16[4,32,1024]{2,1,0:T(8,128)(2,1)}), bf16[4,32,1024]{2,1,0:T(8,128)(2,1)S(1)}, u32[]{:S(2)}, u32[]{:S(2)}) async-start(bf16[4,32,1024]{2,1,0:T(8,128)(2,1)} %convert_element_type.138), calls=%async_computation | async-start | bytes 524288 | tf_op jit(solution)/shard_map/all_to_all | solution.py:162
  63.4 76.6 %all-gather.7.cloned.1.call-start = ((), (), s32[]{:S(2)}) async-start(), calls=%async_computation.5 | async-start | bytes 7077888 | tf_op jit(solution)/shard_map/all_gather | solution.py:92
  63.8 107.2 %copy-start.14 = (s32[64]{0:T(128)}, s32[64]{0:T(128)S(1)}, u32[]{:S(2)}) copy-start(s32[64]{0:T(128)S(1)} %multiply_add_fusion) | copy-start | bytes 772
  96.2 136.7 %reduce-scatter.2.cloned.1.call-start = ((), (), s32[]{:S(2)}) async-start(), calls=%async_computation.6 | async-start | bytes 7077888 | tf_op jit(solution)/shard_map/reduce_scatter | solution.py:97
  171.0 1.0 copy-start.2
  171.0 1.2 copy-start.8
  171.0 2.4 copy-start.17
  171.0 2.3 copy-start.15
  171.0 112.3 %copy-start.1 = (bf16[128,128]{1,0:T(8,128)(2,1)S(1)}, bf16[128,128]{1,0:T(8,128)(2,1)}, u32[]{:S(2)}) copy-start(bf16[128,128]{1,0:T(8,128)(2,1)} %param.18) | copy-start | bytes 98308
  171.0 112.3 %copy-start.6 = (f32[128,16]{0,1:T(8,128)S(1)}, f32[128,16]{0,1:T(8,128)}, u32[]{:S(2)}) copy-start(f32[128,16]{0,1:T(8,128)} %copy-done.5) | copy-start | bytes 24580
  171.1 92.3 %all-gather.11.cloned.1.call-start = ((), (), s32[]{:S(2)}) async-start(), calls=%async_computation.8 | async-start | bytes 2359296 | tf_op jit(solution)/shard_map/all_gather | solution.py:23
  172.1 111.6 %copy-start.4 = (f32[16,128]{1,0:T(8,128)S(1)}, f32[16,128]{1,0:T(8,128)}, u32[]{:S(2)}) copy-start(f32[16,128]{1,0:T(8,128)} %copy-done.3) | copy-start | bytes 24580
  172.1 111.6 %copy-start.10 = (f32[128,128]{1,0:T(8,128)S(1)}, f32[128,128]{1,0:T(8,128)}, u32[]{:S(2)}) copy-start(f32[128,128]{1,0:T(8,128)} %copy-done.9) | copy-start | bytes 196612
  172.1 111.6 %copy-start.13 = (pred[128,128]{1,0:T(8,128)(4,1)S(1)}, pred[128,128]{1,0:T(8,128)(4,1)}, u32[]{:S(2)}) copy-start(pred[128,128]{1,0:T(8,128)(4,1)} %copy-done.12) | copy-start | bytes 49156
  172.1 111.6 %copy-start.19 = (f32[16]{0:T(128)S(1)}, f32[16]{0:T(128)}, u32[]{:S(2)}) copy-start(f32[16]{0:T(128)} %param.21) | copy-start | bytes 196
  232.9 44.8 %all-to-all-start.2 = ((bf16[4,24,4096]{2,1,0:T(8,128)(2,1)}), bf16[4,24,4096]{2,1,0:T(8,128)(2,1)S(1)}, u32[]{:S(2)}, u32[]{:S(2)}) async-start(bf16[4,24,4096]{2,1,0:T(8,128)(2,1)} %bitcast.116), calls=%async_computation.3 | async-start | bytes 1572864 | tf_op jit(solution)/shard_map/all_to_all | solution.py:181
  278.7 13.9 %all-to-all-start.3 = ((bf16[32,4,1024]{2,0,1:T(8,128)(2,1)}), bf16[32,4,1024]{2,0,1:T(8,128)(2,1)S(1)}, u32[]{:S(2)}, u32[]{:S(2)}) async-start(bf16[32,4,1024]{2,0,1:T(8,128)(2,1)} %bitcast.95), calls=%async_computation.4 | async-start | bytes 524288 | tf_op jit(solution)/shard_map/all_to_all | solution.py:191
Sparse Core Ops, SparseCore 0:
  16.0 30.4 all-gather.8
  96.4 43.6 all-gather.6
  171.1 61.7 reduce-scatter.1
  235.4 27.8 all-gather.10
where the time goes:
time: 301 us; the launch traced here: 300 us
  waiting for transfers between devices  157 us (52%)
  matrix products  38.4 us (13%)
  blocking collectives  36.5 us (12%)
  other arithmetic  26.4 us (9%)
  starting transfers between devices  16.4 us (5%)
  between operations  14.9 us (5%)
  local copies, waits for them, and re-layouts  10.3 us (3%)
    reduce_scatter x1, waiting for transfers between devices, expert_block(): lax.psum_scatter(jnp.dot(hidden, down_local, preferred_element_type=jnp.f...  59.4 us
    all_gather x1, waiting for transfers between devices, expert_block(): lax.all_gather(rows_in, 'ctx', axis=0, tiled=True)  43.6 us
    all_gather x2, waiting for transfers between devices, prefix(): lax.all_gather(part.astype(kind), axis)  37.6 us
    dot_general x1, matrix products, expert_block(): jnp.dot(hidden, down_local, preferred_element_type=jnp.float32)  30.9 us
    all_to_all x1, blocking collectives, shards(): lax.all_to_all(outgoing.reshape(experts, most_rows, normed.shape[1]), 'ex...  22 us
    select_n x16, other arithmetic, turn(): return jax.tree.map(lambda a, b: jnp.where(reached, a, b), new, before)  17.5 us
    unnamed x1, blocking collectives  14.5 us
    all_to_all x1, waiting for transfers between devices, shards(): lax.all_to_all(ssd_out, 'exp', split_axis=0, concat_axis=1, tiled=True)  8.94 us
  transfers between devices with their start and end apart: 8, of which 6 were waited for; matrix products, arithmetic and copies ran while one was open for 8% of the time, Pallas kernels for 0%

commit v1 on v0

--- a/solution.py
+++ b/solution.py
@@ -1,6 +1,8 @@
 import jax
 import jax.numpy as jnp
 from jax import lax
+from jax.experimental import pallas as pl
+from jax.experimental.pallas import tpu as pltpu
 from jax.sharding import PartitionSpec as P
 
 CONV = 4
@@ -103,7 +105,7 @@
     return summed
 
 
-def shards(
+def general_shards(
     conv_input,
     conv_weight,
     b_proj,
@@ -192,6 +194,449 @@
     return (moe_out, grad_conv)
 
 
+CHUNKS = 2
+DECAY_ROWS = 16
+RIM = 8
+F32 = jnp.float32
+BF16 = jnp.bfloat16
+
+
+def shape_of(shape, dtype):
+    return jax.ShapeDtypeStruct(shape, dtype)
+
+
+def call(body, outs, smem=0, scratch=(), cost=None, limit=40):
+    def run(*args):
+        specs = [pl.BlockSpec(memory_space=pltpu.SMEM)] * smem
+        specs += [pl.BlockSpec(memory_space=pltpu.VMEM)] * (len(args) - smem)
+        return pl.pallas_call(
+            body,
+            out_shape=outs,
+            in_specs=specs,
+            out_specs=jax.tree.map(lambda _: pl.BlockSpec(memory_space=pltpu.VMEM), outs),
+            scratch_shapes=scratch,
+            cost_estimate=cost,
+            compiler_params=pltpu.CompilerParams(vmem_limit_bytes=limit << 20),
+        )(*args)
+
+    return run
+
+
+def swap(x, axis, mask):
+    size = lax.axis_size(axis)
+    return lax.ppermute(x, axis, [(i, i ^ mask) for i in range(size)])
+
+
+def exact_dot(a, b, dims=(((1,), (0,)), ((), ()))):
+    return lax.dot_general(a, b, dims, precision=HIGHEST, preferred_element_type=F32)
+
+
+def fast_dot(a, b):
+    return jnp.dot(a, b, preferred_element_type=F32)
+
+
+def iota(shape, dim):
+    return lax.broadcasted_iota(jnp.int32, shape, dim)
+
+
+def decay_columns(decay):
+    rows = decay.shape[1]
+    tri = (iota((rows, rows), 0) >= iota((rows, rows), 1)).astype(F32)
+    return exact_dot(tri, decay, (((1,), (1,)), ((), ())))
+
+
+def mix_kernel(core, conv, rim, taps, b, c, decay, grad, mixed_out, sent, kept, grow, fade):
+    heads = decay.shape[0]
+    rows, lanes = conv.shape
+    x = conv[...].astype(F32)
+    extended = jnp.concatenate([rim[...].astype(F32), x], axis=0)
+    total = jnp.zeros((rows, lanes), F32)
+    for tap in range(CONV):
+        start = RIM - (CONV - 1) + tap
+        total = total + taps[tap : tap + 1, :] * extended[start : start + rows]
+    mixed = (total * jax.nn.sigmoid(total)).astype(BF16)
+    mixed_out[...] = mixed
+    columns = decay_columns(decay[...])
+    width = lanes // heads
+    spread = (iota((heads, lanes), 1) // width == iota((heads, lanes), 0)).astype(F32)
+    totals = exact_dot(columns, spread)
+    last = totals[rows - 1 : rows, :]
+    growing = jnp.exp(totals)
+    fading = jnp.exp(last - totals)
+    grow[...] = growing
+    fade[...] = fading
+    through = jnp.broadcast_to(jnp.exp(last), (DECAY_ROWS, lanes)).astype(BF16)
+    states = b.shape[1]
+    forward = fast_dot(b[...].T, (fading * mixed.astype(F32)).astype(BF16)).astype(BF16)
+    backward = fast_dot(c[...].T, (growing * grad[...].astype(F32)).astype(BF16)).astype(BF16)
+    first = core[0] == 0
+    sent[0:states, :] = jnp.where(first, forward, backward)
+    kept[0:states, :] = jnp.where(first, backward, forward)
+    sent[states:, :] = through
+    kept[states:, :] = through
+
+
+def pair_kernel(received, kept, chip):
+    states = kept.shape[0] - DECAY_ROWS
+    decay = kept[states : states + 1, :].astype(F32)
+    got = received[0:states, :].astype(F32)
+    chip[0:states, :] = (got * decay + kept[0:states, :].astype(F32)).astype(BF16)
+    both = decay * received[states : states + 1, :].astype(F32)
+    chip[states:, :] = jnp.broadcast_to(both, (DECAY_ROWS, both.shape[1])).astype(BF16)
+
+
+def reach_kernel(flip, near, middle, far, mine):
+    states = mine.shape[0]
+    flipped = flip[0] != 0
+
+    def part(ref):
+        return ref[0:states, :].astype(F32), ref[states : states + 1, :].astype(F32)
+
+    a, a_decay = part(near)
+    b, b_decay = part(middle)
+    c, c_decay = part(far)
+    first, first_decay = jnp.where(flipped, c, a), jnp.where(flipped, c_decay, a_decay)
+    third = jnp.where(flipped, a, c)
+    mine[...] = (first + first_decay * (b + b_decay * third)).astype(BF16)
+
+
+def inner_kernel(mixed, b, c, decay, grad, skip, out, grad_out):
+    heads, rows = decay.shape
+    lanes = mixed.shape[1]
+    width = lanes // heads
+    pack = 128 // width
+    columns = decay_columns(decay[...])
+    tri_rows = (iota((rows, rows), 0) <= iota((rows, rows), 1)).astype(F32)
+    totals = exact_dot(decay[...], tri_rows)
+    nt = (((1,), (1,)), ((), ()))
+    scores = lax.dot_general(c[...], b[...], nt, preferred_element_type=F32)
+    flipped = lax.dot_general(b[...], c[...], nt, preferred_element_type=F32)
+    t, s = iota((rows, rows), 0), iota((rows, rows), 1)
+    spread = (iota((heads, lanes), 1) // width == iota((heads, lanes), 0)).astype(F32)
+    gains = exact_dot(skip[...], spread)
+    lane = iota((rows, 128), 1) // width
+    for group in range(lanes // 128):
+        at = slice(group * 128, group * 128 + 128)
+        x = mixed[:, at]
+        g = grad[:, at]
+        left, right, xs, gs = [], [], [], []
+        for k in range(pack):
+            h = group * pack + k
+            gap = columns[:, h : h + 1] - totals[h : h + 1, :]
+            left.append((jnp.exp(jnp.where(t >= s, gap, -1e30)) * scores).astype(BF16))
+            right.append((jnp.exp(jnp.where(t <= s, -gap, -1e30)) * flipped).astype(BF16))
+            xs.append(jnp.where(lane == k, x, jnp.zeros_like(x)))
+            gs.append(jnp.where(lane == k, g, jnp.zeros_like(g)))
+        gain = gains[0:1, at]
+        out[:, at] = fast_dot(jnp.concatenate(left, 1), jnp.concatenate(xs, 0)) + gain * x.astype(F32)
+        grad_out[:, at] = fast_dot(jnp.concatenate(right, 1), jnp.concatenate(gs, 0)) + gain * g.astype(F32)
+
+
+def choices(ids, mine, masks, rows, chunks):
+    named = []
+    for mask in range(masks):
+        wanted = mine ^ mask
+        named.append(((ids[0:1, :] == wanted) | (ids[1:2, :] == wanted)).astype(F32))
+    named.append(jnp.zeros((8 - masks, rows), F32))
+    names = jnp.concatenate(named, axis=0)
+    before, after = iota((rows, rows), 0), iota((rows, rows), 1)
+    share = rows // chunks
+    tri = ((before <= after) & (before // share == after // share)).astype(BF16)
+    return names, fast_dot(names.astype(BF16), tri).astype(jnp.int32)
+
+
+def carry_kernel(core, mine, shared, prefix, received, inner, grow, c, ids, *outs):
+    chunks, masks = len(outs) // N_MASKS, N_MASKS
+    states, lanes = prefix.shape
+    rows = inner.shape[0]
+    own = carried(prefix, received)
+    carry = jnp.where(core[0] != 0, own, shared[...].astype(F32))
+    out = inner[...] + grow[...] * fast_dot(c[...], carry.astype(BF16))
+    out = out.astype(BF16)
+    names, counts = choices(ids[...], mine[0], masks, rows, chunks)
+    slots = outs[0].shape[0]
+    chunk_of = iota((slots, rows), 1) // (rows // chunks)
+    slot = iota((slots, rows), 0)
+    for chunk in range(chunks):
+        for mask in range(masks):
+            row = (counts[mask : mask + 1, :] - 1 == slot) & (names[mask : mask + 1, :] > 0)
+            pick = (row & (chunk_of == chunk)).astype(BF16)
+            outs[chunk * masks + mask][...] = fast_dot(pick, out).astype(BF16)
+
+
+def carried(prefix, received):
+    states = prefix.shape[0]
+    decay = received[states : states + 1, :].astype(F32)
+    return prefix[...].astype(F32) * decay + received[0:states, :].astype(F32)
+
+
+def grad_kernel(core, shared, prefix, received, inner, fade, b, out):
+    own = carried(prefix, received)
+    carry = jnp.where(core[0] != 0, shared[...].astype(F32), own)
+    out[...] = inner[...] + fade[...] * fast_dot(b[...], carry.astype(BF16))
+
+
+N_MASKS = 4
+
+
+def norm_kernel(mine, gain, *refs):
+    parts, out = refs[:-1], refs[-1]
+    width = parts[0].shape[1]
+    features = width * len(parts)
+    values = [part[...].astype(F32) for part in parts]
+    squares = sum(jnp.sum(v * v, axis=1, keepdims=True) for v in values)
+    scale = lax.rsqrt(squares / features + EPSILON)
+    per_half = len(parts) // 2
+    for mask, value in enumerate(values):
+        at = mine[0] ^ mask
+        to = pl.multiple_of((at % per_half) * width, width)
+        gains = gain[:, pl.ds(pl.multiple_of(at * width, width), width)]
+        out[at // per_half, :, pl.ds(to, width)] = (value * scale * gains).astype(BF16)
+
+
+def ffn_kernel(n_up, split, *refs):
+    blocks, (up, down, even, odd, rows_in, hidden, sems) = refs[:-7], refs[-7:]
+    step = pl.program_id(0)
+    slots = blocks[0].shape[-2]
+    half = rows_in.shape[1] // 2
+
+    @pl.when(step == 0)
+    def _():
+        copies = []
+        for n, (place, part) in enumerate(split):
+            at = rows_in.at[pl.ds(place * slots, slots)]
+            if part is None:
+                for side in range(2):
+                    copies.append(
+                        pltpu.make_async_copy(
+                            blocks[n].at[side], at.at[:, pl.ds(side * half, half)], sems.at[len(copies)]
+                        )
+                    )
+            else:
+                copies.append(
+                    pltpu.make_async_copy(
+                        blocks[n], at.at[:, pl.ds(part * half, half)], sems.at[len(copies)]
+                    )
+                )
+        for copy in copies:
+            copy.start()
+        for copy in copies:
+            copy.wait()
+
+    @pl.when(step < n_up)
+    def _():
+        value = fast_dot(rows_in[...], up[...])
+        width = up.shape[1]
+        to = pl.multiple_of(step * width, width)
+        hidden[:, pl.ds(to, width)] = (value * jax.nn.sigmoid(value)).astype(BF16)
+
+    @pl.when(step >= n_up)
+    def _():
+        value = fast_dot(hidden[...], down[...]).astype(BF16)
+        count = even.shape[0] * slots
+        even[...] = value[:count].reshape(even.shape)
+        odd[...] = value[count:].reshape(odd.shape)
+
+
+UP_TILE = 256
+DOWN_TILE = 512
+
+
+def expert_rows(blocks, split, places, up, down):
+    slots, half = blocks[0].shape[-2:]
+    features, hidden = up.shape
+    n_up, n_down = hidden // UP_TILE, features // DOWN_TILE
+    per_half = half // DOWN_TILE
+    rows = places * slots
+
+    def out_at(i):
+        j = jnp.maximum(i - n_up, 0)
+        return (0, j // per_half, 0, j % per_half)
+
+    spec = pl.BlockSpec((places // 2, None, slots, DOWN_TILE), out_at)
+    n_copies = sum(2 if part is None else 1 for _, part in split)
+    return pl.pallas_call(
+        lambda *refs: ffn_kernel(n_up, split, *refs),
+        grid=(n_up + n_down,),
+        in_specs=[pl.BlockSpec(memory_space=pl.ANY)] * len(blocks)
+        + [
+            pl.BlockSpec((features, UP_TILE), lambda i: (0, jnp.minimum(i, n_up - 1))),
+            pl.BlockSpec((hidden, DOWN_TILE), lambda i: (0, jnp.maximum(i - n_up, 0))),
+        ],
+        out_specs=[spec, spec],
+        out_shape=[shape_of((places // 2, 2, slots, half), BF16)] * 2,
+        scratch_shapes=[
+            pltpu.VMEM((rows, features), BF16),
+            pltpu.VMEM((rows, hidden), BF16),
+            pltpu.SemaphoreType.DMA((n_copies,)),
+        ],
+        cost_estimate=pl.CostEstimate(
+            flops=4 * rows * features * hidden,
+            transcendentals=rows * hidden,
+            bytes_accessed=4 * features * hidden + 4 * rows * features,
+        ),
+        compiler_params=pltpu.CompilerParams(
+            dimension_semantics=("arbitrary",), vmem_limit_bytes=48 << 20
+        ),
+    )(*blocks, up, down)
+
+
+def both(a, b):
+    return (a.astype(F32) + b.astype(F32)).astype(BF16)
+
+
+def chip_sum_kernel(even, other, own, to_x, to_y, rest_x, rest_y):
+    own[...] = both(even[0], other[0])
+    to_x[0] = both(even[3, 0], other[3, 0])
+    to_y[0] = both(even[3, 1], other[3, 1])
+    to_x[1] = both(even[1, 0], other[1, 0])
+    to_y[1] = both(even[2, 1], other[2, 1])
+    rest_x[...] = both(even[1, 1], other[1, 1])
+    rest_y[...] = both(even[2, 0], other[2, 0])
+
+
+def relay_kernel(from_x, from_y, rest_x, rest_y, next_x, next_y):
+    next_x[...] = both(rest_x[...], from_y[0])
+    next_y[...] = both(rest_y[...], from_x[0])
+
+
+def total_kernel(mine, own, from_x, from_y, last_x, last_y, *refs):
+    outs, total = refs[:-1], refs[-1]
+    width = outs[0].shape[1]
+    per_half = len(outs) // 2
+
+    def add(a, b, c):
+        return (a.astype(F32) + b.astype(F32) + c.astype(F32)).astype(BF16)
+
+    total[0] = add(own[0], from_x[1], last_y[...])
+    total[1] = add(own[1], last_x[...], from_y[1])
+    for mask, out in enumerate(outs):
+        at = mine[0] ^ mask
+        to = pl.multiple_of((at % per_half) * width, width)
+        out[...] = total[at // per_half, :, pl.ds(to, width)]
+
+
+def combine_kernel(mine, ids, weights, *refs):
+    parts, out = refs[:-1], refs[-1]
+    masks = N_MASKS
+    chunks = len(parts) // masks
+    slots = parts[0].shape[0]
+    rows = out.shape[0]
+    chosen = ids[...]
+    names, counts = choices(chosen, mine[0], masks, rows, chunks)
+    chunk_of = iota((slots, rows), 1) // (rows // chunks)
+    slot = iota((slots, rows), 0)
+    values = jnp.concatenate([part[...] for part in parts], axis=0)
+    result = jnp.zeros(out.shape, F32)
+    for k in range(TOPK):
+        picks = []
+        for chunk in range(chunks):
+            for mask in range(masks):
+                row = (counts[mask : mask + 1, :] - 1 == slot) & (chosen[k : k + 1, :] == mine[0] ^ mask)
+                picks.append((row & (chunk_of == chunk)).astype(F32))
+        pick = jnp.concatenate(picks, axis=0).T.astype(BF16)
+        result = result + weights[:, k : k + 1] * fast_dot(pick, values)
+    out[...] = result.astype(BF16)
+
+
+def directed(x, mask):
+    size = lax.axis_size("ctx")
+    route = []
+    for i in range(size):
+        j = i ^ mask
+        if (j > i) == (i % 2 == 1):
+            route.append((i, j))
+    return lax.ppermute(x, "ctx", route)
+
+
+def exchange_shards(
+    conv_input,
+    conv_weight,
+    b_proj,
+    c_proj,
+    log_decay,
+    skip_gain,
+    grad_in,
+    norm_gain,
+    expert_ids,
+    expert_weights,
+    up_weight,
+    down_weight,
+):
+    rows, lanes = conv_input.shape
+    heads = log_decay.shape[0]
+    states = b_proj.shape[1]
+    experts = lax.axis_size("exp")
+    features = lanes * experts
+    place = lax.axis_index("ctx")
+    core = (place & 1).reshape(1)
+    chip = place >> 1
+    mine = lax.axis_index("exp").reshape(1)
+    ids = expert_ids.T
+    block = shape_of((rows, lanes), F32)
+    payload = shape_of((states + DECAY_ROWS, lanes), BF16)
+
+    rim = passed_along(conv_input[rows - RIM :], "ctx", 1)
+    mixed, sent, kept, grow, fade = call(
+        mix_kernel, [shape_of((rows, lanes), BF16), payload, payload, block, block], smem=1
+    )(core, conv_input, rim, conv_weight, b_proj, c_proj, log_decay, grad_in)
+    received = swap(sent, "ctx", 1)
+    chip_sum = call(pair_kernel, payload)(received, kept)
+    near, middle, far = (directed(chip_sum, mask) for mask in (2, 4, 6))
+    inner, grad_inner = call(inner_kernel, [block, block])(
+        mixed, b_proj, c_proj, log_decay, grad_in, skip_gain.reshape(1, heads)
+    )
+    later = place & 1
+    flip = jnp.where(later == 1, chip == 2, chip == 1).astype(jnp.int32).reshape(1)
+    prefix = call(reach_kernel, shape_of((states, lanes), BF16), smem=1)(flip, near, middle, far)
+    shared = swap(prefix, "ctx", 1)
+
+    slots = 3 * TOPK * rows // (2 * experts * CHUNKS)
+    picked = call(carry_kernel, [shape_of((slots, lanes), BF16)] * (CHUNKS * experts), smem=2)(
+        core, mine, shared, prefix, received, inner, grow, c_proj, ids
+    )
+    grad_conv = call(grad_kernel, block, smem=1)(
+        core, shared, prefix, received, grad_inner, fade, b_proj
+    )
+
+    gain = norm_gain.reshape(1, features)
+    half = features // 2
+    row_block = shape_of((2, slots, half), BF16)
+    half_block = shape_of((slots, half), BF16)
+    up_local, down_local = up_weight[0], down_weight[0]
+    split = [(0, None), (4, None), (1, None), (5, None), (2, None), (6, None), (3, 0), (7, 0), (3, 1), (7, 1)]
+    returned = []
+    for chunk in range(CHUNKS):
+        parts = picked[chunk * experts : (chunk + 1) * experts]
+        arrived = [parts[0]] + [swap(parts[m], "exp", m) for m in range(1, experts)]
+        own = call(norm_kernel, row_block, smem=1)(mine, gain, *arrived)
+        twin = swap(own, "ctx", 1)
+        along_x, along_y = swap(own, "ctx", 2), swap(own, "ctx", 4)
+        diagonal = [swap(along_y[0], "ctx", 2), swap(along_x[1], "ctx", 4)]
+        blocks = [own, twin]
+        for block_in in (along_x, along_y, *diagonal):
+            blocks += [block_in, swap(block_in, "ctx", 1)]
+        even, odd = expert_rows(blocks, split, 8, up_local, down_local)
+        other = swap(odd, "ctx", 1)
+        own_sum, to_x, to_y, rest_x, rest_y = call(
+            chip_sum_kernel, [row_block, row_block, row_block, half_block, half_block]
+        )(even, other)
+        from_x, from_y = swap(to_x, "ctx", 2), swap(to_y, "ctx", 4)
+        next_x, next_y = call(relay_kernel, [half_block, half_block])(from_x, from_y, rest_x, rest_y)
+        last_x, last_y = swap(next_x, "ctx", 2), swap(next_y, "ctx", 4)
+        results = call(
+            total_kernel,
+            [shape_of((slots, lanes), BF16)] * experts,
+            smem=1,
+            scratch=[pltpu.VMEM((2, slots, half), BF16)],
+        )(mine, own_sum, from_x, from_y, last_x, last_y)
+        returned += [results[0]] + [swap(results[m], "exp", m) for m in range(1, experts)]
+    moe_out = call(combine_kernel, shape_of((rows, lanes), BF16), smem=1)(
+        mine, ids, expert_weights, *returned
+    )
+    return (moe_out, grad_conv)
+
+
 def solution(mesh):
     placed = (
         P("ctx", "exp"),
@@ -207,8 +652,9 @@
         P("exp", None, "ctx"),
         P("exp", "ctx", None),
     )
+    swaps = mesh.shape["ctx"] == 8 and mesh.shape["exp"] == 4
     return jax.shard_map(
-        shards,
+        exchange_shards if swaps else general_shards,
         mesh=mesh,
         in_specs=placed,
         out_specs=(P("ctx", "exp"), P("ctx", "exp")),

time: 301 us -> 174 us (0.58)
  waiting for transfers between devices: 157 us -> 65.1 us
  Pallas kernels: 0 us -> 50.6 us
  matrix products: 38.4 us -> 0 us
  blocking collectives: 36.5 us -> 0 us
  starting transfers between devices: 16.4 us -> 49.3 us
  other arithmetic: 26.4 us -> 0 us
  between operations: 14.9 us -> 0.96 us
  local copies, waits for them, and re-layouts: 10.3 us -> 6.72 us
    all_gather x3 -> x0, waiting for transfers between devices: 81.2 us -> none  [the longest x1 43.6 us: expert_block(): lax.all_gather(rows_in, 'ctx', axis=0, tiled=True)]
    ppermute x0 -> x45, waiting for transfers between devices: none -> 64.3 us  [the longest x42 53.4 us: swap(): return lax.ppermute(x, axis, [(i, i ^ mask) for i in range(size)])]
    reduce_scatter x1 -> x0, waiting for transfers between devices: 59.4 us -> none  [expert_block(): lax.psum_scatter(jnp.dot(hidden, down_local, preferred_element_type=jnp.f...]
    pallas_call x0 -> x17, Pallas kernels: none -> 50.6 us  [the longest x2 41.3 us: expert_rows(): pl.pallas_call(lambda *refs: ffn_kernel(n_up, split, *refs), grid=(n_up +...]
    ppermute x0 -> x45, starting transfers between devices: none -> 47 us  [the longest x42 43.1 us: swap(): return lax.ppermute(x, axis, [(i, i ^ mask) for i in range(size)])]
    dot_general x10 -> x0, matrix products: 38.4 us -> none  [the longest x1 30.9 us: expert_block(): jnp.dot(hidden, down_local, preferred_element_type=jnp.float32)]
    all_to_all x1 -> x0, blocking collectives: 22 us -> none  [shards(): lax.all_to_all(outgoing.reshape(experts, most_rows, normed.shape[1]), 'ex...]
    select_n x16 -> x0, other arithmetic: 17.5 us -> none  [turn(): return jax.tree.map(lambda a, b: jnp.where(reached, a, b), new, before)]
  transfers between devices with their start and end apart: 8 -> 46, of which waited for: 6 -> 25; matrix products, arithmetic and copies ran while one was open for 8% -> 0% of each run, Pallas kernels for 0% -> 27%
where the time goes in v1:
time: 174 us; the launch traced here: 173 us
  waiting for transfers between devices  65.1 us (37%)
  Pallas kernels  50.6 us (29%)
  starting transfers between devices  49.3 us (28%)
  local copies, waits for them, and re-layouts  6.72 us (4%)
    ppermute x42, waiting for transfers between devices, swap(): return lax.ppermute(x, axis, [(i, i ^ mask) for i in range(size)])  53.4 us
    ppermute x42, starting transfers between devices, swap(): return lax.ppermute(x, axis, [(i, i ^ mask) for i in range(size)])  43.1 us
    pallas_call x2, Pallas kernels, expert_rows(): pl.pallas_call(lambda *refs: ffn_kernel(n_up, split, *refs), grid=(n_up +...  41.3 us
    ppermute x3, waiting for transfers between devices, directed(): return lax.ppermute(x, 'ctx', route)  10.9 us
    pallas_call x15, Pallas kernels, run(): pl.pallas_call(body, out_shape=outs, in_specs=specs, out_specs=jax.tree.m...  9.27 us
    unnamed x33, local copies, waits for them, and re-layouts  5.93 us
    ppermute x3, starting transfers between devices, directed(): return lax.ppermute(x, 'ctx', route)  3.88 us
  transfers between devices with their start and end apart: 46, of which 25 were waited for; matrix products, arithmetic and copies ran while one was open for 0% of the time, Pallas kernels for 27%

profile of v1, /device:TPU:0, one launch (start us, length us, event | category | flops | bytes accessed | tf_op | source)
XLA Modules:
  0.0 172.6 jit_solution(14191647784280237070)
XLA Ops:
  1.4 2.3 %collective-permute-start = (bf16[8,1024]{1,0:T(8,128)(2,1)S(1)}, bf16[8,1024]{1,0:T(8,128)(2,1)S(1)}, u32[]{:S(2)}, u32[]{:S(2)}) collective-permute-start(bf16[8,1024]{1,0:T(8,128)(2,1)S(1)} %slice.15), channel_id=1, source_target_pairs={{0,4},{4,8},{8,12},{12,16},{16,20},{20,24},{24,28},{1,5},{5,9},{9,... | collective-permute-start | bytes 49160 | tf_op jit(solution)/shard_map/ppermute | solution.py:19
  9.4 1.3 shard_map.131
  10.7 2.7 %collective-permute-start.1 = (bf16[144,1024]{1,0:T(8,128)(2,1)S(1)}, bf16[144,1024]{1,0:T(8,128)(2,1)S(1)}, u32[]{:S(2)}, u32[]{:S(2)}) collective-permute-start(bf16[144,1024]{1,0:T(8,128)(2,1)S(1)} %get-tuple-element.43), channel_id=1, source_target_pairs={{0,4},{4,0},{8,12},{12,8},{16,20},{20,16},{24,28},{28,24},{1,5},{5... | collective-permute-start | bytes 884744 | tf_op jit(solution)/shard_map/ppermute | solution.py:227
  13.4 1.2 collective-permute-done.1.received
  14.7 1.3 collective-permute-start.2
  16.0 1.3 collective-permute-start.3
  17.3 1.3 collective-permute-start.4
  18.7 4.7 %collective-permute-done.2.near = bf16[144,1024]{1,0:T(8,128)(2,1)S(1)} collective-permute-done((bf16[144,1024]{1,0:T(8,128)(2,1)S(1)}, bf16[144,1024]{1,0:T(8,128)(2,1)S(1)}, u32[]{:S(2)}, u32[]{:S(2)}) %collective-permute-start.2) | collective-permute-done | bytes 294944 | tf_op jit(solution)/shard_map/ppermute | solution.py:549
  23.4 2.1 %collective-permute-done.3.middle = bf16[144,1024]{1,0:T(8,128)(2,1)S(1)} collective-permute-done((bf16[144,1024]{1,0:T(8,128)(2,1)S(1)}, bf16[144,1024]{1,0:T(8,128)(2,1)S(1)}, u32[]{:S(2)}, u32[]{:S(2)}) %collective-permute-start.3) | collective-permute-done | bytes 294944 | tf_op jit(solution)/shard_map/ppermute | solution.py:549
  25.5 4.0 %collective-permute-done.4.far = bf16[144,1024]{1,0:T(8,128)(2,1)} collective-permute-done((bf16[144,1024]{1,0:T(8,128)(2,1)S(1)}, bf16[144,1024]{1,0:T(8,128)(2,1)}, u32[]{:S(2)}, u32[]{:S(2)}) %collective-permute-start.4) | collective-permute-done | bytes 294944 | tf_op jit(solution)/shard_map/ppermute | solution.py:549
  29.5 1.1 shard_map.133.prefix
  33.6 1.6 collective-permute-start.26
  35.2 2.6 %collective-permute-start.27 = (bf16[48,1024]{1,0:T(8,128)(2,1)S(1)}, bf16[48,1024]{1,0:T(8,128)(2,1)S(1)}, u32[]{:S(2)}, u32[]{:S(2)}) collective-permute-start(bf16[48,1024]{1,0:T(8,128)(2,1)S(1)} %get-tuple-element.67), channel_id=1, source_target_pairs={{0,2},{1,3},{2,0},{3,1},{4,6},{5,7},{6,4},{7,5},{8,10},{9,11},{10,... | collective-permute-start | bytes 294920 | tf_op jit(solution)/shard_map/ppermute | solution.py:227
  38.8 7.2 %collective-permute-done.27.refs_2_ = bf16[48,1024]{1,0:T(8,128)(2,1)S(1)} collective-permute-done((bf16[48,1024]{1,0:T(8,128)(2,1)S(1)}, bf16[48,1024]{1,0:T(8,128)(2,1)S(1)}, u32[]{:S(2)}, u32[]{:S(2)}) %collective-permute-start.27) | collective-permute-done | bytes 98336 | tf_op jit(solution)/shard_map/ppermute | solution.py:227
  46.2 1.6 collective-permute-start.32
  47.8 1.7 collective-permute-start.6
  49.5 1.4 collective-permute-start.7
  50.9 1.3 collective-permute-start.8
  53.0 5.6 %collective-permute-done.7.refs_2_ = bf16[48,1024]{1,0:T(8,128)(2,1)S(1)} collective-permute-done((bf16[48,1024]{1,0:T(8,128)(2,1)S(1)}, bf16[48,1024]{1,0:T(8,128)(2,1)S(1)}, u32[]{:S(2)}, u32[]{:S(2)}) %collective-permute-start.7) | collective-permute-done | bytes 98336 | tf_op jit(solution)/shard_map/ppermute | solution.py:227
  58.9 1.3 collective-permute-start.12
  60.2 1.8 %collective-permute-start.10 = (bf16[2,48,2048]{2,1,0:T(8,128)(2,1)S(1)}, bf16[2,48,2048]{2,1,0:T(8,128)(2,1)S(1)}, u32[]{:S(2)}, u32[]{:S(2)}) collective-permute-start(bf16[2,48,2048]{2,1,0:T(8,128)(2,1)S(1)} %shard_map.136.refs_0_), channel_id=1, source_target_pairs={{0,8},{4,12},{8,0},{12,4},{16,24},{20,28},{24,16},{28,20},{1,9},{5... | collective-permute-start | bytes 1179656 | tf_op jit(solution)/shard_map/ppermute | solution.py:227
  63.0 1.8 %collective-permute-start.36 = (bf16[48,2048]{1,0:T(8,128)(2,1)S(1)}, bf16[48,2048]{1,0:T(8,128)(2,1)S(1)}, u32[]{:S(2)}, u32[]{:S(2)}) collective-permute-start(bf16[48,2048]{1,0:T(8,128)(2,1)S(1)} %slice_bitcast_fusion), channel_id=1, source_target_pairs={{0,16},{4,20},{8,24},{12,28},{16,0},{20,4},{24,8},{28,12},{1,17},{... | collective-permute-start | bytes 589832 | tf_op jit(solution)/shard_map/ppermute | solution.py:227
  64.8 3.7 %collective-permute-done.12.refs_4_ = bf16[2,48,2048]{2,1,0:T(8,128)(2,1)S(1)} collective-permute-done((bf16[2,48,2048]{2,1,0:T(8,128)(2,1)S(1)}, bf16[2,48,2048]{2,1,0:T(8,128)(2,1)S(1)}, u32[]{:S(2)}, u32[]{:S(2)}) %collective-permute-start.12) | collective-permute-done | bytes 393248 | tf_op jit(solution)/shard_map/ppermute | solution.py:227
  68.5 2.0 %collective-permute-start.14 = (bf16[48,2048]{1,0:T(8,128)(2,1)S(1)}, bf16[48,2048]{1,0:T(8,128)(2,1)S(1)}, u32[]{:S(2)}, u32[]{:S(2)}) collective-permute-start(bf16[48,2048]{1,0:T(8,128)(2,1)S(1)} %slice_bitcast_fusion.3), channel_id=1, source_target_pairs={{0,8},{4,12},{8,0},{12,4},{16,24},{20,28},{24,16},{28,20},{1,9},{5... | collective-permute-start | bytes 589832 | tf_op jit(solution)/shard_map/ppermute | solution.py:227
  70.5 1.8 %collective-permute-done.10.refs_2_ = bf16[2,48,2048]{2,1,0:T(8,128)(2,1)S(1)} collective-permute-done((bf16[2,48,2048]{2,1,0:T(8,128)(2,1)S(1)}, bf16[2,48,2048]{2,1,0:T(8,128)(2,1)S(1)}, u32[]{:S(2)}, u32[]{:S(2)}) %collective-permute-start.10) | collective-permute-done | bytes 393248 | tf_op jit(solution)/shard_map/ppermute | solution.py:227
  72.3 3.6 %collective-permute-done.34.refs_6_ = bf16[48,2048]{1,0:T(8,128)(2,1)S(1)} collective-permute-done((bf16[48,2048]{1,0:T(8,128)(2,1)S(1)}, bf16[48,2048]{1,0:T(8,128)(2,1)S(1)}, u32[]{:S(2)}, u32[]{:S(2)}) %collective-permute-start.34) | collective-permute-done | bytes 196640 | tf_op jit(solution)/shard_map/ppermute | solution.py:227
  75.9 1.2 collective-permute-start.16
  78.0 3.6 %collective-permute-done.16.refs_8_ = bf16[48,2048]{1,0:T(8,128)(2,1)S(1)} collective-permute-done((bf16[48,2048]{1,0:T(8,128)(2,1)S(1)}, bf16[48,2048]{1,0:T(8,128)(2,1)S(1)}, u32[]{:S(2)}, u32[]{:S(2)}) %collective-permute-start.16) | collective-permute-done | bytes 196640 | tf_op jit(solution)/shard_map/ppermute | solution.py:227
  82.6 20.6 %shard_map.142 = (bf16[4,2,48,2048]{3,2,1,0:T(8,128)(2,1)S(1)}, bf16[4,2,48,2048]{3,2,1,0:T(8,128)(2,1)}) custom-call(bf16[2,48,2048]{2,1,0:T(8,128)(2,1)S(1)} %shard_map.141.refs_0_, bf16[2,48,2048]{2,1,0:T(8,128)(2,1)S(1)} %collective-permute-done.29.refs_1_, bf16[2,48,2048]{2,1,0:T(8,128)(2,1)S(1)} %collective-permute-done.30.refs_2_, ...), custom_call_target="tpu_custom_call" | custom-call | flops 9663676416 | bytes 31457280 | tf_op jit(solution)/shard_map/pallas_call | solution.py:458
  103.8 20.7 %shard_map.137 = (bf16[4,2,48,2048]{3,2,1,0:T(8,128)(2,1)S(1)}, bf16[4,2,48,2048]{3,2,1,0:T(8,128)(2,1)}) custom-call(bf16[2,48,2048]{2,1,0:T(8,128)(2,1)S(1)} %shard_map.136.refs_0_, bf16[2,48,2048]{2,1,0:T(8,128)(2,1)S(1)} %collective-permute-done.9.refs_1_, bf16[2,48,2048]{2,1,0:T(8,128)(2,1)S(1)} %collective-permute-done.10.refs_2_, ...), custom_call_target="tpu_custom_call" | custom-call | flops 9663676416 | bytes 31457280 | tf_op jit(solution)/shard_map/pallas_call | solution.py:458
  125.0 1.3 collective-permute-start.39
  126.3 1.7 collective-permute-start.40
  128.5 1.3 collective-permute-start.19
  129.9 1.7 collective-permute-start.20
  131.5 5.4 %collective-permute-done.39.from_x = bf16[2,48,2048]{2,1,0:T(8,128)(2,1)S(1)} collective-permute-done((bf16[2,48,2048]{2,1,0:T(8,128)(2,1)S(1)}, bf16[2,48,2048]{2,1,0:T(8,128)(2,1)S(1)}, u32[]{:S(2)}, u32[]{:S(2)}) %collective-permute-start.39) | collective-permute-done | bytes 393248 | tf_op jit(solution)/shard_map/ppermute | solution.py:227
  137.0 1.3 collective-permute-done.40.from_y
  139.2 1.2 collective-permute-start.42
  140.4 5.0 %collective-permute-done.19.from_x = bf16[2,48,2048]{2,1,0:T(8,128)(2,1)S(1)} collective-permute-done((bf16[2,48,2048]{2,1,0:T(8,128)(2,1)S(1)}, bf16[2,48,2048]{2,1,0:T(8,128)(2,1)S(1)}, u32[]{:S(2)}, u32[]{:S(2)}) %collective-permute-start.19) | collective-permute-done | bytes 393248 | tf_op jit(solution)/shard_map/ppermute | solution.py:227
  145.4 1.3 collective-permute-done.20.from_y
  147.7 1.2 collective-permute-start.22
  149.6 1.3 collective-permute-done.42.last_y
  151.2 2.5 %collective-permute-start.43 = (bf16[48,1024]{1,0:T(8,128)(2,1)S(1)}, bf16[48,1024]{1,0:T(8,128)(2,1)S(1)}, u32[]{:S(2)}, u32[]{:S(2)}) collective-permute-start(bf16[48,1024]{1,0:T(8,128)(2,1)S(1)} %get-tuple-element.79), channel_id=1, source_target_pairs={{0,1},{1,0},{2,3},{3,2},{4,5},{5,4},{6,7},{7,6},{8,9},{9,8},{10,11... | collective-permute-start | bytes 294920 | tf_op jit(solution)/shard_map/ppermute | solution.py:227
  153.7 1.1 collective-permute-start.44
  154.8 1.4 collective-permute-start.45
  158.1 2.0 %collective-permute-start.24 = (bf16[48,1024]{1,0:T(8,128)(2,1)S(1)}, bf16[48,1024]{1,0:T(8,128)(2,1)S(1)}, u32[]{:S(2)}, u32[]{:S(2)}) collective-permute-start(bf16[48,1024]{1,0:T(8,128)(2,1)S(1)} %get-tuple-element.63), channel_id=1, source_target_pairs={{0,2},{1,3},{2,0},{3,1},{4,6},{5,7},{6,4},{7,5},{8,10},{9,11},{10,... | collective-permute-start | bytes 294920 | tf_op jit(solution)/shard_map/ppermute | solution.py:227
  160.1 1.4 collective-permute-start.25
  163.8 7.5 %collective-permute-done.24.refs_2_ = bf16[48,1024]{1,0:T(8,128)(2,1)S(1)} collective-permute-done((bf16[48,1024]{1,0:T(8,128)(2,1)S(1)}, bf16[48,1024]{1,0:T(8,128)(2,1)S(1)}, u32[]{:S(2)}, u32[]{:S(2)}) %collective-permute-start.24) | collective-permute-done | bytes 98336 | tf_op jit(solution)/shard_map/ppermute | solution.py:227
  171.3 1.4 shard_map.146
  (99 shorter events, 23.3 us)
Async XLA Ops:
  0.6 30.1 %copy-start.4 = (bf16[128,128]{1,0:T(8,128)(2,1)S(1)}, bf16[128,128]{1,0:T(8,128)(2,1)}, u32[]{:S(2)}) copy-start(bf16[128,128]{1,0:T(8,128)(2,1)} %c.5) | copy-start | bytes 98308
  0.6 30.1 %copy-start.11 = (f32[16,128]{1,0:T(8,128)S(1)}, f32[16,128]{1,0:T(8,128)}, u32[]{:S(2)}) copy-start(f32[16,128]{1,0:T(8,128)} %decay.3) | copy-start | bytes 24580
  1.4 3.2 %collective-permute-start = (bf16[8,1024]{1,0:T(8,128)(2,1)S(1)}, bf16[8,1024]{1,0:T(8,128)(2,1)S(1)}, u32[]{:S(2)}, u32[]{:S(2)}) collective-permute-start(bf16[8,1024]{1,0:T(8,128)(2,1)S(1)} %slice.15), channel_id=1, source_target_pairs={{0,4},{4,8},{8,12},{12,16},{16,20},{20,24},{24,28},{1,5},{5,9},{9,... | collective-permute-start | bytes 49160 | tf_op jit(solution)/shard_map/ppermute | solution.py:19
  10.7 3.9 %collective-permute-start.1 = (bf16[144,1024]{1,0:T(8,128)(2,1)S(1)}, bf16[144,1024]{1,0:T(8,128)(2,1)S(1)}, u32[]{:S(2)}, u32[]{:S(2)}) collective-permute-start(bf16[144,1024]{1,0:T(8,128)(2,1)S(1)} %get-tuple-element.43), channel_id=1, source_target_pairs={{0,4},{4,0},{8,12},{12,8},{16,20},{20,16},{24,28},{28,24},{1,5},{5... | collective-permute-start | bytes 884744 | tf_op jit(solution)/shard_map/ppermute | solution.py:227
  14.7 8.6 %collective-permute-start.2 = (bf16[144,1024]{1,0:T(8,128)(2,1)S(1)}, bf16[144,1024]{1,0:T(8,128)(2,1)S(1)}, u32[]{:S(2)}, u32[]{:S(2)}) collective-permute-start(bf16[144,1024]{1,0:T(8,128)(2,1)S(1)} %shard_map.132), channel_id=1, source_target_pairs={{4,12},{8,0},{20,28},{24,16},{5,13},{9,1},{21,29},{25,17},{6,14},{... | collective-permute-start | bytes 884744 | tf_op jit(solution)/shard_map/ppermute | solution.py:549
  16.0 9.5 %collective-permute-start.3 = (bf16[144,1024]{1,0:T(8,128)(2,1)S(1)}, bf16[144,1024]{1,0:T(8,128)(2,1)S(1)}, u32[]{:S(2)}, u32[]{:S(2)}) collective-permute-start(bf16[144,1024]{1,0:T(8,128)(2,1)S(1)} %shard_map.132), channel_id=1, source_target_pairs={{4,20},{12,28},{16,0},{24,8},{5,21},{13,29},{17,1},{25,9},{6,22},{... | collective-permute-start | bytes 884744 | tf_op jit(solution)/shard_map/ppermute | solution.py:549
  17.3 12.2 %collective-permute-start.4 = (bf16[144,1024]{1,0:T(8,128)(2,1)S(1)}, bf16[144,1024]{1,0:T(8,128)(2,1)}, u32[]{:S(2)}, u32[]{:S(2)}) collective-permute-start(bf16[144,1024]{1,0:T(8,128)(2,1)S(1)} %shard_map.132), channel_id=1, source_target_pairs={{4,28},{12,20},{16,8},{24,0},{5,29},{13,21},{17,9},{25,1},{6,30},{... | collective-permute-start | bytes 884744 | tf_op jit(solution)/shard_map/ppermute | solution.py:549
  30.7 2.2 %collective-permute-start.5 = (bf16[128,1024]{1,0:T(8,128)(2,1)S(1)}, bf16[128,1024]{1,0:T(8,128)(2,1)S(1)}, u32[]{:S(2)}, u32[]{:S(2)}) collective-permute-start(bf16[128,1024]{1,0:T(8,128)(2,1)S(1)} %shard_map.133.prefix), channel_id=1, source_target_pairs={{0,4},{4,0},{8,12},{12,8},{16,20},{20,16},{24,28},{28,24},{1,5},{5... | collective-permute-start | bytes 786440 | tf_op jit(solution)/shard_map/ppermute | solution.py:227
  33.6 5.2 %collective-permute-start.26 = (bf16[48,1024]{1,0:T(8,128)(2,1)S(1)}, bf16[48,1024]{1,0:T(8,128)(2,1)S(1)}, u32[]{:S(2)}, u32[]{:S(2)}) collective-permute-start(bf16[48,1024]{1,0:T(8,128)(2,1)S(1)} %get-tuple-element.66), channel_id=1, source_target_pairs={{0,1},{1,0},{2,3},{3,2},{4,5},{5,4},{6,7},{7,6},{8,9},{9,8},{10,11... | collective-permute-start | bytes 294920 | tf_op jit(solution)/shard_map/ppermute | solution.py:227
  35.2 10.7 %collective-permute-start.27 = (bf16[48,1024]{1,0:T(8,128)(2,1)S(1)}, bf16[48,1024]{1,0:T(8,128)(2,1)S(1)}, u32[]{:S(2)}, u32[]{:S(2)}) collective-permute-start(bf16[48,1024]{1,0:T(8,128)(2,1)S(1)} %get-tuple-element.67), channel_id=1, source_target_pairs={{0,2},{1,3},{2,0},{3,1},{4,6},{5,7},{6,4},{7,5},{8,10},{9,11},{10,... | collective-permute-start | bytes 294920 | tf_op jit(solution)/shard_map/ppermute | solution.py:227
  37.8 8.2 %collective-permute-start.28 = (bf16[48,1024]{1,0:T(8,128)(2,1)S(1)}, bf16[48,1024]{1,0:T(8,128)(2,1)S(1)}, u32[]{:S(2)}, u32[]{:S(2)}) collective-permute-start(bf16[48,1024]{1,0:T(8,128)(2,1)S(1)} %get-tuple-element.68), channel_id=1, source_target_pairs={{0,3},{1,2},{2,1},{3,0},{4,7},{5,6},{6,5},{7,4},{8,11},{9,10},{10,... | collective-permute-start | bytes 294920 | tf_op jit(solution)/shard_map/ppermute | solution.py:227
  46.2 15.8 %collective-permute-start.32 = (bf16[2,48,2048]{2,1,0:T(8,128)(2,1)S(1)}, bf16[2,48,2048]{2,1,0:T(8,128)(2,1)S(1)}, u32[]{:S(2)}, u32[]{:S(2)}) collective-permute-start(bf16[2,48,2048]{2,1,0:T(8,128)(2,1)S(1)} %shard_map.141.refs_0_), channel_id=1, source_target_pairs={{0,16},{4,20},{8,24},{12,28},{16,0},{20,4},{24,8},{28,12},{1,17},{... | collective-permute-start | bytes 1179656 | tf_op jit(solution)/shard_map/ppermute | solution.py:227
  47.8 5.2 %collective-permute-start.6 = (bf16[48,1024]{1,0:T(8,128)(2,1)S(1)}, bf16[48,1024]{1,0:T(8,128)(2,1)S(1)}, u32[]{:S(2)}, u32[]{:S(2)}) collective-permute-start(bf16[48,1024]{1,0:T(8,128)(2,1)S(1)} %get-tuple-element.49), channel_id=1, source_target_pairs={{0,1},{1,0},{2,3},{3,2},{4,5},{5,4},{6,7},{7,6},{8,9},{9,8},{10,11... | collective-permute-start | bytes 294920 | tf_op jit(solution)/shard_map/ppermute | solution.py:227
  49.5 9.2 %collective-permute-start.7 = (bf16[48,1024]{1,0:T(8,128)(2,1)S(1)}, bf16[48,1024]{1,0:T(8,128)(2,1)S(1)}, u32[]{:S(2)}, u32[]{:S(2)}) collective-permute-start(bf16[48,1024]{1,0:T(8,128)(2,1)S(1)} %get-tuple-element.50), channel_id=1, source_target_pairs={{0,2},{1,3},{2,0},{3,1},{4,6},{5,7},{6,4},{7,5},{8,10},{9,11},{10,... | collective-permute-start | bytes 294920 | tf_op jit(solution)/shard_map/ppermute | solution.py:227
  50.9 7.7 %collective-permute-start.8 = (bf16[48,1024]{1,0:T(8,128)(2,1)S(1)}, bf16[48,1024]{1,0:T(8,128)(2,1)S(1)}, u32[]{:S(2)}, u32[]{:S(2)}) collective-permute-start(bf16[48,1024]{1,0:T(8,128)(2,1)S(1)} %get-tuple-element.51), channel_id=1, source_target_pairs={{0,3},{1,2},{2,1},{3,0},{4,7},{5,6},{6,5},{7,4},{8,11},{9,10},{10,... | collective-permute-start | bytes 294920 | tf_op jit(solution)/shard_map/ppermute | solution.py:227
  52.2 10.8 %collective-permute-start.30 = (bf16[2,48,2048]{2,1,0:T(8,128)(2,1)S(1)}, bf16[2,48,2048]{2,1,0:T(8,128)(2,1)S(1)}, u32[]{:S(2)}, u32[]{:S(2)}) collective-permute-start(bf16[2,48,2048]{2,1,0:T(8,128)(2,1)S(1)} %shard_map.141.refs_0_), channel_id=1, source_target_pairs={{0,8},{4,12},{8,0},{12,4},{16,24},{20,28},{24,16},{28,20},{1,9},{5... | collective-permute-start | bytes 1179656 | tf_op jit(solution)/shard_map/ppermute | solution.py:227
  53.0 17.5 %collective-permute-start.29 = (bf16[2,48,2048]{2,1,0:T(8,128)(2,1)S(1)}, bf16[2,48,2048]{2,1,0:T(8,128)(2,1)S(1)}, u32[]{:S(2)}, u32[]{:S(2)}) collective-permute-start(bf16[2,48,2048]{2,1,0:T(8,128)(2,1)S(1)} %shard_map.141.refs_0_), channel_id=1, source_target_pairs={{0,4},{4,0},{8,12},{12,8},{16,20},{20,16},{24,28},{28,24},{1,5},{5... | collective-permute-start | bytes 1179656 | tf_op jit(solution)/shard_map/ppermute | solution.py:227
  58.9 9.6 %collective-permute-start.12 = (bf16[2,48,2048]{2,1,0:T(8,128)(2,1)S(1)}, bf16[2,48,2048]{2,1,0:T(8,128)(2,1)S(1)}, u32[]{:S(2)}, u32[]{:S(2)}) collective-permute-start(bf16[2,48,2048]{2,1,0:T(8,128)(2,1)S(1)} %shard_map.136.refs_0_), channel_id=1, source_target_pairs={{0,16},{4,20},{8,24},{12,28},{16,0},{20,4},{24,8},{28,12},{1,17},{... | collective-permute-start | bytes 1179656 | tf_op jit(solution)/shard_map/ppermute | solution.py:227
  60.2 12.1 %collective-permute-start.10 = (bf16[2,48,2048]{2,1,0:T(8,128)(2,1)S(1)}, bf16[2,48,2048]{2,1,0:T(8,128)(2,1)S(1)}, u32[]{:S(2)}, u32[]{:S(2)}) collective-permute-start(bf16[2,48,2048]{2,1,0:T(8,128)(2,1)S(1)} %shard_map.136.refs_0_), channel_id=1, source_target_pairs={{0,8},{4,12},{8,0},{12,4},{16,24},{20,28},{24,16},{28,20},{1,9},{5... | collective-permute-start | bytes 1179656 | tf_op jit(solution)/shard_map/ppermute | solution.py:227
  62.0 13.9 %collective-permute-start.34 = (bf16[48,2048]{1,0:T(8,128)(2,1)S(1)}, bf16[48,2048]{1,0:T(8,128)(2,1)S(1)}, u32[]{:S(2)}, u32[]{:S(2)}) collective-permute-start(bf16[48,2048]{1,0:T(8,128)(2,1)S(1)} %slice_bitcast_fusion.1), channel_id=1, source_target_pairs={{0,8},{4,12},{8,0},{12,4},{16,24},{20,28},{24,16},{28,20},{1,9},{5... | collective-permute-start | bytes 589832 | tf_op jit(solution)/shard_map/ppermute | solution.py:227
  63.0 14.1 %collective-permute-start.36 = (bf16[48,2048]{1,0:T(8,128)(2,1)S(1)}, bf16[48,2048]{1,0:T(8,128)(2,1)S(1)}, u32[]{:S(2)}, u32[]{:S(2)}) collective-permute-start(bf16[48,2048]{1,0:T(8,128)(2,1)S(1)} %slice_bitcast_fusion), channel_id=1, source_target_pairs={{0,16},{4,20},{8,24},{12,28},{16,0},{20,4},{24,8},{28,12},{1,17},{... | collective-permute-start | bytes 589832 | tf_op jit(solution)/shard_map/ppermute | solution.py:227
  68.5 9.5 %collective-permute-start.14 = (bf16[48,2048]{1,0:T(8,128)(2,1)S(1)}, bf16[48,2048]{1,0:T(8,128)(2,1)S(1)}, u32[]{:S(2)}, u32[]{:S(2)}) collective-permute-start(bf16[48,2048]{1,0:T(8,128)(2,1)S(1)} %slice_bitcast_fusion.3), channel_id=1, source_target_pairs={{0,8},{4,12},{8,0},{12,4},{16,24},{20,28},{24,16},{28,20},{1,9},{5... | collective-permute-start | bytes 589832 | tf_op jit(solution)/shard_map/ppermute | solution.py:227
  70.5 11.7 %collective-permute-start.31 = (bf16[2,48,2048]{2,1,0:T(8,128)(2,1)S(1)}, bf16[2,48,2048]{2,1,0:T(8,128)(2,1)S(1)}, u32[]{:S(2)}, u32[]{:S(2)}) collective-permute-start(bf16[2,48,2048]{2,1,0:T(8,128)(2,1)S(1)} %collective-permute-done.30.refs_2_), channel_id=1, source_target_pairs={{0,4},{4,0},{8,12},{12,8},{16,20},{20,16},{24,28},{28,24},{1,5},{5... | collective-permute-start | bytes 1179656 | tf_op jit(solution)/shard_map/ppermute | solution.py:227
  72.2 10.3 %collective-permute-start.33 = (bf16[2,48,2048]{2,1,0:T(8,128)(2,1)S(1)}, bf16[2,48,2048]{2,1,0:T(8,128)(2,1)S(1)}, u32[]{:S(2)}, u32[]{:S(2)}) collective-permute-start(bf16[2,48,2048]{2,1,0:T(8,128)(2,1)S(1)} %collective-permute-done.32.refs_4_), channel_id=1, source_target_pairs={{0,4},{4,0},{8,12},{12,8},{16,20},{20,16},{24,28},{28,24},{1,5},{5... | collective-permute-start | bytes 1179656 | tf_op jit(solution)/shard_map/ppermute | solution.py:227
  75.9 5.7 %collective-permute-start.16 = (bf16[48,2048]{1,0:T(8,128)(2,1)S(1)}, bf16[48,2048]{1,0:T(8,128)(2,1)S(1)}, u32[]{:S(2)}, u32[]{:S(2)}) collective-permute-start(bf16[48,2048]{1,0:T(8,128)(2,1)S(1)} %slice_bitcast_fusion.2), channel_id=1, source_target_pairs={{0,16},{4,20},{8,24},{12,28},{16,0},{20,4},{24,8},{28,12},{1,17},{... | collective-permute-start | bytes 589832 | tf_op jit(solution)/shard_map/ppermute | solution.py:227
  77.1 4.5 %collective-permute-start.35 = (bf16[48,2048]{1,0:T(8,128)(2,1)S(1)}, bf16[48,2048]{1,0:T(8,128)(2,1)S(1)}, u32[]{:S(2)}, u32[]{:S(2)}) collective-permute-start(bf16[48,2048]{1,0:T(8,128)(2,1)S(1)} %collective-permute-done.34.refs_6_), channel_id=1, source_target_pairs={{0,4},{4,0},{8,12},{12,8},{16,20},{20,16},{24,28},{28,24},{1,5},{5... | collective-permute-start | bytes 589832 | tf_op jit(solution)/shard_map/ppermute | solution.py:227
  78.0 4.1 %collective-permute-start.37 = (bf16[48,2048]{1,0:T(8,128)(2,1)S(1)}, bf16[48,2048]{1,0:T(8,128)(2,1)S(1)}, u32[]{:S(2)}, u32[]{:S(2)}) collective-permute-start(bf16[48,2048]{1,0:T(8,128)(2,1)S(1)} %collective-permute-done.36.refs_8_), channel_id=1, source_target_pairs={{0,4},{4,0},{8,12},{12,8},{16,20},{20,16},{24,28},{28,24},{1,5},{5... | collective-permute-start | bytes 589832 | tf_op jit(solution)/shard_map/ppermute | solution.py:227
  81.5 21.7 %collective-permute-start.9 = (bf16[2,48,2048]{2,1,0:T(8,128)(2,1)S(1)}, bf16[2,48,2048]{2,1,0:T(8,128)(2,1)S(1)}, u32[]{:S(2)}, u32[]{:S(2)}) collective-permute-start(bf16[2,48,2048]{2,1,0:T(8,128)(2,1)S(1)} %shard_map.136.refs_0_), channel_id=1, source_target_pairs={{0,4},{4,0},{8,12},{12,8},{16,20},{20,16},{24,28},{28,24},{1,5},{5... | collective-permute-start | bytes 1179656 | tf_op jit(solution)/shard_map/ppermute | solution.py:227
  81.5 22.2 %collective-permute-start.11 = (bf16[2,48,2048]{2,1,0:T(8,128)(2,1)S(1)}, bf16[2,48,2048]{2,1,0:T(8,128)(2,1)S(1)}, u32[]{:S(2)}, u32[]{:S(2)}) collective-permute-start(bf16[2,48,2048]{2,1,0:T(8,128)(2,1)S(1)} %collective-permute-done.10.refs_2_), channel_id=1, source_target_pairs={{0,4},{4,0},{8,12},{12,8},{16,20},{20,16},{24,28},{28,24},{1,5},{5... | collective-permute-start | bytes 1179656 | tf_op jit(solution)/shard_map/ppermute | solution.py:227
  82.1 21.7 %collective-permute-start.13 = (bf16[2,48,2048]{2,1,0:T(8,128)(2,1)S(1)}, bf16[2,48,2048]{2,1,0:T(8,128)(2,1)S(1)}, u32[]{:S(2)}, u32[]{:S(2)}) collective-permute-start(bf16[2,48,2048]{2,1,0:T(8,128)(2,1)S(1)} %collective-permute-done.12.refs_4_), channel_id=1, source_target_pairs={{0,4},{4,0},{8,12},{12,8},{16,20},{20,16},{24,28},{28,24},{1,5},{5... | collective-permute-start | bytes 1179656 | tf_op jit(solution)/shard_map/ppermute | solution.py:227
  82.1 21.7 %collective-permute-start.15 = (bf16[48,2048]{1,0:T(8,128)(2,1)S(1)}, bf16[48,2048]{1,0:T(8,128)(2,1)S(1)}, u32[]{:S(2)}, u32[]{:S(2)}) collective-permute-start(bf16[48,2048]{1,0:T(8,128)(2,1)S(1)} %collective-permute-done.14.refs_6_), channel_id=1, source_target_pairs={{0,4},{4,0},{8,12},{12,8},{16,20},{20,16},{24,28},{28,24},{1,5},{5... | collective-permute-start | bytes 589832 | tf_op jit(solution)/shard_map/ppermute | solution.py:227
  82.6 21.2 %collective-permute-start.17 = (bf16[48,2048]{1,0:T(8,128)(2,1)S(1)}, bf16[48,2048]{1,0:T(8,128)(2,1)S(1)}, u32[]{:S(2)}, u32[]{:S(2)}) collective-permute-start(bf16[48,2048]{1,0:T(8,128)(2,1)S(1)} %collective-permute-done.16.refs_8_), channel_id=1, source_target_pairs={{0,4},{4,0},{8,12},{12,8},{16,20},{20,16},{24,28},{28,24},{1,5},{5... | collective-permute-start | bytes 589832 | tf_op jit(solution)/shard_map/ppermute | solution.py:227
  103.3 21.4 %collective-permute-start.38 = (bf16[4,2,48,2048]{3,2,1,0:T(8,128)(2,1)}, bf16[4,2,48,2048]{3,2,1,0:T(8,128)(2,1)S(1)}, u32[]{:S(2)}, u32[]{:S(2)}) collective-permute-start(bf16[4,2,48,2048]{3,2,1,0:T(8,128)(2,1)} %get-tuple-element.70), channel_id=1, source_target_pairs={{0,4},{4,0},{8,12},{12,8},{16,20},{20,16},{24,28},{28,24},{1,5},{5... | collective-permute-start | bytes 4718600 | tf_op jit(solution)/shard_map/ppermute | solution.py:227
  124.5 3.7 %collective-permute-start.18 = (bf16[4,2,48,2048]{3,2,1,0:T(8,128)(2,1)}, bf16[4,2,48,2048]{3,2,1,0:T(8,128)(2,1)S(1)}, u32[]{:S(2)}, u32[]{:S(2)}) collective-permute-start(bf16[4,2,48,2048]{3,2,1,0:T(8,128)(2,1)} %get-tuple-element.53), channel_id=1, source_target_pairs={{0,4},{4,0},{8,12},{12,8},{16,20},{20,16},{24,28},{28,24},{1,5},{5... | collective-permute-start | bytes 4718600 | tf_op jit(solution)/shard_map/ppermute | solution.py:227
  125.0 12.0 %collective-permute-start.39 = (bf16[2,48,2048]{2,1,0:T(8,128)(2,1)S(1)}, bf16[2,48,2048]{2,1,0:T(8,128)(2,1)S(1)}, u32[]{:S(2)}, u32[]{:S(2)}) collective-permute-start(bf16[2,48,2048]{2,1,0:T(8,128)(2,1)S(1)} %get-tuple-element.72), channel_id=1, source_target_pairs={{0,8},{4,12},{8,0},{12,4},{16,24},{20,28},{24,16},{28,20},{1,9},{5... | collective-permute-start | bytes 1179656 | tf_op jit(solution)/shard_map/ppermute | solution.py:227
  126.3 12.0 %collective-permute-start.40 = (bf16[2,48,2048]{2,1,0:T(8,128)(2,1)S(1)}, bf16[2,48,2048]{2,1,0:T(8,128)(2,1)S(1)}, u32[]{:S(2)}, u32[]{:S(2)}) collective-permute-start(bf16[2,48,2048]{2,1,0:T(8,128)(2,1)S(1)} %get-tuple-element.73), channel_id=1, source_target_pairs={{0,16},{4,20},{8,24},{12,28},{16,0},{20,4},{24,8},{28,12},{1,17},{... | collective-permute-start | bytes 1179656 | tf_op jit(solution)/shard_map/ppermute | solution.py:227
  128.5 16.9 %collective-permute-start.19 = (bf16[2,48,2048]{2,1,0:T(8,128)(2,1)S(1)}, bf16[2,48,2048]{2,1,0:T(8,128)(2,1)S(1)}, u32[]{:S(2)}, u32[]{:S(2)}) collective-permute-start(bf16[2,48,2048]{2,1,0:T(8,128)(2,1)S(1)} %get-tuple-element.55), channel_id=1, source_target_pairs={{0,8},{4,12},{8,0},{12,4},{16,24},{20,28},{24,16},{28,20},{1,9},{5... | collective-permute-start | bytes 1179656 | tf_op jit(solution)/shard_map/ppermute | solution.py:227
  129.9 16.8 %collective-permute-start.20 = (bf16[2,48,2048]{2,1,0:T(8,128)(2,1)S(1)}, bf16[2,48,2048]{2,1,0:T(8,128)(2,1)S(1)}, u32[]{:S(2)}, u32[]{:S(2)}) collective-permute-start(bf16[2,48,2048]{2,1,0:T(8,128)(2,1)S(1)} %get-tuple-element.56), channel_id=1, source_target_pairs={{0,16},{4,20},{8,24},{12,28},{16,0},{20,4},{24,8},{28,12},{1,17},{... | collective-permute-start | bytes 1179656 | tf_op jit(solution)/shard_map/ppermute | solution.py:227
  138.4 11.2 %collective-permute-start.41 = (bf16[48,2048]{1,0:T(8,128)(2,1)S(1)}, bf16[48,2048]{1,0:T(8,128)(2,1)S(1)}, u32[]{:S(2)}, u32[]{:S(2)}) collective-permute-start(bf16[48,2048]{1,0:T(8,128)(2,1)S(1)} %get-tuple-element.76), channel_id=1, source_target_pairs={{0,8},{4,12},{8,0},{12,4},{16,24},{20,28},{24,16},{28,20},{1,9},{5... | collective-permute-start | bytes 589832 | tf_op jit(solution)/shard_map/ppermute | solution.py:227
  139.2 11.7 %collective-permute-start.42 = (bf16[48,2048]{1,0:T(8,128)(2,1)S(1)}, bf16[48,2048]{1,0:T(8,128)(2,1)S(1)}, u32[]{:S(2)}, u32[]{:S(2)}) collective-permute-start(bf16[48,2048]{1,0:T(8,128)(2,1)S(1)} %get-tuple-element.77), channel_id=1, source_target_pairs={{0,16},{4,20},{8,24},{12,28},{16,0},{20,4},{24,8},{28,12},{1,17},{... | collective-permute-start | bytes 589832 | tf_op jit(solution)/shard_map/ppermute | solution.py:227
  146.8 9.4 %collective-permute-start.21 = (bf16[48,2048]{1,0:T(8,128)(2,1)S(1)}, bf16[48,2048]{1,0:T(8,128)(2,1)S(1)}, u32[]{:S(2)}, u32[]{:S(2)}) collective-permute-start(bf16[48,2048]{1,0:T(8,128)(2,1)S(1)} %get-tuple-element.59), channel_id=1, source_target_pairs={{0,8},{4,12},{8,0},{12,4},{16,24},{20,28},{24,16},{28,20},{1,9},{5... | collective-permute-start | bytes 589832 | tf_op jit(solution)/shard_map/ppermute | solution.py:227
  147.7 8.6 %collective-permute-start.22 = (bf16[48,2048]{1,0:T(8,128)(2,1)S(1)}, bf16[48,2048]{1,0:T(8,128)(2,1)S(1)}, u32[]{:S(2)}, u32[]{:S(2)}) collective-permute-start(bf16[48,2048]{1,0:T(8,128)(2,1)S(1)} %get-tuple-element.60), channel_id=1, source_target_pairs={{0,16},{4,20},{8,24},{12,28},{16,0},{20,4},{24,8},{28,12},{1,17},{... | collective-permute-start | bytes 589832 | tf_op jit(solution)/shard_map/ppermute | solution.py:227
  151.2 8.9 %collective-permute-start.43 = (bf16[48,1024]{1,0:T(8,128)(2,1)S(1)}, bf16[48,1024]{1,0:T(8,128)(2,1)S(1)}, u32[]{:S(2)}, u32[]{:S(2)}) collective-permute-start(bf16[48,1024]{1,0:T(8,128)(2,1)S(1)} %get-tuple-element.79), channel_id=1, source_target_pairs={{0,1},{1,0},{2,3},{3,2},{4,5},{5,4},{6,7},{7,6},{8,9},{9,8},{10,11... | collective-permute-start | bytes 294920 | tf_op jit(solution)/shard_map/ppermute | solution.py:227
  153.7 9.8 %collective-permute-start.44 = (bf16[48,1024]{1,0:T(8,128)(2,1)S(1)}, bf16[48,1024]{1,0:T(8,128)(2,1)S(1)}, u32[]{:S(2)}, u32[]{:S(2)}) collective-permute-start(bf16[48,1024]{1,0:T(8,128)(2,1)S(1)} %get-tuple-element.80), channel_id=1, source_target_pairs={{0,2},{1,3},{2,0},{3,1},{4,6},{5,7},{6,4},{7,5},{8,10},{9,11},{10,... | collective-permute-start | bytes 294920 | tf_op jit(solution)/shard_map/ppermute | solution.py:227
  154.8 8.7 %collective-permute-start.45 = (bf16[48,1024]{1,0:T(8,128)(2,1)S(1)}, bf16[48,1024]{1,0:T(8,128)(2,1)S(1)}, u32[]{:S(2)}, u32[]{:S(2)}) collective-permute-start(bf16[48,1024]{1,0:T(8,128)(2,1)S(1)} %get-tuple-element.81), channel_id=1, source_target_pairs={{0,3},{1,2},{2,1},{3,0},{4,7},{5,6},{6,5},{7,4},{8,11},{9,10},{10,... | collective-permute-start | bytes 294920 | tf_op jit(solution)/shard_map/ppermute | solution.py:227
  157.1 6.6 %collective-permute-start.23 = (bf16[48,1024]{1,0:T(8,128)(2,1)}, bf16[48,1024]{1,0:T(8,128)(2,1)S(1)}, u32[]{:S(2)}, u32[]{:S(2)}) collective-permute-start(bf16[48,1024]{1,0:T(8,128)(2,1)} %get-tuple-element.62), channel_id=1, source_target_pairs={{0,1},{1,0},{2,3},{3,2},{4,5},{5,4},{6,7},{7,6},{8,9},{9,8},{10,11... | collective-permute-start | bytes 294920 | tf_op jit(solution)/shard_map/ppermute | solution.py:227
  158.1 13.2 %collective-permute-start.24 = (bf16[48,1024]{1,0:T(8,128)(2,1)S(1)}, bf16[48,1024]{1,0:T(8,128)(2,1)S(1)}, u32[]{:S(2)}, u32[]{:S(2)}) collective-permute-start(bf16[48,1024]{1,0:T(8,128)(2,1)S(1)} %get-tuple-element.63), channel_id=1, source_target_pairs={{0,2},{1,3},{2,0},{3,1},{4,6},{5,7},{6,4},{7,5},{8,10},{9,11},{10,... | collective-permute-start | bytes 294920 | tf_op jit(solution)/shard_map/ppermute | solution.py:227
  160.1 11.2 %collective-permute-start.25 = (bf16[48,1024]{1,0:T(8,128)(2,1)S(1)}, bf16[48,1024]{1,0:T(8,128)(2,1)S(1)}, u32[]{:S(2)}, u32[]{:S(2)}) collective-permute-start(bf16[48,1024]{1,0:T(8,128)(2,1)S(1)} %get-tuple-element.64), channel_id=1, source_target_pairs={{0,3},{1,2},{2,1},{3,0},{4,7},{5,6},{6,5},{7,4},{8,11},{9,10},{10,... | collective-permute-start | bytes 294920 | tf_op jit(solution)/shard_map/ppermute | solution.py:227
  (14 other events, 134.5 us)

commit v2 on v1

--- a/solution.py
+++ b/solution.py
@@ -195,7 +195,8 @@
 
 
 CHUNKS = 2
-DECAY_ROWS = 16
+LIGHT = pl.CostEstimate(flops=1, transcendentals=0, bytes_accessed=1)
+DECAY_ROWS = 8
 RIM = 8
 F32 = jnp.float32
 BF16 = jnp.bfloat16
@@ -205,7 +206,7 @@
     return jax.ShapeDtypeStruct(shape, dtype)
 
 
-def call(body, outs, smem=0, scratch=(), cost=None, limit=40):
+def call(body, outs, smem=0, scratch=(), limit=6):
     def run(*args):
         specs = [pl.BlockSpec(memory_space=pltpu.SMEM)] * smem
         specs += [pl.BlockSpec(memory_space=pltpu.VMEM)] * (len(args) - smem)
@@ -215,7 +216,7 @@
             in_specs=specs,
             out_specs=jax.tree.map(lambda _: pl.BlockSpec(memory_space=pltpu.VMEM), outs),
             scratch_shapes=scratch,
-            cost_estimate=cost,
+            cost_estimate=LIGHT,
             compiler_params=pltpu.CompilerParams(vmem_limit_bytes=limit << 20),
         )(*args)
 
@@ -245,8 +246,30 @@
     return exact_dot(tri, decay, (((1,), (1,)), ((), ())))
 
 
-def mix_kernel(core, conv, rim, taps, b, c, decay, grad, mixed_out, sent, kept, grow, fade):
+def prepare_kernel(n, *refs):
+    sources, held = refs[:n], refs[n : 2 * n]
+    grow, fade, backward, through, sems = refs[2 * n :]
+    copies = [pltpu.make_async_copy(a, b, sems.at[k]) for k, (a, b) in enumerate(zip(sources, held))]
+    for copy in copies:
+        copy.start()
+    for copy in copies:
+        copy.wait()
+    decay, c, grad = held[:3]
     heads = decay.shape[0]
+    rows, lanes = grad.shape
+    columns = decay_columns(decay[...])
+    width = lanes // heads
+    spread = (iota((heads, lanes), 1) // width == iota((heads, lanes), 0)).astype(F32)
+    totals = exact_dot(columns, spread)
+    last = totals[rows - 1 : rows, :]
+    growing = jnp.exp(totals)
+    grow[...] = growing
+    fade[...] = jnp.exp(last - totals)
+    through[...] = jnp.broadcast_to(jnp.exp(last), (DECAY_ROWS, lanes)).astype(BF16)
+    backward[...] = fast_dot(c[...].T, (growing * grad[...].astype(F32)).astype(BF16)).astype(BF16)
+
+
+def mix_kernel(core, conv, rim, taps, b, fade, backward, through, mixed_out, sent, kept):
     rows, lanes = conv.shape
     x = conv[...].astype(F32)
     extended = jnp.concatenate([rim[...].astype(F32), x], axis=0)
@@ -256,24 +279,35 @@
         total = total + taps[tap : tap + 1, :] * extended[start : start + rows]
     mixed = (total * jax.nn.sigmoid(total)).astype(BF16)
     mixed_out[...] = mixed
-    columns = decay_columns(decay[...])
-    width = lanes // heads
-    spread = (iota((heads, lanes), 1) // width == iota((heads, lanes), 0)).astype(F32)
-    totals = exact_dot(columns, spread)
-    last = totals[rows - 1 : rows, :]
-    growing = jnp.exp(totals)
-    fading = jnp.exp(last - totals)
-    grow[...] = growing
-    fade[...] = fading
-    through = jnp.broadcast_to(jnp.exp(last), (DECAY_ROWS, lanes)).astype(BF16)
     states = b.shape[1]
-    forward = fast_dot(b[...].T, (fading * mixed.astype(F32)).astype(BF16)).astype(BF16)
-    backward = fast_dot(c[...].T, (growing * grad[...].astype(F32)).astype(BF16)).astype(BF16)
+    forward = fast_dot(b[...].T, (fade[...] * mixed.astype(F32)).astype(BF16)).astype(BF16)
     first = core[0] == 0
-    sent[0:states, :] = jnp.where(first, forward, backward)
-    kept[0:states, :] = jnp.where(first, backward, forward)
-    sent[states:, :] = through
-    kept[states:, :] = through
+    sent[0:states, :] = jnp.where(first, forward, backward[...])
+    kept[0:states, :] = jnp.where(first, backward[...], forward)
+    sent[states:, :] = through[...]
+    kept[states:, :] = through[...]
+
+
+def load_kernel(source, held, sem):
+    copy = pltpu.make_async_copy(source, held, sem)
+    copy.start()
+    copy.wait()
+
+
+def load(source, limit):
+    return pl.pallas_call(
+        load_kernel,
+        out_shape=pltpu.VMEM(source.shape, source.dtype),
+        in_specs=[pl.BlockSpec(memory_space=pltpu.HBM)],
+        out_specs=pl.BlockSpec(memory_space=pltpu.VMEM),
+        scratch_shapes=[pltpu.SemaphoreType.DMA],
+        cost_estimate=LIGHT,
+        compiler_params=pltpu.CompilerParams(vmem_limit_bytes=limit << 20),
+    )(pltpu.with_memory_space_constraint(source, pltpu.HBM))
+
+
+def after(x, *others):
+    return lax.optimization_barrier((x, *others))[0]
 
 
 def pair_kernel(received, kept, chip):
@@ -394,113 +428,95 @@
         out[at // per_half, :, pl.ds(to, width)] = (value * scale * gains).astype(BF16)
 
 
-def ffn_kernel(n_up, split, *refs):
-    blocks, (up, down, even, odd, rows_in, hidden, sems) = refs[:-7], refs[-7:]
-    step = pl.program_id(0)
-    slots = blocks[0].shape[-2]
-    half = rows_in.shape[1] // 2
-
-    @pl.when(step == 0)
-    def _():
-        copies = []
-        for n, (place, part) in enumerate(split):
-            at = rows_in.at[pl.ds(place * slots, slots)]
-            if part is None:
-                for side in range(2):
-                    copies.append(
-                        pltpu.make_async_copy(
-                            blocks[n].at[side], at.at[:, pl.ds(side * half, half)], sems.at[len(copies)]
-                        )
-                    )
-            else:
-                copies.append(
-                    pltpu.make_async_copy(
-                        blocks[n], at.at[:, pl.ds(part * half, half)], sems.at[len(copies)]
-                    )
-                )
-        for copy in copies:
-            copy.start()
-        for copy in copies:
-            copy.wait()
-
-    @pl.when(step < n_up)
-    def _():
-        value = fast_dot(rows_in[...], up[...])
-        width = up.shape[1]
-        to = pl.multiple_of(step * width, width)
-        hidden[:, pl.ds(to, width)] = (value * jax.nn.sigmoid(value)).astype(BF16)
-
-    @pl.when(step >= n_up)
-    def _():
-        value = fast_dot(hidden[...], down[...]).astype(BF16)
-        count = even.shape[0] * slots
-        even[...] = value[:count].reshape(even.shape)
-        odd[...] = value[count:].reshape(odd.shape)
-
-
-UP_TILE = 256
+def onward_kernel(along_x, along_y, own, to_x, to_y):
+    to_x[0] = along_y[0]
+    to_y[0] = along_x[1]
+    to_x[1:] = own[...]
+    to_y[1:] = own[...]
+
+
+def arrive_kernel(from_x, from_y, far, along_x, along_y):
+    far[0] = from_x[0]
+    far[1] = from_y[0]
+    along_x[...] = from_x[1:]
+    along_y[...] = from_y[1:]
+
+
+def join_kernel(from_x, from_y, far):
+    far[0] = from_x[0]
+    far[1] = from_y[0]
+
+
+def expert_kernel(n, *refs):
+    blocks, (up, down), outs, (rows_in, hidden) = refs[: 2 * n], refs[2 * n : 2 * n + 2], refs[2 * n + 2 : -2], refs[-2:]
+    _, slots, half = blocks[0].shape
+    for k, block in enumerate(blocks):
+        rows = slice(k * slots, (k + 1) * slots)
+        rows_in[rows, :half] = block[0]
+        rows_in[rows, half:] = block[1]
+    for j in range(0, hidden.shape[1], UP_TILE):
+        value = fast_dot(rows_in[...], up[:, j : j + UP_TILE])
+        hidden[:, j : j + UP_TILE] = (value * jax.nn.sigmoid(value)).astype(BF16)
+    for j in range(0, down.shape[1], DOWN_TILE):
+        value = fast_dot(hidden[...], down[:, j : j + DOWN_TILE]).astype(BF16)
+        at = slice(j % half, j % half + DOWN_TILE)
+        for k, out in enumerate(outs):
+            start = (n + k) % (2 * n) * slots
+            out[j // half, :, at] = value[start : start + slots]
+
+
+UP_TILE = 512
 DOWN_TILE = 512
 
 
-def expert_rows(blocks, split, places, up, down):
-    slots, half = blocks[0].shape[-2:]
+def expert_rows(blocks, twins, up, down):
+    n = len(blocks)
+    _, slots, half = blocks[0].shape
     features, hidden = up.shape
-    n_up, n_down = hidden // UP_TILE, features // DOWN_TILE
-    per_half = half // DOWN_TILE
-    rows = places * slots
-
-    def out_at(i):
-        j = jnp.maximum(i - n_up, 0)
-        return (0, j // per_half, 0, j % per_half)
-
-    spec = pl.BlockSpec((places // 2, None, slots, DOWN_TILE), out_at)
-    n_copies = sum(2 if part is None else 1 for _, part in split)
-    return pl.pallas_call(
-        lambda *refs: ffn_kernel(n_up, split, *refs),
-        grid=(n_up + n_down,),
-        in_specs=[pl.BlockSpec(memory_space=pl.ANY)] * len(blocks)
-        + [
-            pl.BlockSpec((features, UP_TILE), lambda i: (0, jnp.minimum(i, n_up - 1))),
-            pl.BlockSpec((hidden, DOWN_TILE), lambda i: (0, jnp.maximum(i - n_up, 0))),
-        ],
-        out_specs=[spec, spec],
-        out_shape=[shape_of((places // 2, 2, slots, half), BF16)] * 2,
-        scratch_shapes=[
-            pltpu.VMEM((rows, features), BF16),
-            pltpu.VMEM((rows, hidden), BF16),
-            pltpu.SemaphoreType.DMA((n_copies,)),
-        ],
-        cost_estimate=pl.CostEstimate(
-            flops=4 * rows * features * hidden,
-            transcendentals=rows * hidden,
-            bytes_accessed=4 * features * hidden + 4 * rows * features,
-        ),
-        compiler_params=pltpu.CompilerParams(
-            dimension_semantics=("arbitrary",), vmem_limit_bytes=48 << 20
-        ),
-    )(*blocks, up, down)
+    outs = call(
+        lambda *refs: expert_kernel(n, *refs),
+        [shape_of((2, slots, half), BF16)] * (2 * n),
+        scratch=[pltpu.VMEM((2 * n * slots, features), BF16), pltpu.VMEM((2 * n * slots, hidden), BF16)],
+        limit=8,
+    )(*blocks, *twins, up, down)
+    return outs[:n], outs[n:]
 
 
 def both(a, b):
     return (a.astype(F32) + b.astype(F32)).astype(BF16)
 
 
-def chip_sum_kernel(even, other, own, to_x, to_y, rest_x, rest_y):
-    own[...] = both(even[0], other[0])
-    to_x[0] = both(even[3, 0], other[3, 0])
-    to_y[0] = both(even[3, 1], other[3, 1])
-    to_x[1] = both(even[1, 0], other[1, 0])
-    to_y[1] = both(even[2, 1], other[2, 1])
-    rest_x[...] = both(even[1, 1], other[1, 1])
-    rest_y[...] = both(even[2, 0], other[2, 0])
+def sum_over_chip(places, others, own, to_x, to_y, rest_x, rest_y):
+    here, along_x, along_y, far = zip(places, others)
+    own[...] = both(here[0][...], here[1][...])
+    to_x[1] = both(far[0][0], far[1][0])
+    to_y[1] = both(far[0][1], far[1][1])
+    to_x[2] = both(along_x[0][0], along_x[1][0])
+    to_y[2] = both(along_y[0][1], along_y[1][1])
+    rest_x[...] = both(along_x[0][1], along_x[1][1])
+    rest_y[...] = both(along_y[0][0], along_y[1][0])
+
+
+def first_sum_kernel(from_x, from_y, *refs):
+    places, others, outs = refs[:4], refs[4:8], refs[8:]
+    outs[1][0] = from_y[1]
+    outs[2][0] = from_x[2]
+    sum_over_chip(places, others, *outs)
+
+
+def second_sum_kernel(from_x, from_y, rest_x, rest_y, *refs):
+    places, others, outs = refs[:4], refs[4:8], refs[8:]
+    outs[1][0] = both(rest_x[...], from_y[1])
+    outs[2][0] = both(rest_y[...], from_x[1])
+    sum_over_chip(places, others, *outs)
 
 
 def relay_kernel(from_x, from_y, rest_x, rest_y, next_x, next_y):
-    next_x[...] = both(rest_x[...], from_y[0])
-    next_y[...] = both(rest_y[...], from_x[0])
-
-
-def total_kernel(mine, own, from_x, from_y, last_x, last_y, *refs):
+    next_x[...] = both(rest_x[...], from_y[1])
+    next_y[...] = both(rest_y[...], from_x[1])
+
+
+def total_kernel(at_last, mine, own, from_x, from_y, last_x, last_y, *refs):
     outs, total = refs[:-1], refs[-1]
     width = outs[0].shape[1]
     per_half = len(outs) // 2
@@ -508,35 +524,40 @@
     def add(a, b, c):
         return (a.astype(F32) + b.astype(F32) + c.astype(F32)).astype(BF16)
 
-    total[0] = add(own[0], from_x[1], last_y[...])
-    total[1] = add(own[1], last_x[...], from_y[1])
+    total[0] = add(own[0], from_x[2], last_y[at_last])
+    total[1] = add(own[1], last_x[at_last], from_y[2])
     for mask, out in enumerate(outs):
         at = mine[0] ^ mask
         to = pl.multiple_of((at % per_half) * width, width)
         out[...] = total[at // per_half, :, pl.ds(to, width)]
 
 
-def combine_kernel(mine, ids, weights, *refs):
-    parts, out = refs[:-1], refs[-1]
-    masks = N_MASKS
-    chunks = len(parts) // masks
+def combine_kernel(chunk, mine, ids, weights, *refs):
+    parts, out = refs[:N_MASKS], refs[-1]
+    earlier = refs[N_MASKS:-1]
     slots = parts[0].shape[0]
-    rows = out.shape[0]
+    rows = ids.shape[1]
+    share = rows // CHUNKS
+    here = slice(chunk * share, (chunk + 1) * share)
     chosen = ids[...]
-    names, counts = choices(chosen, mine[0], masks, rows, chunks)
-    chunk_of = iota((slots, rows), 1) // (rows // chunks)
+    names, counts = choices(chosen, mine[0], N_MASKS, rows, CHUNKS)
     slot = iota((slots, rows), 0)
     values = jnp.concatenate([part[...] for part in parts], axis=0)
-    result = jnp.zeros(out.shape, F32)
+    columns = jnp.concatenate([weights[...], jnp.zeros((8 - TOPK, rows), F32)], axis=0).T
+    result = jnp.zeros((share, values.shape[1]), F32)
     for k in range(TOPK):
         picks = []
-        for chunk in range(chunks):
-            for mask in range(masks):
-                row = (counts[mask : mask + 1, :] - 1 == slot) & (chosen[k : k + 1, :] == mine[0] ^ mask)
-                picks.append((row & (chunk_of == chunk)).astype(F32))
-        pick = jnp.concatenate(picks, axis=0).T.astype(BF16)
-        result = result + weights[:, k : k + 1] * fast_dot(pick, values)
-    out[...] = result.astype(BF16)
+        for mask in range(N_MASKS):
+            row = (counts[mask : mask + 1, :] - 1 == slot) & (chosen[k : k + 1, :] == mine[0] ^ mask)
+            picks.append(row.astype(F32))
+        pick = jnp.concatenate(picks, axis=0).T[here].astype(BF16)
+        result = result + columns[here, k : k + 1] * fast_dot(pick, values)
+    result = result.astype(BF16)
+    if earlier:
+        out[:share] = earlier[0][...]
+        out[share:] = result
+    else:
+        out[...] = result
 
 
 def directed(x, mask):
@@ -572,67 +593,123 @@
     core = (place & 1).reshape(1)
     chip = place >> 1
     mine = lax.axis_index("exp").reshape(1)
-    ids = expert_ids.T
     block = shape_of((rows, lanes), F32)
     payload = shape_of((states + DECAY_ROWS, lanes), BF16)
-
-    rim = passed_along(conv_input[rows - RIM :], "ctx", 1)
-    mixed, sent, kept, grow, fade = call(
-        mix_kernel, [shape_of((rows, lanes), BF16), payload, payload, block, block], smem=1
-    )(core, conv_input, rim, conv_weight, b_proj, c_proj, log_decay, grad_in)
-    received = swap(sent, "ctx", 1)
-    chip_sum = call(pair_kernel, payload)(received, kept)
-    near, middle, far = (directed(chip_sum, mask) for mask in (2, 4, 6))
-    inner, grad_inner = call(inner_kernel, [block, block])(
-        mixed, b_proj, c_proj, log_decay, grad_in, skip_gain.reshape(1, heads)
-    )
-    later = place & 1
-    flip = jnp.where(later == 1, chip == 2, chip == 1).astype(jnp.int32).reshape(1)
-    prefix = call(reach_kernel, shape_of((states, lanes), BF16), smem=1)(flip, near, middle, far)
-    shared = swap(prefix, "ctx", 1)
-
     slots = 3 * TOPK * rows // (2 * experts * CHUNKS)
-    picked = call(carry_kernel, [shape_of((slots, lanes), BF16)] * (CHUNKS * experts), smem=2)(
-        core, mine, shared, prefix, received, inner, grow, c_proj, ids
-    )
-    grad_conv = call(grad_kernel, block, smem=1)(
-        core, shared, prefix, received, grad_inner, fade, b_proj
-    )
-
-    gain = norm_gain.reshape(1, features)
     half = features // 2
     row_block = shape_of((2, slots, half), BF16)
     half_block = shape_of((slots, half), BF16)
-    up_local, down_local = up_weight[0], down_weight[0]
-    split = [(0, None), (4, None), (1, None), (5, None), (2, None), (6, None), (3, 0), (7, 0), (3, 1), (7, 1)]
-    returned = []
-    for chunk in range(CHUNKS):
+
+    flip = jnp.where(place & 1 == 1, chip == 2, chip == 1).astype(jnp.int32).reshape(1)
+    edge, core, mine, flip = lax.optimization_barrier((conv_input[rows - RIM :], core, mine, flip))
+    rim = passed_along(edge, "ctx", 1)
+    params = [
+        after(log_decay, edge, core, mine, flip),
+        c_proj,
+        grad_in,
+        b_proj,
+        conv_input,
+        conv_weight,
+        skip_gain.reshape(1, heads),
+        norm_gain.reshape(1, features),
+        expert_ids.T,
+        expert_weights.T,
+    ]
+    prepared = pl.pallas_call(
+        lambda *refs: prepare_kernel(len(params), *refs),
+        in_specs=[pl.BlockSpec(memory_space=pltpu.HBM)] * len(params),
+        out_specs=[pl.BlockSpec(memory_space=pltpu.VMEM)] * (len(params) + 4),
+        out_shape=[pltpu.VMEM(p.shape, p.dtype) for p in params]
+        + [block, block, shape_of((states, lanes), BF16), shape_of((DECAY_ROWS, lanes), BF16)],
+        scratch_shapes=[pltpu.SemaphoreType.DMA((len(params),))],
+        cost_estimate=LIGHT,
+        compiler_params=pltpu.CompilerParams(vmem_limit_bytes=6 << 20),
+    )(*(pltpu.with_memory_space_constraint(p, pltpu.HBM) for p in params))
+    decay, c, grad, b, conv, taps, skip, gain, ids, weights, grow, fade, backward, through = prepared
+    mixed, sent, kept = call(
+        mix_kernel, [shape_of((rows, lanes), BF16), payload, payload], smem=1
+    )(core, conv, rim, taps, b, fade, backward, through)
+    received = swap(sent, "ctx", 1)
+    inner, grad_inner = call(inner_kernel, [block, block])(mixed, b, c, decay, grad, skip)
+    chip_sum = call(pair_kernel, payload)(received, after(kept, inner))
+    up = load(after(up_weight[0], chip_sum), 1)
+    near, middle, far = (directed(chip_sum, mask) for mask in (2, 4, 6))
+    prefix = call(reach_kernel, shape_of((states, lanes), BF16), smem=1)(
+        after(flip, up), near, middle, far
+    )
+    shared = swap(prefix, "ctx", 1)
+    picked = call(carry_kernel, [shape_of((slots, lanes), BF16)] * (CHUNKS * experts), smem=2)(
+        core, mine, shared, prefix, received, inner, grow, c, ids
+    )
+    down = load(after(down_weight[0], picked[0]), 1)
+    masks = (2, 3, 1)
+
+    def to_experts(chunk):
         parts = picked[chunk * experts : (chunk + 1) * experts]
-        arrived = [parts[0]] + [swap(parts[m], "exp", m) for m in range(1, experts)]
-        own = call(norm_kernel, row_block, smem=1)(mine, gain, *arrived)
-        twin = swap(own, "ctx", 1)
-        along_x, along_y = swap(own, "ctx", 2), swap(own, "ctx", 4)
-        diagonal = [swap(along_y[0], "ctx", 2), swap(along_x[1], "ctx", 4)]
-        blocks = [own, twin]
-        for block_in in (along_x, along_y, *diagonal):
-            blocks += [block_in, swap(block_in, "ctx", 1)]
-        even, odd = expert_rows(blocks, split, 8, up_local, down_local)
-        other = swap(odd, "ctx", 1)
-        own_sum, to_x, to_y, rest_x, rest_y = call(
-            chip_sum_kernel, [row_block, row_block, row_block, half_block, half_block]
-        )(even, other)
-        from_x, from_y = swap(to_x, "ctx", 2), swap(to_y, "ctx", 4)
-        next_x, next_y = call(relay_kernel, [half_block, half_block])(from_x, from_y, rest_x, rest_y)
-        last_x, last_y = swap(next_x, "ctx", 2), swap(next_y, "ctx", 4)
-        results = call(
-            total_kernel,
+        arrived = {m: swap(parts[m], "exp", m) for m in masks}
+        return [parts[0]] + [arrived[m] for m in range(1, experts)]
+
+    def twin(x):
+        return swap(x, "ctx", 1)
+
+    def along(to_x, to_y):
+        return swap(to_x, "ctx", 2), swap(to_y, "ctx", 4)
+
+    def results(at_last, *sums):
+        return call(
+            lambda *refs: total_kernel(at_last, *refs),
             [shape_of((slots, lanes), BF16)] * experts,
             smem=1,
             scratch=[pltpu.VMEM((2, slots, half), BF16)],
-        )(mine, own_sum, from_x, from_y, last_x, last_y)
-        returned += [results[0]] + [swap(results[m], "exp", m) for m in range(1, experts)]
-    moe_out = call(combine_kernel, shape_of((rows, lanes), BF16), smem=1)(
-        mine, ids, expert_weights, *returned
+        )(mine, *sums)
+
+    def normed(arrived):
+        return call(norm_kernel, row_block, smem=1)(mine, gain, *arrived)
+
+    def back(parts):
+        arrived = {m: swap(parts[m], "exp", m) for m in masks}
+        return [parts[0]] + [arrived[m] for m in range(1, experts)]
+
+    onward = shape_of((3, slots, half), BF16)
+    sums = [row_block, onward, onward, half_block, half_block]
+    share = rows // CHUNKS
+    first1, *others1 = to_experts(0)
+    own1 = normed([after(first1, down), *others1])
+    x1, y1 = along(own1, own1)
+    own2 = normed(to_experts(1))
+    from_x, from_y = along(*call(onward_kernel, [onward, onward])(x1, y1, own2))
+    near1 = [own1, x1, y1]
+    odd1, even1 = expert_rows(near1, [twin(block) for block in near1], up, down)
+    far1, x2, y2 = call(arrive_kernel, [row_block] * 3)(after(from_x, even1[0]), from_y)
+    odd_far1, even_far1 = expert_rows([far1], [twin(far1)], up, down)
+    own_sum1, to_x, to_y, rest_x1, rest_y1 = call(first_sum_kernel, sums)(
+        from_x, from_y, *even1, *even_far1, *(twin(block) for block in (*odd1, *odd_far1))
+    )
+    from_x3, from_y3 = along(to_x, to_y)
+    near2 = [own2, x2, y2]
+    odd2, even2 = expert_rows(
+        [after(own2, own_sum1), x2, y2], [twin(block) for block in near2], up, down
+    )
+    far2 = call(join_kernel, row_block)(after(from_x3, even2[0]), from_y3)
+    odd_far2, even_far2 = expert_rows([far2], [twin(far2)], up, down)
+    own_sum2, to_x, to_y, rest_x2, rest_y2 = call(second_sum_kernel, sums)(
+        from_x3, from_y3, rest_x1, rest_y1,
+        *even2, *even_far2, *(twin(block) for block in (*odd2, *odd_far2)),
+    )
+    from_x4, from_y4 = along(to_x, to_y)
+    next_x, next_y = call(relay_kernel, [half_block, half_block])(from_x4, from_y4, rest_x2, rest_y2)
+    done1 = results(0, own_sum1, from_x3, from_y3, after(from_x4, next_x), from_y4)
+    last_x, last_y = along(next_x, next_y)
+    back1 = back(done1)
+    grad_conv = call(grad_kernel, block, smem=1)(
+        core, shared, after(prefix, done1[0]), received, grad_inner, fade, b
+    )
+    done2 = results(slice(None), after(own_sum2, grad_conv), from_x4, from_y4, last_x, last_y)
+    combined = call(
+        lambda *refs: combine_kernel(0, *refs), shape_of((share, lanes), BF16), smem=1
+    )(mine, after(ids, done2[0]), weights, *back1)
+    moe_out = call(lambda *refs: combine_kernel(1, *refs), shape_of((rows, lanes), BF16), smem=1)(
+        mine, ids, weights, *back(done2), combined
     )
     return (moe_out, grad_conv)
 

time: 174 us -> 141 us (0.81)
  waiting for transfers between devices: 65.1 us -> 52.3 us
  Pallas kernels: 50.6 us -> 42.4 us
  local copies, waits for them, and re-layouts: 6.72 us -> 0.72 us
  starting transfers between devices: 49.3 us -> 44.7 us
    pallas_call x2 -> x3, Pallas kernels: 41.3 us -> 11.3 us  [the longest x2 9.17 us: load(): pl.pallas_call(load_kernel, out_shape=pltpu.VMEM(source.shape, source.dty...]
    pallas_call x15 -> x22, Pallas kernels: 9.27 us -> 31 us  [run(): pl.pallas_call(body, out_shape=outs, in_specs=specs, out_specs=jax.tree.m...]
    ppermute x3, waiting for transfers between devices: 10.9 us -> 4.46 us  [directed(): return lax.ppermute(x, 'ctx', route)]
    unnamed x33 -> x0, local copies, waits for them, and re-layouts: 5.93 us -> none
    ppermute x42 -> x40, waiting for transfers between devices: 53.4 us -> 47.9 us  [swap(): return lax.ppermute(x, axis, [(i, i ^ mask) for i in range(size)])]
    ppermute x42 -> x40, starting transfers between devices: 43.1 us -> 38.3 us  [swap(): return lax.ppermute(x, axis, [(i, i ^ mask) for i in range(size)])]
  transfers between devices with their start and end apart: 46 -> 44, of which waited for: 25 -> 24; matrix products, arithmetic and copies ran while one was open for 0% -> 0% of each run, Pallas kernels for 27% -> 27%
where the time goes in v2:
time: 141 us
  waiting for transfers between devices  52.3 us (37%)
  starting transfers between devices  44.7 us (32%)
  Pallas kernels  42.4 us (30%)
    ppermute x40, waiting for transfers between devices, swap(): return lax.ppermute(x, axis, [(i, i ^ mask) for i in range(size)])  47.9 us
    ppermute x40, starting transfers between devices, swap(): return lax.ppermute(x, axis, [(i, i ^ mask) for i in range(size)])  38.3 us
    pallas_call x22, Pallas kernels, run(): pl.pallas_call(body, out_shape=outs, in_specs=specs, out_specs=jax.tree.m...  31 us
    pallas_call x2, Pallas kernels, load(): pl.pallas_call(load_kernel, out_shape=pltpu.VMEM(source.shape, source.dty...  9.17 us
    ppermute x3, waiting for transfers between devices, directed(): return lax.ppermute(x, 'ctx', route)  4.46 us
    ppermute x3, starting transfers between devices, directed(): return lax.ppermute(x, 'ctx', route)  4.06 us
  transfers between devices with their start and end apart: 44, of which 24 were waited for; matrix products, arithmetic and copies ran while one was open for 0% of the time, Pallas kernels for 27%

profile of v2, /device:TPU:0, one launch (start us, length us, event | category | flops | bytes accessed | tf_op | source)
XLA Modules:
  0.0 141.0 jit_solution(4420508735450575664)
XLA Ops:
  0.6 0.7 slice.3
  1.4 2.3 %collective-permute-start = (bf16[8,1024]{1,0:T(8,128)(2,1)S(1)}, bf16[8,1024]{1,0:T(8,128)(2,1)S(1)}, u32[]{:S(2)}, u32[]{:S(2)}) collective-permute-start(bf16[8,1024]{1,0:T(8,128)(2,1)S(1)} %slice.3), channel_id=1, source_target_pairs={{0,4},{4,8},{8,12},{12,16},{16,20},{20,24},{24,28},{1,5},{5,9},{9,... | collective-permute-start | bytes 49160 | tf_op jit(solution)/shard_map/ppermute | solution.py:19
  3.7 2.2 %shard_map.131 = (f32[16,128]{1,0:T(8,128)S(1)}, bf16[128,128]{1,0:T(8,128)(2,1)S(1)}, bf16[128,1024]{1,0:T(8,128)(2,1)S(1)}, bf16[128,128]{1,0:T(8,128)(2,1)S(1...) custom-call(f32[16,128]{1,0:T(8,128)} %refs_0_, ...), custom_call_target="tpu_custom_call" | custom-call | flops 1 | bytes 1 | tf_op jit(solution)/shard_map/pallas_call | solution.py:618
  6.6 2.7 %collective-permute-start.1 = (bf16[136,1024]{1,0:T(8,128)(2,1)S(1)}, bf16[136,1024]{1,0:T(8,128)(2,1)S(1)}, u32[]{:S(2)}, u32[]{:S(2)}) collective-permute-start(bf16[136,1024]{1,0:T(8,128)(2,1)S(1)} %get-tuple-element.101), channel_id=1, source_target_pairs={{0,4},{4,0},{8,12},{12,8},{16,20},{20,16},{24,28},{28,24},{1,5},{5... | collective-permute-start | bytes 835592 | tf_op jit(solution)/shard_map/ppermute | solution.py:228
  9.3 1.1 shard_map.133
  10.5 1.3 collective-permute-start.2
  11.8 1.3 collective-permute-start.3
  13.1 1.5 %collective-permute-start.4 = (bf16[136,1024]{1,0:T(8,128)(2,1)S(1)}, bf16[136,1024]{1,0:T(8,128)(2,1)S(1)}, u32[]{:S(2)}, u32[]{:S(2)}) collective-permute-start(bf16[136,1024]{1,0:T(8,128)(2,1)S(1)} %shard_map.134), channel_id=1, source_target_pairs={{4,28},{12,20},{16,8},{24,0},{5,29},{13,21},{17,9},{25,1},{6,30},{... | collective-permute-start | bytes 835592 | tf_op jit(solution)/shard_map/ppermute | solution.py:570
  14.6 4.6 %shard_map.135.refs_6_.refs_2_ = bf16[4096,1536]{1,0:T(8,128)(2,1)S(1)} custom-call(bf16[4096,1536]{1,0:T(8,128)(2,1)} %bitcast.9), custom_call_target="tpu_custom_call" | custom-call | flops 1 | bytes 1 | tf_op jit(solution)/shard_map/pallas_call | solution.py:298
  19.2 1.1 collective-permute-done.3.middle
  20.3 3.4 %collective-permute-done.4.far = bf16[136,1024]{1,0:T(8,128)(2,1)S(1)} collective-permute-done((bf16[136,1024]{1,0:T(8,128)(2,1)S(1)}, bf16[136,1024]{1,0:T(8,128)(2,1)S(1)}, u32[]{:S(2)}, u32[]{:S(2)}) %collective-permute-start.4) | collective-permute-done | bytes 278560 | tf_op jit(solution)/shard_map/ppermute | solution.py:570
  23.9 1.5 %collective-permute-done.5.shared = bf16[128,1024]{1,0:T(8,128)(2,1)S(1)} collective-permute-done((bf16[128,1024]{1,0:T(8,128)(2,1)S(1)}, bf16[128,1024]{1,0:T(8,128)(2,1)S(1)}, u32[]{:S(2)}, u32[]{:S(2)}) %collective-permute-start.5) | collective-permute-done | bytes 262176 | tf_op jit(solution)/shard_map/ppermute | solution.py:228
  26.1 1.6 %collective-permute-start.6 = (bf16[48,1024]{1,0:T(8,128)(2,1)S(1)}, bf16[48,1024]{1,0:T(8,128)(2,1)S(1)}, u32[]{:S(2)}, u32[]{:S(2)}) collective-permute-start(bf16[48,1024]{1,0:T(8,128)(2,1)S(1)} %get-tuple-element.116), channel_id=1, source_target_pairs={{0,1},{1,0},{2,3},{3,2},{4,5},{5,4},{6,7},{7,6},{8,9},{9,8},{10,11... | collective-permute-start | bytes 294920 | tf_op jit(solution)/shard_map/ppermute | solution.py:228
  27.8 2.6 %collective-permute-start.7 = (bf16[48,1024]{1,0:T(8,128)(2,1)S(1)}, bf16[48,1024]{1,0:T(8,128)(2,1)S(1)}, u32[]{:S(2)}, u32[]{:S(2)}) collective-permute-start(bf16[48,1024]{1,0:T(8,128)(2,1)S(1)} %get-tuple-element.117), channel_id=1, source_target_pairs={{0,2},{1,3},{2,0},{3,1},{4,6},{5,7},{6,4},{7,5},{8,10},{9,11},{10,... | collective-permute-start | bytes 294920 | tf_op jit(solution)/shard_map/ppermute | solution.py:228
  30.6 4.6 %shard_map.138.refs_7_.refs_3_ = bf16[1536,4096]{1,0:T(8,128)(2,1)S(1)} custom-call(bf16[1536,4096]{1,0:T(8,128)(2,1)} %bitcast.10), custom_call_target="tpu_custom_call" | custom-call | flops 1 | bytes 1 | tf_op jit(solution)/shard_map/pallas_call | solution.py:298
  35.2 3.3 %collective-permute-done.7.refs_2_ = bf16[48,1024]{1,0:T(8,128)(2,1)S(1)} collective-permute-done((bf16[48,1024]{1,0:T(8,128)(2,1)S(1)}, bf16[48,1024]{1,0:T(8,128)(2,1)S(1)}, u32[]{:S(2)}, u32[]{:S(2)}) %collective-permute-start.7) | collective-permute-done | bytes 98336 | tf_op jit(solution)/shard_map/ppermute | solution.py:228
  38.7 2.3 %collective-permute-start.9 = (bf16[2,48,2048]{2,1,0:T(8,128)(2,1)S(1)}, bf16[2,48,2048]{2,1,0:T(8,128)(2,1)S(1)}, u32[]{:S(2)}, u32[]{:S(2)}) collective-permute-start(bf16[2,48,2048]{2,1,0:T(8,128)(2,1)S(1)} %shard_map.139.refs_0_), channel_id=1, source_target_pairs={{0,8},{4,12},{8,0},{12,4},{16,24},{20,28},{24,16},{28,20},{1,9},{5... | collective-permute-start | bytes 1179656 | tf_op jit(solution)/shard_map/ppermute | solution.py:228
  41.0 1.7 %collective-permute-start.11 = (bf16[48,1024]{1,0:T(8,128)(2,1)S(1)}, bf16[48,1024]{1,0:T(8,128)(2,1)S(1)}, u32[]{:S(2)}, u32[]{:S(2)}) collective-permute-start(bf16[48,1024]{1,0:T(8,128)(2,1)S(1)} %get-tuple-element.120), channel_id=1, source_target_pairs={{0,1},{1,0},{2,3},{3,2},{4,5},{5,4},{6,7},{7,6},{8,9},{9,8},{10,11... | collective-permute-start | bytes 294920 | tf_op jit(solution)/shard_map/ppermute | solution.py:228
  42.7 1.4 collective-permute-start.12
  44.1 1.3 collective-permute-start.13
  45.4 0.8 collective-permute-done.11.refs_1_
  46.2 5.7 %collective-permute-done.12.refs_2_ = bf16[48,1024]{1,0:T(8,128)(2,1)S(1)} collective-permute-done((bf16[48,1024]{1,0:T(8,128)(2,1)S(1)}, bf16[48,1024]{1,0:T(8,128)(2,1)S(1)}, u32[]{:S(2)}, u32[]{:S(2)}) %collective-permute-start.12) | collective-permute-done | bytes 98336 | tf_op jit(solution)/shard_map/ppermute | solution.py:228
  52.2 1.5 %collective-permute-start.14 = (bf16[3,48,2048]{2,1,0:T(8,128)(2,1)S(1)}, bf16[3,48,2048]{2,1,0:T(8,128)(2,1)S(1)}, u32[]{:S(2)}, u32[]{:S(2)}) collective-permute-start(bf16[3,48,2048]{2,1,0:T(8,128)(2,1)S(1)} %get-tuple-element.123), channel_id=1, source_target_pairs={{0,8},{4,12},{8,0},{12,4},{16,24},{20,28},{24,16},{28,20},{1,9},{5... | collective-permute-start | bytes 1769480 | tf_op jit(solution)/shard_map/ppermute | solution.py:228
  54.9 1.2 collective-permute-done.16.refs_3_
  57.3 7.5 %shard_map.142 = (bf16[2,48,2048]{2,1,0:T(8,128)(2,1)S(1)}, bf16[2,48,2048]{2,1,0:T(8,128)(2,1)S(1)}, bf16[2,48,2048]{2,1,0:T(8,128)(2,1)S(1)}, bf16[2,48,2048]{...) custom-call(bf16[2,48,2048]{2,1,0:T(8,128)(2,1)S(1)} %shard_map.139.refs_0_, ...), custom_call_target="tpu_custom_call" | custom-call | flops 1 | bytes 1 | tf_op jit(solution)/shard_map/pallas_call | solution.py:213
  66.8 4.1 %shard_map.144 = (bf16[2,48,2048]{2,1,0:T(8,128)(2,1)S(1)}, bf16[2,48,2048]{2,1,0:T(8,128)(2,1)S(1)}) custom-call(bf16[2,48,2048]{2,1,0:T(8,128)(2,1)S(1)} %get-tuple-element.129.refs_0_, bf16[2,48,2048]{2,1,0:T(8,128)(2,1)S(1)} %collective-permute-done.19.refs_1_, bf16[4096,1536]{1,0:T(8,128)(2,1)S(1)} %shard_map.135.refs_6_.refs_2_, ...), custom_call_target="tpu_custom_call" | custom-call | flops 1 | bytes 1 | tf_op jit(solution)/shard_map/pallas_call | solution.py:213
  71.2 1.6 %collective-permute-done.23.refs_7_ = bf16[2,48,2048]{2,1,0:T(8,128)(2,1)S(1)} collective-permute-done((bf16[2,48,2048]{2,1,0:T(8,128)(2,1)S(1)}, bf16[2,48,2048]{2,1,0:T(8,128)(2,1)S(1)}, u32[]{:S(2)}, u32[]{:S(2)}) %collective-permute-start.23) | collective-permute-done | bytes 393248 | tf_op jit(solution)/shard_map/ppermute | solution.py:228
  73.2 1.5 %collective-permute-start.24 = (bf16[3,48,2048]{2,1,0:T(8,128)(2,1)S(1)}, bf16[3,48,2048]{2,1,0:T(8,128)(2,1)S(1)}, u32[]{:S(2)}, u32[]{:S(2)}) collective-permute-start(bf16[3,48,2048]{2,1,0:T(8,128)(2,1)S(1)} %get-tuple-element.135), channel_id=1, source_target_pairs={{0,8},{4,12},{8,0},{12,4},{16,24},{20,28},{24,16},{28,20},{1,9},{5... | collective-permute-start | bytes 1769480 | tf_op jit(solution)/shard_map/ppermute | solution.py:228
  74.7 1.1 collective-permute-start.25
  76.3 1.2 collective-permute-done.26.refs_3_
  78.6 7.7 %shard_map.146 = (bf16[2,48,2048]{2,1,0:T(8,128)(2,1)S(1)}, bf16[2,48,2048]{2,1,0:T(8,128)(2,1)S(1)}, bf16[2,48,2048]{2,1,0:T(8,128)(2,1)S(1)}, bf16[2,48,2048]{...) custom-call(bf16[2,48,2048]{2,1,0:T(8,128)(2,1)S(1)} %shard_map.140.own.refs_0_, ...), custom_call_target="tpu_custom_call" | custom-call | flops 1 | bytes 1 | tf_op jit(solution)/shard_map/pallas_call | solution.py:213
  86.3 2.3 %collective-permute-done.24.from_x.refs_2_ = bf16[3,48,2048]{2,1,0:T(8,128)(2,1)S(1)} collective-permute-done((bf16[3,48,2048]{2,1,0:T(8,128)(2,1)S(1)}, bf16[3,48,2048]{2,1,0:T(8,128)(2,1)S(1)}, u32[]{:S(2)}, u32[]{:S(2)}) %collective-permute-start.24) | collective-permute-done | bytes 589856 | tf_op jit(solution)/shard_map/ppermute | solution.py:228
  88.6 1.2 collective-permute-done.25.from_y.refs_3_
  91.6 4.1 %shard_map.148 = (bf16[2,48,2048]{2,1,0:T(8,128)(2,1)S(1)}, bf16[2,48,2048]{2,1,0:T(8,128)(2,1)S(1)}) custom-call(bf16[2,48,2048]{2,1,0:T(8,128)(2,1)S(1)} %shard_map.147.refs_0_, bf16[2,48,2048]{2,1,0:T(8,128)(2,1)S(1)} %collective-permute-done.29.refs_1_, bf16[4096,1536]{1,0:T(8,128)(2,1)S(1)} %shard_map.135.refs_6_.refs_2_, ...), custom_call_target="tpu_custom_call" | custom-call | flops 1 | bytes 1 | tf_op jit(solution)/shard_map/pallas_call | solution.py:213
  95.9 1.6 %collective-permute-done.33.refs_7_ = bf16[2,48,2048]{2,1,0:T(8,128)(2,1)S(1)} collective-permute-done((bf16[2,48,2048]{2,1,0:T(8,128)(2,1)S(1)}, bf16[2,48,2048]{2,1,0:T(8,128)(2,1)S(1)}, u32[]{:S(2)}, u32[]{:S(2)}) %collective-permute-start.33) | collective-permute-done | bytes 393248 | tf_op jit(solution)/shard_map/ppermute | solution.py:228
  98.6 1.1 collective-permute-start.35
  99.7 13.7 %collective-permute-done.34.from_x.refs_4_.refs_2_ = bf16[3,48,2048]{2,1,0:T(8,128)(2,1)S(1)} collective-permute-done((bf16[3,48,2048]{2,1,0:T(8,128)(2,1)S(1)}, bf16[3,48,2048]{2,1,0:T(8,128)(2,1)S(1)}, u32[]{:S(2)}, u32[]{:S(2)}) %collective-permute-start.34) | collective-permute-done | bytes 589856 | tf_op jit(solution)/shard_map/ppermute | solution.py:228
  113.8 1.5 %collective-permute-start.36 = (bf16[48,2048]{1,0:T(8,128)(2,1)S(1)}, bf16[48,2048]{1,0:T(8,128)(2,1)S(1)}, u32[]{:S(2)}, u32[]{:S(2)}) collective-permute-start(bf16[48,2048]{1,0:T(8,128)(2,1)S(1)} %get-tuple-element.157), channel_id=1, source_target_pairs={{0,8},{4,12},{8,0},{12,4},{16,24},{20,28},{24,16},{28,20},{1,9},{5... | collective-permute-start | bytes 589832 | tf_op jit(solution)/shard_map/ppermute | solution.py:228
  115.3 1.1 collective-permute-start.37
  116.7 4.8 %collective-permute-start.41 = (bf16[48,1024]{1,0:T(8,128)(2,1)S(1)}, bf16[48,1024]{1,0:T(8,128)(2,1)S(1)}, u32[]{:S(2)}, u32[]{:S(2)}) collective-permute-start(bf16[48,1024]{1,0:T(8,128)(2,1)S(1)} %get-tuple-element.169), channel_id=1, source_target_pairs={{0,1},{1,0},{2,3},{3,2},{4,5},{5,4},{6,7},{7,6},{8,9},{9,8},{10,11... | collective-permute-start | bytes 294920 | tf_op jit(solution)/shard_map/ppermute | solution.py:228
  121.5 1.1 shard_map.152
  123.0 2.0 %collective-permute-start.43 = (bf16[48,1024]{1,0:T(8,128)(2,1)S(1)}, bf16[48,1024]{1,0:T(8,128)(2,1)S(1)}, u32[]{:S(2)}, u32[]{:S(2)}) collective-permute-start(bf16[48,1024]{1,0:T(8,128)(2,1)S(1)} %get-tuple-element.171), channel_id=1, source_target_pairs={{0,3},{1,2},{2,1},{3,0},{4,7},{5,6},{6,5},{7,4},{8,11},{9,10},{10,... | collective-permute-start | bytes 294920 | tf_op jit(solution)/shard_map/ppermute | solution.py:228
  125.3 1.2 collective-permute-start.38
  126.4 1.3 collective-permute-start.39
  127.7 2.0 %collective-permute-start.40 = (bf16[48,1024]{1,0:T(8,128)(2,1)S(1)}, bf16[48,1024]{1,0:T(8,128)(2,1)S(1)}, u32[]{:S(2)}, u32[]{:S(2)}) collective-permute-start(bf16[48,1024]{1,0:T(8,128)(2,1)S(1)} %get-tuple-element.167), channel_id=1, source_target_pairs={{0,3},{1,2},{2,1},{3,0},{4,7},{5,6},{6,5},{7,4},{8,11},{9,10},{10,... | collective-permute-start | bytes 294920 | tf_op jit(solution)/shard_map/ppermute | solution.py:228
  129.7 6.0 %collective-permute-done.42.refs_5_ = bf16[48,1024]{1,0:T(8,128)(2,1)S(1)} collective-permute-done((bf16[48,1024]{1,0:T(8,128)(2,1)S(1)}, bf16[48,1024]{1,0:T(8,128)(2,1)S(1)}, u32[]{:S(2)}, u32[]{:S(2)}) %collective-permute-start.42) | collective-permute-done | bytes 98336 | tf_op jit(solution)/shard_map/ppermute | solution.py:228
  136.2 3.6 %collective-permute-done.39.refs_5_ = bf16[48,1024]{1,0:T(8,128)(2,1)S(1)} collective-permute-done((bf16[48,1024]{1,0:T(8,128)(2,1)S(1)}, bf16[48,1024]{1,0:T(8,128)(2,1)S(1)}, u32[]{:S(2)}, u32[]{:S(2)}) %collective-permute-start.39) | collective-permute-done | bytes 98336 | tf_op jit(solution)/shard_map/ppermute | solution.py:228
  139.8 1.2 shard_map.155
  (66 shorter events, 14.1 us)
Async XLA Ops:
  1.4 4.5 %collective-permute-start = (bf16[8,1024]{1,0:T(8,128)(2,1)S(1)}, bf16[8,1024]{1,0:T(8,128)(2,1)S(1)}, u32[]{:S(2)}, u32[]{:S(2)}) collective-permute-start(bf16[8,1024]{1,0:T(8,128)(2,1)S(1)} %slice.3), channel_id=1, source_target_pairs={{0,4},{4,8},{8,12},{12,16},{16,20},{20,24},{24,28},{1,5},{5,9},{9,... | collective-permute-start | bytes 49160 | tf_op jit(solution)/shard_map/ppermute | solution.py:19
  6.6 3.9 %collective-permute-start.1 = (bf16[136,1024]{1,0:T(8,128)(2,1)S(1)}, bf16[136,1024]{1,0:T(8,128)(2,1)S(1)}, u32[]{:S(2)}, u32[]{:S(2)}) collective-permute-start(bf16[136,1024]{1,0:T(8,128)(2,1)S(1)} %get-tuple-element.101), channel_id=1, source_target_pairs={{0,4},{4,0},{8,12},{12,8},{16,20},{20,16},{24,28},{28,24},{1,5},{5... | collective-permute-start | bytes 835592 | tf_op jit(solution)/shard_map/ppermute | solution.py:228
  10.5 8.7 %collective-permute-start.2 = (bf16[136,1024]{1,0:T(8,128)(2,1)S(1)}, bf16[136,1024]{1,0:T(8,128)(2,1)S(1)}, u32[]{:S(2)}, u32[]{:S(2)}) collective-permute-start(bf16[136,1024]{1,0:T(8,128)(2,1)S(1)} %shard_map.134), channel_id=1, source_target_pairs={{4,12},{8,0},{20,28},{24,16},{5,13},{9,1},{21,29},{25,17},{6,14},{... | collective-permute-start | bytes 835592 | tf_op jit(solution)/shard_map/ppermute | solution.py:570
  11.8 8.4 %collective-permute-start.3 = (bf16[136,1024]{1,0:T(8,128)(2,1)S(1)}, bf16[136,1024]{1,0:T(8,128)(2,1)S(1)}, u32[]{:S(2)}, u32[]{:S(2)}) collective-permute-start(bf16[136,1024]{1,0:T(8,128)(2,1)S(1)} %shard_map.134), channel_id=1, source_target_pairs={{4,20},{12,28},{16,0},{24,8},{5,21},{13,29},{17,1},{25,9},{6,22},{... | collective-permute-start | bytes 835592 | tf_op jit(solution)/shard_map/ppermute | solution.py:570
  13.1 10.5 %collective-permute-start.4 = (bf16[136,1024]{1,0:T(8,128)(2,1)S(1)}, bf16[136,1024]{1,0:T(8,128)(2,1)S(1)}, u32[]{:S(2)}, u32[]{:S(2)}) collective-permute-start(bf16[136,1024]{1,0:T(8,128)(2,1)S(1)} %shard_map.134), channel_id=1, source_target_pairs={{4,28},{12,20},{16,8},{24,0},{5,29},{13,21},{17,9},{25,1},{6,30},{... | collective-permute-start | bytes 835592 | tf_op jit(solution)/shard_map/ppermute | solution.py:570
  23.9 1.6 %collective-permute-start.5 = (bf16[128,1024]{1,0:T(8,128)(2,1)S(1)}, bf16[128,1024]{1,0:T(8,128)(2,1)S(1)}, u32[]{:S(2)}, u32[]{:S(2)}) collective-permute-start(bf16[128,1024]{1,0:T(8,128)(2,1)S(1)} %shard_map.136.prefix), channel_id=1, source_target_pairs={{0,4},{4,0},{8,12},{12,8},{16,20},{20,16},{24,28},{28,24},{1,5},{5... | collective-permute-start | bytes 786440 | tf_op jit(solution)/shard_map/ppermute | solution.py:228
  26.1 9.0 %collective-permute-start.6 = (bf16[48,1024]{1,0:T(8,128)(2,1)S(1)}, bf16[48,1024]{1,0:T(8,128)(2,1)S(1)}, u32[]{:S(2)}, u32[]{:S(2)}) collective-permute-start(bf16[48,1024]{1,0:T(8,128)(2,1)S(1)} %get-tuple-element.116), channel_id=1, source_target_pairs={{0,1},{1,0},{2,3},{3,2},{4,5},{5,4},{6,7},{7,6},{8,9},{9,8},{10,11... | collective-permute-start | bytes 294920 | tf_op jit(solution)/shard_map/ppermute | solution.py:228
  27.8 10.7 %collective-permute-start.7 = (bf16[48,1024]{1,0:T(8,128)(2,1)S(1)}, bf16[48,1024]{1,0:T(8,128)(2,1)S(1)}, u32[]{:S(2)}, u32[]{:S(2)}) collective-permute-start(bf16[48,1024]{1,0:T(8,128)(2,1)S(1)} %get-tuple-element.117), channel_id=1, source_target_pairs={{0,2},{1,3},{2,0},{3,1},{4,6},{5,7},{6,4},{7,5},{8,10},{9,11},{10,... | collective-permute-start | bytes 294920 | tf_op jit(solution)/shard_map/ppermute | solution.py:228
  30.4 8.1 %collective-permute-start.8 = (bf16[48,1024]{1,0:T(8,128)(2,1)S(1)}, bf16[48,1024]{1,0:T(8,128)(2,1)S(1)}, u32[]{:S(2)}, u32[]{:S(2)}) collective-permute-start(bf16[48,1024]{1,0:T(8,128)(2,1)S(1)} %get-tuple-element.118), channel_id=1, source_target_pairs={{0,3},{1,2},{2,1},{3,0},{4,7},{5,6},{6,5},{7,4},{8,11},{9,10},{10,... | collective-permute-start | bytes 294920 | tf_op jit(solution)/shard_map/ppermute | solution.py:228
  38.7 13.4 %collective-permute-start.9 = (bf16[2,48,2048]{2,1,0:T(8,128)(2,1)S(1)}, bf16[2,48,2048]{2,1,0:T(8,128)(2,1)S(1)}, u32[]{:S(2)}, u32[]{:S(2)}) collective-permute-start(bf16[2,48,2048]{2,1,0:T(8,128)(2,1)S(1)} %shard_map.139.refs_0_), channel_id=1, source_target_pairs={{0,8},{4,12},{8,0},{12,4},{16,24},{20,28},{24,16},{28,20},{1,9},{5... | collective-permute-start | bytes 1179656 | tf_op jit(solution)/shard_map/ppermute | solution.py:228
  41.0 11.1 %collective-permute-start.10 = (bf16[2,48,2048]{2,1,0:T(8,128)(2,1)S(1)}, bf16[2,48,2048]{2,1,0:T(8,128)(2,1)S(1)}, u32[]{:S(2)}, u32[]{:S(2)}) collective-permute-start(bf16[2,48,2048]{2,1,0:T(8,128)(2,1)S(1)} %shard_map.139.refs_0_), channel_id=1, source_target_pairs={{0,16},{4,20},{8,24},{12,28},{16,0},{20,4},{24,8},{28,12},{1,17},{... | collective-permute-start | bytes 1179656 | tf_op jit(solution)/shard_map/ppermute | solution.py:228
  41.0 5.2 %collective-permute-start.11 = (bf16[48,1024]{1,0:T(8,128)(2,1)S(1)}, bf16[48,1024]{1,0:T(8,128)(2,1)S(1)}, u32[]{:S(2)}, u32[]{:S(2)}) collective-permute-start(bf16[48,1024]{1,0:T(8,128)(2,1)S(1)} %get-tuple-element.120), channel_id=1, source_target_pairs={{0,1},{1,0},{2,3},{3,2},{4,5},{5,4},{6,7},{7,6},{8,9},{9,8},{10,11... | collective-permute-start | bytes 294920 | tf_op jit(solution)/shard_map/ppermute | solution.py:228
  42.7 9.2 %collective-permute-start.12 = (bf16[48,1024]{1,0:T(8,128)(2,1)S(1)}, bf16[48,1024]{1,0:T(8,128)(2,1)S(1)}, u32[]{:S(2)}, u32[]{:S(2)}) collective-permute-start(bf16[48,1024]{1,0:T(8,128)(2,1)S(1)} %get-tuple-element.121), channel_id=1, source_target_pairs={{0,2},{1,3},{2,0},{3,1},{4,6},{5,7},{6,4},{7,5},{8,10},{9,11},{10,... | collective-permute-start | bytes 294920 | tf_op jit(solution)/shard_map/ppermute | solution.py:228
  44.1 7.8 %collective-permute-start.13 = (bf16[48,1024]{1,0:T(8,128)(2,1)S(1)}, bf16[48,1024]{1,0:T(8,128)(2,1)S(1)}, u32[]{:S(2)}, u32[]{:S(2)}) collective-permute-start(bf16[48,1024]{1,0:T(8,128)(2,1)S(1)} %get-tuple-element.122), channel_id=1, source_target_pairs={{0,3},{1,2},{2,1},{3,0},{4,7},{5,6},{6,5},{7,4},{8,11},{9,10},{10,... | collective-permute-start | bytes 294920 | tf_op jit(solution)/shard_map/ppermute | solution.py:228
  52.2 12.5 %collective-permute-start.14 = (bf16[3,48,2048]{2,1,0:T(8,128)(2,1)S(1)}, bf16[3,48,2048]{2,1,0:T(8,128)(2,1)S(1)}, u32[]{:S(2)}, u32[]{:S(2)}) collective-permute-start(bf16[3,48,2048]{2,1,0:T(8,128)(2,1)S(1)} %get-tuple-element.123), channel_id=1, source_target_pairs={{0,8},{4,12},{8,0},{12,4},{16,24},{20,28},{24,16},{28,20},{1,9},{5... | collective-permute-start | bytes 1769480 | tf_op jit(solution)/shard_map/ppermute | solution.py:228
  53.7 11.3 %collective-permute-start.15 = (bf16[3,48,2048]{2,1,0:T(8,128)(2,1)S(1)}, bf16[3,48,2048]{2,1,0:T(8,128)(2,1)S(1)}, u32[]{:S(2)}, u32[]{:S(2)}) collective-permute-start(bf16[3,48,2048]{2,1,0:T(8,128)(2,1)S(1)} %get-tuple-element.124), channel_id=1, source_target_pairs={{0,16},{4,20},{8,24},{12,28},{16,0},{20,4},{24,8},{28,12},{1,17},{... | collective-permute-start | bytes 1769480 | tf_op jit(solution)/shard_map/ppermute | solution.py:228
  54.4 1.7 %collective-permute-start.16 = (bf16[2,48,2048]{2,1,0:T(8,128)(2,1)S(1)}, bf16[2,48,2048]{2,1,0:T(8,128)(2,1)S(1)}, u32[]{:S(2)}, u32[]{:S(2)}) collective-permute-start(bf16[2,48,2048]{2,1,0:T(8,128)(2,1)S(1)} %shard_map.139.refs_0_), channel_id=1, source_target_pairs={{0,4},{4,0},{8,12},{12,8},{16,20},{20,16},{24,28},{28,24},{1,5},{5... | collective-permute-start | bytes 1179656 | tf_op jit(solution)/shard_map/ppermute | solution.py:228
  54.4 2.3 %collective-permute-start.17 = (bf16[2,48,2048]{2,1,0:T(8,128)(2,1)S(1)}, bf16[2,48,2048]{2,1,0:T(8,128)(2,1)S(1)}, u32[]{:S(2)}, u32[]{:S(2)}) collective-permute-start(bf16[2,48,2048]{2,1,0:T(8,128)(2,1)S(1)} %collective-permute-done.9.along_x.refs_1_), channel_id=1, source_target_pairs={{0,4},{4,0},{8,12},{12,8},{16,20},{20,16},{24,28},{28,24},{1,5},{5... | collective-permute-start | bytes 1179656 | tf_op jit(solution)/shard_map/ppermute | solution.py:228
  54.9 2.3 %collective-permute-start.18 = (bf16[2,48,2048]{2,1,0:T(8,128)(2,1)S(1)}, bf16[2,48,2048]{2,1,0:T(8,128)(2,1)S(1)}, u32[]{:S(2)}, u32[]{:S(2)}) collective-permute-start(bf16[2,48,2048]{2,1,0:T(8,128)(2,1)S(1)} %collective-permute-done.10.along_y.refs_2_), channel_id=1, source_target_pairs={{0,4},{4,0},{8,12},{12,8},{16,20},{20,16},{24,28},{28,24},{1,5},{5... | collective-permute-start | bytes 1179656 | tf_op jit(solution)/shard_map/ppermute | solution.py:228
  65.0 1.8 %collective-permute-start.19 = (bf16[2,48,2048]{2,1,0:T(8,128)(2,1)S(1)}, bf16[2,48,2048]{2,1,0:T(8,128)(2,1)S(1)}, u32[]{:S(2)}, u32[]{:S(2)}) collective-permute-start(bf16[2,48,2048]{2,1,0:T(8,128)(2,1)S(1)} %get-tuple-element.129.refs_0_), channel_id=1, source_target_pairs={{0,4},{4,0},{8,12},{12,8},{16,20},{20,16},{24,28},{28,24},{1,5},{5... | collective-permute-start | bytes 1179656 | tf_op jit(solution)/shard_map/ppermute | solution.py:228
  65.1 6.1 %collective-permute-start.20 = (bf16[2,48,2048]{2,1,0:T(8,128)(2,1)S(1)}, bf16[2,48,2048]{2,1,0:T(8,128)(2,1)S(1)}, u32[]{:S(2)}, u32[]{:S(2)}) collective-permute-start(bf16[2,48,2048]{2,1,0:T(8,128)(2,1)S(1)} %get-tuple-element.131), channel_id=1, source_target_pairs={{0,4},{4,0},{8,12},{12,8},{16,20},{20,16},{24,28},{28,24},{1,5},{5... | collective-permute-start | bytes 1179656 | tf_op jit(solution)/shard_map/ppermute | solution.py:228
  65.6 5.6 %collective-permute-start.21 = (bf16[2,48,2048]{2,1,0:T(8,128)(2,1)S(1)}, bf16[2,48,2048]{2,1,0:T(8,128)(2,1)S(1)}, u32[]{:S(2)}, u32[]{:S(2)}) collective-permute-start(bf16[2,48,2048]{2,1,0:T(8,128)(2,1)S(1)} %get-tuple-element.132), channel_id=1, source_target_pairs={{0,4},{4,0},{8,12},{12,8},{16,20},{20,16},{24,28},{28,24},{1,5},{5... | collective-permute-start | bytes 1179656 | tf_op jit(solution)/shard_map/ppermute | solution.py:228
  65.7 5.5 %collective-permute-start.22 = (bf16[2,48,2048]{2,1,0:T(8,128)(2,1)S(1)}, bf16[2,48,2048]{2,1,0:T(8,128)(2,1)S(1)}, u32[]{:S(2)}, u32[]{:S(2)}) collective-permute-start(bf16[2,48,2048]{2,1,0:T(8,128)(2,1)S(1)} %get-tuple-element.133), channel_id=1, source_target_pairs={{0,4},{4,0},{8,12},{12,8},{16,20},{20,16},{24,28},{28,24},{1,5},{5... | collective-permute-start | bytes 1179656 | tf_op jit(solution)/shard_map/ppermute | solution.py:228
  71.0 1.8 %collective-permute-start.23 = (bf16[2,48,2048]{2,1,0:T(8,128)(2,1)S(1)}, bf16[2,48,2048]{2,1,0:T(8,128)(2,1)S(1)}, u32[]{:S(2)}, u32[]{:S(2)}) collective-permute-start(bf16[2,48,2048]{2,1,0:T(8,128)(2,1)S(1)} %get-tuple-element.134), channel_id=1, source_target_pairs={{0,4},{4,0},{8,12},{12,8},{16,20},{20,16},{24,28},{28,24},{1,5},{5... | collective-permute-start | bytes 1179656 | tf_op jit(solution)/shard_map/ppermute | solution.py:228
  73.2 15.4 %collective-permute-start.24 = (bf16[3,48,2048]{2,1,0:T(8,128)(2,1)S(1)}, bf16[3,48,2048]{2,1,0:T(8,128)(2,1)S(1)}, u32[]{:S(2)}, u32[]{:S(2)}) collective-permute-start(bf16[3,48,2048]{2,1,0:T(8,128)(2,1)S(1)} %get-tuple-element.135), channel_id=1, source_target_pairs={{0,8},{4,12},{8,0},{12,4},{16,24},{20,28},{24,16},{28,20},{1,9},{5... | collective-permute-start | bytes 1769480 | tf_op jit(solution)/shard_map/ppermute | solution.py:228
  74.7 15.1 %collective-permute-start.25 = (bf16[3,48,2048]{2,1,0:T(8,128)(2,1)S(1)}, bf16[3,48,2048]{2,1,0:T(8,128)(2,1)S(1)}, u32[]{:S(2)}, u32[]{:S(2)}) collective-permute-start(bf16[3,48,2048]{2,1,0:T(8,128)(2,1)S(1)} %get-tuple-element.136), channel_id=1, source_target_pairs={{0,16},{4,20},{8,24},{12,28},{16,0},{20,4},{24,8},{28,12},{1,17},{... | collective-permute-start | bytes 1769480 | tf_op jit(solution)/shard_map/ppermute | solution.py:228
  75.8 1.7 %collective-permute-start.26 = (bf16[2,48,2048]{2,1,0:T(8,128)(2,1)S(1)}, bf16[2,48,2048]{2,1,0:T(8,128)(2,1)S(1)}, u32[]{:S(2)}, u32[]{:S(2)}) collective-permute-start(bf16[2,48,2048]{2,1,0:T(8,128)(2,1)S(1)} %shard_map.140.own.refs_0_), channel_id=1, source_target_pairs={{0,4},{4,0},{8,12},{12,8},{16,20},{20,16},{24,28},{28,24},{1,5},{5... | collective-permute-start | bytes 1179656 | tf_op jit(solution)/shard_map/ppermute | solution.py:228
  75.8 2.3 %collective-permute-start.27 = (bf16[2,48,2048]{2,1,0:T(8,128)(2,1)S(1)}, bf16[2,48,2048]{2,1,0:T(8,128)(2,1)S(1)}, u32[]{:S(2)}, u32[]{:S(2)}) collective-permute-start(bf16[2,48,2048]{2,1,0:T(8,128)(2,1)S(1)} %get-tuple-element.141.refs_1_), channel_id=1, source_target_pairs={{0,4},{4,0},{8,12},{12,8},{16,20},{20,16},{24,28},{28,24},{1,5},{5... | collective-permute-start | bytes 1179656 | tf_op jit(solution)/shard_map/ppermute | solution.py:228
  76.3 2.3 %collective-permute-start.28 = (bf16[2,48,2048]{2,1,0:T(8,128)(2,1)S(1)}, bf16[2,48,2048]{2,1,0:T(8,128)(2,1)S(1)}, u32[]{:S(2)}, u32[]{:S(2)}) collective-permute-start(bf16[2,48,2048]{2,1,0:T(8,128)(2,1)S(1)} %get-tuple-element.142.refs_2_), channel_id=1, source_target_pairs={{0,4},{4,0},{8,12},{12,8},{16,20},{20,16},{24,28},{28,24},{1,5},{5... | collective-permute-start | bytes 1179656 | tf_op jit(solution)/shard_map/ppermute | solution.py:228
  89.8 1.8 %collective-permute-start.29 = (bf16[2,48,2048]{2,1,0:T(8,128)(2,1)S(1)}, bf16[2,48,2048]{2,1,0:T(8,128)(2,1)S(1)}, u32[]{:S(2)}, u32[]{:S(2)}) collective-permute-start(bf16[2,48,2048]{2,1,0:T(8,128)(2,1)S(1)} %shard_map.147.refs_0_), channel_id=1, source_target_pairs={{0,4},{4,0},{8,12},{12,8},{16,20},{20,16},{24,28},{28,24},{1,5},{5... | collective-permute-start | bytes 1179656 | tf_op jit(solution)/shard_map/ppermute | solution.py:228
  89.9 6.1 %collective-permute-start.30 = (bf16[2,48,2048]{2,1,0:T(8,128)(2,1)S(1)}, bf16[2,48,2048]{2,1,0:T(8,128)(2,1)S(1)}, u32[]{:S(2)}, u32[]{:S(2)}) collective-permute-start(bf16[2,48,2048]{2,1,0:T(8,128)(2,1)S(1)} %get-tuple-element.148), channel_id=1, source_target_pairs={{0,4},{4,0},{8,12},{12,8},{16,20},{20,16},{24,28},{28,24},{1,5},{5... | collective-permute-start | bytes 1179656 | tf_op jit(solution)/shard_map/ppermute | solution.py:228
  90.4 5.6 %collective-permute-start.31 = (bf16[2,48,2048]{2,1,0:T(8,128)(2,1)S(1)}, bf16[2,48,2048]{2,1,0:T(8,128)(2,1)S(1)}, u32[]{:S(2)}, u32[]{:S(2)}) collective-permute-start(bf16[2,48,2048]{2,1,0:T(8,128)(2,1)S(1)} %get-tuple-element.149), channel_id=1, source_target_pairs={{0,4},{4,0},{8,12},{12,8},{16,20},{20,16},{24,28},{28,24},{1,5},{5... | collective-permute-start | bytes 1179656 | tf_op jit(solution)/shard_map/ppermute | solution.py:228
  90.5 5.5 %collective-permute-start.32 = (bf16[2,48,2048]{2,1,0:T(8,128)(2,1)S(1)}, bf16[2,48,2048]{2,1,0:T(8,128)(2,1)S(1)}, u32[]{:S(2)}, u32[]{:S(2)}) collective-permute-start(bf16[2,48,2048]{2,1,0:T(8,128)(2,1)S(1)} %get-tuple-element.150), channel_id=1, source_target_pairs={{0,4},{4,0},{8,12},{12,8},{16,20},{20,16},{24,28},{28,24},{1,5},{5... | collective-permute-start | bytes 1179656 | tf_op jit(solution)/shard_map/ppermute | solution.py:228
  95.7 1.8 %collective-permute-start.33 = (bf16[2,48,2048]{2,1,0:T(8,128)(2,1)S(1)}, bf16[2,48,2048]{2,1,0:T(8,128)(2,1)S(1)}, u32[]{:S(2)}, u32[]{:S(2)}) collective-permute-start(bf16[2,48,2048]{2,1,0:T(8,128)(2,1)S(1)} %get-tuple-element.151), channel_id=1, source_target_pairs={{0,4},{4,0},{8,12},{12,8},{16,20},{20,16},{24,28},{28,24},{1,5},{5... | collective-permute-start | bytes 1179656 | tf_op jit(solution)/shard_map/ppermute | solution.py:228
  98.0 15.4 %collective-permute-start.34 = (bf16[3,48,2048]{2,1,0:T(8,128)(2,1)S(1)}, bf16[3,48,2048]{2,1,0:T(8,128)(2,1)S(1)}, u32[]{:S(2)}, u32[]{:S(2)}) collective-permute-start(bf16[3,48,2048]{2,1,0:T(8,128)(2,1)S(1)} %get-tuple-element.153), channel_id=1, source_target_pairs={{0,8},{4,12},{8,0},{12,4},{16,24},{20,28},{24,16},{28,20},{1,9},{5... | collective-permute-start | bytes 1769480 | tf_op jit(solution)/shard_map/ppermute | solution.py:228
  98.6 15.1 %collective-permute-start.35 = (bf16[3,48,2048]{2,1,0:T(8,128)(2,1)S(1)}, bf16[3,48,2048]{2,1,0:T(8,128)(2,1)S(1)}, u32[]{:S(2)}, u32[]{:S(2)}) collective-permute-start(bf16[3,48,2048]{2,1,0:T(8,128)(2,1)S(1)} %get-tuple-element.154), channel_id=1, source_target_pairs={{0,16},{4,20},{8,24},{12,28},{16,0},{20,4},{24,8},{28,12},{1,17},{... | collective-permute-start | bytes 1769480 | tf_op jit(solution)/shard_map/ppermute | solution.py:228
  113.8 11.2 %collective-permute-start.36 = (bf16[48,2048]{1,0:T(8,128)(2,1)S(1)}, bf16[48,2048]{1,0:T(8,128)(2,1)S(1)}, u32[]{:S(2)}, u32[]{:S(2)}) collective-permute-start(bf16[48,2048]{1,0:T(8,128)(2,1)S(1)} %get-tuple-element.157), channel_id=1, source_target_pairs={{0,8},{4,12},{8,0},{12,4},{16,24},{20,28},{24,16},{28,20},{1,9},{5... | collective-permute-start | bytes 589832 | tf_op jit(solution)/shard_map/ppermute | solution.py:228
  115.3 9.7 %collective-permute-start.37 = (bf16[48,2048]{1,0:T(8,128)(2,1)S(1)}, bf16[48,2048]{1,0:T(8,128)(2,1)S(1)}, u32[]{:S(2)}, u32[]{:S(2)}) collective-permute-start(bf16[48,2048]{1,0:T(8,128)(2,1)S(1)} %get-tuple-element.163), channel_id=1, source_target_pairs={{0,16},{4,20},{8,24},{12,28},{16,0},{20,4},{24,8},{28,12},{1,17},{... | collective-permute-start | bytes 589832 | tf_op jit(solution)/shard_map/ppermute | solution.py:228
  116.7 11.1 %collective-permute-start.41 = (bf16[48,1024]{1,0:T(8,128)(2,1)S(1)}, bf16[48,1024]{1,0:T(8,128)(2,1)S(1)}, u32[]{:S(2)}, u32[]{:S(2)}) collective-permute-start(bf16[48,1024]{1,0:T(8,128)(2,1)S(1)} %get-tuple-element.169), channel_id=1, source_target_pairs={{0,1},{1,0},{2,3},{3,2},{4,5},{5,4},{6,7},{7,6},{8,9},{9,8},{10,11... | collective-permute-start | bytes 294920 | tf_op jit(solution)/shard_map/ppermute | solution.py:228
  122.6 13.1 %collective-permute-start.42 = (bf16[48,1024]{1,0:T(8,128)(2,1)S(1)}, bf16[48,1024]{1,0:T(8,128)(2,1)S(1)}, u32[]{:S(2)}, u32[]{:S(2)}) collective-permute-start(bf16[48,1024]{1,0:T(8,128)(2,1)S(1)} %get-tuple-element.170), channel_id=1, source_target_pairs={{0,2},{1,3},{2,0},{3,1},{4,6},{5,7},{6,4},{7,5},{8,10},{9,11},{10,... | collective-permute-start | bytes 294920 | tf_op jit(solution)/shard_map/ppermute | solution.py:228
  123.0 12.7 %collective-permute-start.43 = (bf16[48,1024]{1,0:T(8,128)(2,1)S(1)}, bf16[48,1024]{1,0:T(8,128)(2,1)S(1)}, u32[]{:S(2)}, u32[]{:S(2)}) collective-permute-start(bf16[48,1024]{1,0:T(8,128)(2,1)S(1)} %get-tuple-element.171), channel_id=1, source_target_pairs={{0,3},{1,2},{2,1},{3,0},{4,7},{5,6},{6,5},{7,4},{8,11},{9,10},{10,... | collective-permute-start | bytes 294920 | tf_op jit(solution)/shard_map/ppermute | solution.py:228
  125.3 10.9 %collective-permute-start.38 = (bf16[48,1024]{1,0:T(8,128)(2,1)S(1)}, bf16[48,1024]{1,0:T(8,128)(2,1)S(1)}, u32[]{:S(2)}, u32[]{:S(2)}) collective-permute-start(bf16[48,1024]{1,0:T(8,128)(2,1)S(1)} %get-tuple-element.165), channel_id=1, source_target_pairs={{0,1},{1,0},{2,3},{3,2},{4,5},{5,4},{6,7},{7,6},{8,9},{9,8},{10,11... | collective-permute-start | bytes 294920 | tf_op jit(solution)/shard_map/ppermute | solution.py:228
  126.4 13.3 %collective-permute-start.39 = (bf16[48,1024]{1,0:T(8,128)(2,1)S(1)}, bf16[48,1024]{1,0:T(8,128)(2,1)S(1)}, u32[]{:S(2)}, u32[]{:S(2)}) collective-permute-start(bf16[48,1024]{1,0:T(8,128)(2,1)S(1)} %get-tuple-element.166), channel_id=1, source_target_pairs={{0,2},{1,3},{2,0},{3,1},{4,6},{5,7},{6,4},{7,5},{8,10},{9,11},{10,... | collective-permute-start | bytes 294920 | tf_op jit(solution)/shard_map/ppermute | solution.py:228
  127.7 12.0 %collective-permute-start.40 = (bf16[48,1024]{1,0:T(8,128)(2,1)S(1)}, bf16[48,1024]{1,0:T(8,128)(2,1)S(1)}, u32[]{:S(2)}, u32[]{:S(2)}) collective-permute-start(bf16[48,1024]{1,0:T(8,128)(2,1)S(1)} %get-tuple-element.167), channel_id=1, source_target_pairs={{0,3},{1,2},{2,1},{3,0},{4,7},{5,6},{6,5},{7,4},{8,11},{9,10},{10,... | collective-permute-start | bytes 294920 | tf_op jit(solution)/shard_map/ppermute | solution.py:228

commit v3 on v2

--- a/solution.py
+++ b/solution.py
@@ -435,19 +435,12 @@
     to_y[1:] = own[...]
 
 
-def arrive_kernel(from_x, from_y, far, along_x, along_y):
-    far[0] = from_x[0]
-    far[1] = from_y[0]
-    along_x[...] = from_x[1:]
-    along_y[...] = from_y[1:]
-
-
 def join_kernel(from_x, from_y, far):
     far[0] = from_x[0]
     far[1] = from_y[0]
 
 
-def expert_kernel(n, *refs):
+def expert_kernel(n, n_split, *refs):
     blocks, (up, down), outs, (rows_in, hidden) = refs[: 2 * n], refs[2 * n : 2 * n + 2], refs[2 * n + 2 : -2], refs[-2:]
     _, slots, half = blocks[0].shape
     for k, block in enumerate(blocks):
@@ -460,55 +453,69 @@
     for j in range(0, down.shape[1], DOWN_TILE):
         value = fast_dot(hidden[...], down[:, j : j + DOWN_TILE]).astype(BF16)
         at = slice(j % half, j % half + DOWN_TILE)
-        for k, out in enumerate(outs):
+        for k in range(2 * n):
             start = (n + k) % (2 * n) * slots
-            out[j // half, :, at] = value[start : start + slots]
+            rows = value[start : start + slots]
+            if k < n_split:
+                outs[2 * k + j // half][:, at] = rows
+            else:
+                outs[n_split + k][j // half, :, at] = rows
 
 
 UP_TILE = 512
 DOWN_TILE = 512
 
 
-def expert_rows(blocks, twins, up, down):
+def expert_rows(blocks, twins, up, down, n_split=0):
     n = len(blocks)
     _, slots, half = blocks[0].shape
     features, hidden = up.shape
+    whole, part = shape_of((2, slots, half), BF16), shape_of((slots, half), BF16)
     outs = call(
-        lambda *refs: expert_kernel(n, *refs),
-        [shape_of((2, slots, half), BF16)] * (2 * n),
+        lambda *refs: expert_kernel(n, n_split, *refs),
+        [part] * (2 * n_split) + [whole] * (2 * n - n_split),
         scratch=[pltpu.VMEM((2 * n * slots, features), BF16), pltpu.VMEM((2 * n * slots, hidden), BF16)],
-        limit=8,
+        limit=9,
     )(*blocks, *twins, up, down)
-    return outs[:n], outs[n:]
+    return outs[: n + n_split], outs[n + n_split :]
 
 
 def both(a, b):
     return (a.astype(F32) + b.astype(F32)).astype(BF16)
 
 
-def sum_over_chip(places, others, own, to_x, to_y, rest_x, rest_y):
-    here, along_x, along_y, far = zip(places, others)
+def arrive_kernel(from_x, from_y, *refs):
+    places, others, (far, along_x, along_y, own, to_x, to_y, rest_x, rest_y) = refs[:3], refs[3:6], refs[6:]
+    far[0] = from_x[0]
+    far[1] = from_y[0]
+    along_x[...] = from_x[1:]
+    along_y[...] = from_y[1:]
+    to_x[0] = from_y[1]
+    to_y[0] = from_x[2]
+    direct_sums(places, others, own, to_x.at[1], to_y.at[1], rest_x, rest_y)
+
+
+def direct_sums(places, others, own, to_x, to_y, rest_x, rest_y):
+    here, along_x, along_y = zip(places, others)
     own[...] = both(here[0][...], here[1][...])
-    to_x[1] = both(far[0][0], far[1][0])
-    to_y[1] = both(far[0][1], far[1][1])
-    to_x[2] = both(along_x[0][0], along_x[1][0])
-    to_y[2] = both(along_y[0][1], along_y[1][1])
+    to_x[...] = both(along_x[0][0], along_x[1][0])
+    to_y[...] = both(along_y[0][1], along_y[1][1])
     rest_x[...] = both(along_x[0][1], along_x[1][1])
     rest_y[...] = both(along_y[0][0], along_y[1][0])
 
 
-def first_sum_kernel(from_x, from_y, *refs):
-    places, others, outs = refs[:4], refs[4:8], refs[8:]
-    outs[1][0] = from_y[1]
-    outs[2][0] = from_x[2]
-    sum_over_chip(places, others, *outs)
-
-
-def second_sum_kernel(from_x, from_y, rest_x, rest_y, *refs):
-    places, others, outs = refs[:4], refs[4:8], refs[8:]
-    outs[1][0] = both(rest_x[...], from_y[1])
-    outs[2][0] = both(rest_y[...], from_x[1])
-    sum_over_chip(places, others, *outs)
+def middle_kernel(far, far_other, *refs):
+    places, others, (own, to_x, to_y, rest_x, rest_y) = refs[:3], refs[3:6], refs[6:]
+    to_x[0] = both(far[0], far_other[0])
+    to_y[0] = both(far[1], far_other[1])
+    direct_sums(places, others, own, to_x.at[1], to_y.at[1], rest_x, rest_y)
+
+
+def late_kernel(from_x, from_y, rest_x, rest_y, far, first_half, second_half, to_x, to_y):
+    to_x[0] = both(rest_x[...], from_y[0])
+    to_y[0] = both(rest_y[...], from_x[0])
+    to_x[1] = both(far[0], first_half[...])
+    to_y[1] = both(far[1], second_half[...])
 
 
 def relay_kernel(from_x, from_y, rest_x, rest_y, next_x, next_y):
@@ -524,8 +531,8 @@
     def add(a, b, c):
         return (a.astype(F32) + b.astype(F32) + c.astype(F32)).astype(BF16)
 
-    total[0] = add(own[0], from_x[2], last_y[at_last])
-    total[1] = add(own[1], last_x[at_last], from_y[2])
+    total[0] = add(own[0], from_x[1], last_y[at_last])
+    total[1] = add(own[1], last_x[at_last], from_y[1])
     for mask, out in enumerate(outs):
         at = mine[0] ^ mask
         to = pl.multiple_of((at % per_half) * width, width)
@@ -671,34 +678,37 @@
         return [parts[0]] + [arrived[m] for m in range(1, experts)]
 
     onward = shape_of((3, slots, half), BF16)
-    sums = [row_block, onward, onward, half_block, half_block]
     share = rows // CHUNKS
     first1, *others1 = to_experts(0)
     own1 = normed([after(first1, down), *others1])
     x1, y1 = along(own1, own1)
     own2 = normed(to_experts(1))
     from_x, from_y = along(*call(onward_kernel, [onward, onward])(x1, y1, own2))
-    near1 = [own1, x1, y1]
-    odd1, even1 = expert_rows(near1, [twin(block) for block in near1], up, down)
-    far1, x2, y2 = call(arrive_kernel, [row_block] * 3)(after(from_x, even1[0]), from_y)
-    odd_far1, even_far1 = expert_rows([far1], [twin(far1)], up, down)
-    own_sum1, to_x, to_y, rest_x1, rest_y1 = call(first_sum_kernel, sums)(
-        from_x, from_y, *even1, *even_far1, *(twin(block) for block in (*odd1, *odd_far1))
+    double = shape_of((2, slots, half), BF16)
+    sums = [row_block, double, double, half_block, half_block]
+    now = [own1, x1, y1, own2]
+    (*odd1, odd_own2), (*even1, even_own2) = expert_rows(now, [twin(block) for block in now], up, down)
+    far1, x2, y2, own_sum1, to_x, to_y, rest_x1, rest_y1 = call(arrive_kernel, [row_block] * 3 + sums)(
+        after(from_x, even1[0]), from_y, *even1, *(twin(block) for block in odd1)
     )
     from_x3, from_y3 = along(to_x, to_y)
-    near2 = [own2, x2, y2]
-    odd2, even2 = expert_rows(
-        [after(own2, own_sum1), x2, y2], [twin(block) for block in near2], up, down
-    )
-    far2 = call(join_kernel, row_block)(after(from_x3, even2[0]), from_y3)
-    odd_far2, even_far2 = expert_rows([far2], [twin(far2)], up, down)
-    own_sum2, to_x, to_y, rest_x2, rest_y2 = call(second_sum_kernel, sums)(
-        from_x3, from_y3, rest_x1, rest_y1,
-        *even2, *even_far2, *(twin(block) for block in (*odd2, *odd_far2)),
+    now = [far1, x2, y2]
+    odd, even = expert_rows(now, [twin(block) for block in now], up, down)
+    far2 = call(join_kernel, row_block)(after(from_x3, even[0]), from_y3)
+    own_sum2, to_x, to_y, rest_x2, rest_y2 = call(middle_kernel, sums)(
+        after(even[0], far2), twin(odd[0]),
+        even_own2, *even[1:], twin(odd_own2), *(twin(block) for block in odd[1:]),
     )
     from_x4, from_y4 = along(to_x, to_y)
-    next_x, next_y = call(relay_kernel, [half_block, half_block])(from_x4, from_y4, rest_x2, rest_y2)
-    done1 = results(0, own_sum1, from_x3, from_y3, after(from_x4, next_x), from_y4)
+    odd_far2, (even_far2,) = expert_rows(
+        [after(far2, own_sum2)], [twin(far2)], up, down, n_split=1
+    )
+    to_x, to_y = call(late_kernel, [double, double])(
+        from_x4, from_y4, rest_x1, rest_y1, even_far2, *(twin(part) for part in odd_far2)
+    )
+    from_x5, from_y5 = along(to_x, to_y)
+    next_x, next_y = call(relay_kernel, [half_block, half_block])(from_x5, from_y5, rest_x2, rest_y2)
+    done1 = results(0, own_sum1, from_x3, from_y3, after(from_x5, next_x), from_y5)
     last_x, last_y = along(next_x, next_y)
     back1 = back(done1)
     grad_conv = call(grad_kernel, block, smem=1)(

time: 141 us -> 130 us (0.922)
  waiting for transfers between devices: 52.3 us -> 44.2 us
  Pallas kernels: 42.4 us -> 40.6 us
    ppermute x40 -> x43, waiting for transfers between devices: 47.9 us -> 40.5 us  [swap(): return lax.ppermute(x, axis, [(i, i ^ mask) for i in range(size)])]
    pallas_call x22 -> x21, Pallas kernels: 31 us -> 29.3 us  [run(): pl.pallas_call(body, out_shape=outs, in_specs=specs, out_specs=jax.tree.m...]
    ppermute x40 -> x43, starting transfers between devices: 38.3 us -> 37.2 us  [swap(): return lax.ppermute(x, axis, [(i, i ^ mask) for i in range(size)])]
  transfers between devices with their start and end apart: 44 -> 47, of which waited for: 24 -> 22; matrix products, arithmetic and copies ran while one was open for 0% -> 0% of each run, Pallas kernels for 27% -> 28%
where the time goes in v3:
time: 130 us
  waiting for transfers between devices  44.2 us (34%)
  starting transfers between devices  43.6 us (34%)
  Pallas kernels  40.6 us (31%)
    ppermute x43, waiting for transfers between devices, swap(): return lax.ppermute(x, axis, [(i, i ^ mask) for i in range(size)])  40.5 us
    ppermute x43, starting transfers between devices, swap(): return lax.ppermute(x, axis, [(i, i ^ mask) for i in range(size)])  37.2 us
    pallas_call x21, Pallas kernels, run(): pl.pallas_call(body, out_shape=outs, in_specs=specs, out_specs=jax.tree.m...  29.3 us
    pallas_call x2, Pallas kernels, load(): pl.pallas_call(load_kernel, out_shape=pltpu.VMEM(source.shape, source.dty...  9.17 us
    ppermute x3, starting transfers between devices, directed(): return lax.ppermute(x, 'ctx', route)  4.06 us
    ppermute x3, waiting for transfers between devices, directed(): return lax.ppermute(x, 'ctx', route)  3.65 us
  transfers between devices with their start and end apart: 47, of which 22 were waited for; matrix products, arithmetic and copies ran while one was open for 0% of the time, Pallas kernels for 28%

profile of v3, /device:TPU:0, one launch (start us, length us, event | category | flops | bytes accessed | tf_op | source)
XLA Modules:
  0.0 130.0 jit_solution(842389651078260282)
XLA Ops:
  1.4 2.3 %collective-permute-start = (bf16[8,1024]{1,0:T(8,128)(2,1)S(1)}, bf16[8,1024]{1,0:T(8,128)(2,1)S(1)}, u32[]{:S(2)}, u32[]{:S(2)}) collective-permute-start(bf16[8,1024]{1,0:T(8,128)(2,1)S(1)} %slice.3), channel_id=1, source_target_pairs={{0,4},{4,8},{8,12},{12,16},{16,20},{20,24},{24,28},{1,5},{5,9},{9,... | collective-permute-start | bytes 49160 | tf_op jit(solution)/shard_map/ppermute | solution.py:19
  3.7 2.2 %shard_map.131 = (f32[16,128]{1,0:T(8,128)S(1)}, bf16[128,128]{1,0:T(8,128)(2,1)S(1)}, bf16[128,1024]{1,0:T(8,128)(2,1)S(1)}, bf16[128,128]{1,0:T(8,128)(2,1)S(1...) custom-call(f32[16,128]{1,0:T(8,128)} %refs_0_, ...), custom_call_target="tpu_custom_call" | custom-call | flops 1 | bytes 1 | tf_op jit(solution)/shard_map/pallas_call | solution.py:625
  6.6 2.7 %collective-permute-start.1 = (bf16[136,1024]{1,0:T(8,128)(2,1)S(1)}, bf16[136,1024]{1,0:T(8,128)(2,1)S(1)}, u32[]{:S(2)}, u32[]{:S(2)}) collective-permute-start(bf16[136,1024]{1,0:T(8,128)(2,1)S(1)} %get-tuple-element.105), channel_id=1, source_target_pairs={{0,4},{4,0},{8,12},{12,8},{16,20},{20,16},{24,28},{28,24},{1,5},{5... | collective-permute-start | bytes 835592 | tf_op jit(solution)/shard_map/ppermute | solution.py:228
  9.3 1.1 shard_map.133
  10.5 1.3 collective-permute-start.4
  11.8 1.3 collective-permute-start.3
  13.1 1.5 %collective-permute-start.2 = (bf16[136,1024]{1,0:T(8,128)(2,1)S(1)}, bf16[136,1024]{1,0:T(8,128)(2,1)S(1)}, u32[]{:S(2)}, u32[]{:S(2)}) collective-permute-start(bf16[136,1024]{1,0:T(8,128)(2,1)S(1)} %shard_map.134), channel_id=1, source_target_pairs={{4,12},{8,0},{20,28},{24,16},{5,13},{9,1},{21,29},{25,17},{6,14},{... | collective-permute-start | bytes 835592 | tf_op jit(solution)/shard_map/ppermute | solution.py:577
  14.6 4.6 %shard_map.135.refs_8_.refs_6_.refs_2_ = bf16[4096,1536]{1,0:T(8,128)(2,1)S(1)} custom-call(bf16[4096,1536]{1,0:T(8,128)(2,1)} %bitcast.9), custom_call_target="tpu_custom_call" | custom-call | flops 1 | bytes 1 | tf_op jit(solution)/shard_map/pallas_call | solution.py:298
  20.0 2.9 %collective-permute-done.3.middle = bf16[136,1024]{1,0:T(8,128)(2,1)S(1)} collective-permute-done((bf16[136,1024]{1,0:T(8,128)(2,1)S(1)}, bf16[136,1024]{1,0:T(8,128)(2,1)S(1)}, u32[]{:S(2)}, u32[]{:S(2)}) %collective-permute-start.3) | collective-permute-done | bytes 278560 | tf_op jit(solution)/shard_map/ppermute | solution.py:577
  23.0 0.9 collective-permute-start.5
  23.9 1.2 collective-permute-done.5.shared
  25.8 1.7 %collective-permute-start.6 = (bf16[48,1024]{1,0:T(8,128)(2,1)S(1)}, bf16[48,1024]{1,0:T(8,128)(2,1)S(1)}, u32[]{:S(2)}, u32[]{:S(2)}) collective-permute-start(bf16[48,1024]{1,0:T(8,128)(2,1)S(1)} %get-tuple-element.120), channel_id=1, source_target_pairs={{0,1},{1,0},{2,3},{3,2},{4,5},{5,4},{6,7},{7,6},{8,9},{9,8},{10,11... | collective-permute-start | bytes 294920 | tf_op jit(solution)/shard_map/ppermute | solution.py:228
  27.4 2.6 %collective-permute-start.7 = (bf16[48,1024]{1,0:T(8,128)(2,1)S(1)}, bf16[48,1024]{1,0:T(8,128)(2,1)S(1)}, u32[]{:S(2)}, u32[]{:S(2)}) collective-permute-start(bf16[48,1024]{1,0:T(8,128)(2,1)S(1)} %get-tuple-element.121), channel_id=1, source_target_pairs={{0,2},{1,3},{2,0},{3,1},{4,6},{5,7},{6,4},{7,5},{8,10},{9,11},{10,... | collective-permute-start | bytes 294920 | tf_op jit(solution)/shard_map/ppermute | solution.py:228
  30.3 4.6 %shard_map.138.refs_9_.refs_7_.refs_3_ = bf16[1536,4096]{1,0:T(8,128)(2,1)S(1)} custom-call(bf16[1536,4096]{1,0:T(8,128)(2,1)} %bitcast.10), custom_call_target="tpu_custom_call" | custom-call | flops 1 | bytes 1 | tf_op jit(solution)/shard_map/pallas_call | solution.py:298
  34.9 3.3 %collective-permute-done.7.refs_2_ = bf16[48,1024]{1,0:T(8,128)(2,1)S(1)} collective-permute-done((bf16[48,1024]{1,0:T(8,128)(2,1)S(1)}, bf16[48,1024]{1,0:T(8,128)(2,1)S(1)}, u32[]{:S(2)}, u32[]{:S(2)}) %collective-permute-start.7) | collective-permute-done | bytes 98336 | tf_op jit(solution)/shard_map/ppermute | solution.py:228
  38.4 1.9 %collective-permute-start.10 = (bf16[2,48,2048]{2,1,0:T(8,128)(2,1)S(1)}, bf16[2,48,2048]{2,1,0:T(8,128)(2,1)S(1)}, u32[]{:S(2)}, u32[]{:S(2)}) collective-permute-start(bf16[2,48,2048]{2,1,0:T(8,128)(2,1)S(1)} %shard_map.139.refs_0_), channel_id=1, source_target_pairs={{0,16},{4,20},{8,24},{12,28},{16,0},{20,4},{24,8},{28,12},{1,17},{... | collective-permute-start | bytes 1179656 | tf_op jit(solution)/shard_map/ppermute | solution.py:228
  40.6 1.7 %collective-permute-start.11 = (bf16[48,1024]{1,0:T(8,128)(2,1)S(1)}, bf16[48,1024]{1,0:T(8,128)(2,1)S(1)}, u32[]{:S(2)}, u32[]{:S(2)}) collective-permute-start(bf16[48,1024]{1,0:T(8,128)(2,1)S(1)} %get-tuple-element.124), channel_id=1, source_target_pairs={{0,1},{1,0},{2,3},{3,2},{4,5},{5,4},{6,7},{7,6},{8,9},{9,8},{10,11... | collective-permute-start | bytes 294920 | tf_op jit(solution)/shard_map/ppermute | solution.py:228
  42.3 1.4 %collective-permute-start.12 = (bf16[48,1024]{1,0:T(8,128)(2,1)S(1)}, bf16[48,1024]{1,0:T(8,128)(2,1)S(1)}, u32[]{:S(2)}, u32[]{:S(2)}) collective-permute-start(bf16[48,1024]{1,0:T(8,128)(2,1)S(1)} %get-tuple-element.125), channel_id=1, source_target_pairs={{0,2},{1,3},{2,0},{3,1},{4,6},{5,7},{6,4},{7,5},{8,10},{9,11},{10,... | collective-permute-start | bytes 294920 | tf_op jit(solution)/shard_map/ppermute | solution.py:228
  43.7 1.3 collective-permute-start.13
  45.7 5.5 %collective-permute-done.12.refs_2_ = bf16[48,1024]{1,0:T(8,128)(2,1)S(1)} collective-permute-done((bf16[48,1024]{1,0:T(8,128)(2,1)S(1)}, bf16[48,1024]{1,0:T(8,128)(2,1)S(1)}, u32[]{:S(2)}, u32[]{:S(2)}) %collective-permute-start.12) | collective-permute-done | bytes 98336 | tf_op jit(solution)/shard_map/ppermute | solution.py:228
  52.6 1.8 %collective-permute-start.14 = (bf16[3,48,2048]{2,1,0:T(8,128)(2,1)S(1)}, bf16[3,48,2048]{2,1,0:T(8,128)(2,1)S(1)}, u32[]{:S(2)}, u32[]{:S(2)}) collective-permute-start(bf16[3,48,2048]{2,1,0:T(8,128)(2,1)S(1)} %get-tuple-element.127), channel_id=1, source_target_pairs={{0,8},{4,12},{8,0},{12,4},{16,24},{20,28},{24,16},{28,20},{1,9},{5... | collective-permute-start | bytes 1769480 | tf_op jit(solution)/shard_map/ppermute | solution.py:228
  54.4 0.8 collective-permute-start.19
  55.2 9.9 %shard_map.142 = (bf16[2,48,2048]{2,1,0:T(8,128)(2,1)S(1)}, bf16[2,48,2048]{2,1,0:T(8,128)(2,1)S(1)}, bf16[2,48,2048]{2,1,0:T(8,128)(2,1)S(1)}, bf16[2,48,2048]{...) custom-call(bf16[2,48,2048]{2,1,0:T(8,128)(2,1)S(1)} %shard_map.139., ...), custom_call_target="tpu_custom_call" | custom-call | flops 1 | bytes 1 | tf_op jit(solution)/shard_map/pallas_call | solution.py:213
  65.7 2.3 %collective-permute-done.14.from_x = bf16[3,48,2048]{2,1,0:T(8,128)(2,1)S(1)} collective-permute-done((bf16[3,48,2048]{2,1,0:T(8,128)(2,1)S(1)}, bf16[3,48,2048]{2,1,0:T(8,128)(2,1)S(1)}, u32[]{:S(2)}, u32[]{:S(2)}) %collective-permute-start.14) | collective-permute-done | bytes 589856 | tf_op jit(solution)/shard_map/ppermute | solution.py:228
  68.0 1.4 %collective-permute-done.19.from_y = bf16[3,48,2048]{2,1,0:T(8,128)(2,1)S(1)} collective-permute-done((bf16[3,48,2048]{2,1,0:T(8,128)(2,1)S(1)}, bf16[3,48,2048]{2,1,0:T(8,128)(2,1)S(1)}, u32[]{:S(2)}, u32[]{:S(2)}) %collective-permute-start.19) | collective-permute-done | bytes 589856 | tf_op jit(solution)/shard_map/ppermute | solution.py:228
  70.5 0.9 collective-permute-start.26
  72.7 7.7 %shard_map.144 = (bf16[2,48,2048]{2,1,0:T(8,128)(2,1)S(1)}, bf16[2,48,2048]{2,1,0:T(8,128)(2,1)S(1)}, bf16[2,48,2048]{2,1,0:T(8,128)(2,1)S(1)}, bf16[2,48,2048]{...) custom-call(bf16[2,48,2048]{2,1,0:T(8,128)(2,1)S(1)} %get-tuple-element.136.refs_0_, ...), custom_call_target="tpu_custom_call" | custom-call | flops 1 | bytes 1 | tf_op jit(solution)/shard_map/pallas_call | solution.py:213
  81.0 0.9 collective-permute-done.26.from_x.refs_2_
  82.8 0.9 collective-permute-done.31.refs_5_
  84.0 0.9 collective-permute-start.32
  85.8 4.1 %shard_map.147 = (bf16[48,2048]{1,0:T(8,128)(2,1)S(1)}, bf16[48,2048]{1,0:T(8,128)(2,1)S(1)}, bf16[2,48,2048]{2,1,0:T(8,128)(2,1)S(1)}) custom-call(bf16[2,48,2048]{2,1,0:T(8,128)(2,1)S(1)} %shard_map.145.refs_0_, bf16[2,48,2048]{2,1,0:T(8,128)(2,1)S(1)} %collective-permute-done.34.refs_1_, bf16[4096,1536]{1,0:T(8,128)(2,1)S(1)} %shard_map.135.refs_8_.refs_6_.refs_2_, ...), custom_call_target="tpu_custom_call" | custom-call | flops 1 | bytes 1 | tf_op jit(solution)/shard_map/pallas_call | solution.py:213
  90.5 0.9 collective-permute-done.35.first_half
  91.7 3.5 %collective-permute-done.32.from_x.refs_2_ = bf16[2,48,2048]{2,1,0:T(8,128)(2,1)S(1)} collective-permute-done((bf16[2,48,2048]{2,1,0:T(8,128)(2,1)S(1)}, bf16[2,48,2048]{2,1,0:T(8,128)(2,1)S(1)}, u32[]{:S(2)}, u32[]{:S(2)}) %collective-permute-start.32) | collective-permute-done | bytes 393248 | tf_op jit(solution)/shard_map/ppermute | solution.py:228
  96.0 1.2 collective-permute-start.37
  98.0 8.1 %collective-permute-done.37.from_x.refs_4_ = bf16[2,48,2048]{2,1,0:T(8,128)(2,1)S(1)} collective-permute-done((bf16[2,48,2048]{2,1,0:T(8,128)(2,1)S(1)}, bf16[2,48,2048]{2,1,0:T(8,128)(2,1)S(1)}, u32[]{:S(2)}, u32[]{:S(2)}) %collective-permute-start.37) | collective-permute-done | bytes 393248 | tf_op jit(solution)/shard_map/ppermute | solution.py:228
  106.1 0.9 collective-permute-done.38.from_y.refs_5_
  107.0 0.9 collective-permute-start.40
  107.9 1.2 collective-permute-start.39
  109.4 2.0 %collective-permute-start.44 = (bf16[48,1024]{1,0:T(8,128)(2,1)S(1)}, bf16[48,1024]{1,0:T(8,128)(2,1)S(1)}, u32[]{:S(2)}, u32[]{:S(2)}) collective-permute-start(bf16[48,1024]{1,0:T(8,128)(2,1)S(1)} %get-tuple-element.177), channel_id=1, source_target_pairs={{0,1},{1,0},{2,3},{3,2},{4,5},{5,4},{6,7},{7,6},{8,9},{9,8},{10,11... | collective-permute-start | bytes 294920 | tf_op jit(solution)/shard_map/ppermute | solution.py:228
  111.4 1.1 shard_map.151
  112.5 1.0 collective-permute-start.45
  113.5 1.4 %collective-permute-start.46 = (bf16[48,1024]{1,0:T(8,128)(2,1)S(1)}, bf16[48,1024]{1,0:T(8,128)(2,1)S(1)}, u32[]{:S(2)}, u32[]{:S(2)}) collective-permute-start(bf16[48,1024]{1,0:T(8,128)(2,1)S(1)} %get-tuple-element.179), channel_id=1, source_target_pairs={{0,3},{1,2},{2,1},{3,0},{4,7},{5,6},{6,5},{7,4},{8,11},{9,10},{10,... | collective-permute-start | bytes 294920 | tf_op jit(solution)/shard_map/ppermute | solution.py:228
  115.2 1.1 collective-permute-start.41
  116.4 1.9 %collective-permute-start.42 = (bf16[48,1024]{1,0:T(8,128)(2,1)S(1)}, bf16[48,1024]{1,0:T(8,128)(2,1)S(1)}, u32[]{:S(2)}, u32[]{:S(2)}) collective-permute-start(bf16[48,1024]{1,0:T(8,128)(2,1)S(1)} %get-tuple-element.174), channel_id=1, source_target_pairs={{0,2},{1,3},{2,0},{3,1},{4,6},{5,7},{6,4},{7,5},{8,10},{9,11},{10,... | collective-permute-start | bytes 294920 | tf_op jit(solution)/shard_map/ppermute | solution.py:228
  118.2 1.4 %collective-permute-start.43 = (bf16[48,1024]{1,0:T(8,128)(2,1)S(1)}, bf16[48,1024]{1,0:T(8,128)(2,1)S(1)}, u32[]{:S(2)}, u32[]{:S(2)}) collective-permute-start(bf16[48,1024]{1,0:T(8,128)(2,1)S(1)} %get-tuple-element.175), channel_id=1, source_target_pairs={{0,3},{1,2},{2,1},{3,0},{4,7},{5,6},{6,5},{7,4},{8,11},{9,10},{10,... | collective-permute-start | bytes 294920 | tf_op jit(solution)/shard_map/ppermute | solution.py:228
  119.7 5.8 %collective-permute-done.45.refs_5_ = bf16[48,1024]{1,0:T(8,128)(2,1)S(1)} collective-permute-done((bf16[48,1024]{1,0:T(8,128)(2,1)S(1)}, bf16[48,1024]{1,0:T(8,128)(2,1)S(1)}, u32[]{:S(2)}, u32[]{:S(2)}) %collective-permute-start.45) | collective-permute-done | bytes 98336 | tf_op jit(solution)/shard_map/ppermute | solution.py:228
  126.0 2.8 %collective-permute-done.42.refs_5_ = bf16[48,1024]{1,0:T(8,128)(2,1)S(1)} collective-permute-done((bf16[48,1024]{1,0:T(8,128)(2,1)S(1)}, bf16[48,1024]{1,0:T(8,128)(2,1)S(1)}, u32[]{:S(2)}, u32[]{:S(2)}) %collective-permute-start.42) | collective-permute-done | bytes 98336 | tf_op jit(solution)/shard_map/ppermute | solution.py:228
  128.8 1.2 shard_map.154
  (71 shorter events, 15.3 us)
Async XLA Ops:
  1.4 4.5 %collective-permute-start = (bf16[8,1024]{1,0:T(8,128)(2,1)S(1)}, bf16[8,1024]{1,0:T(8,128)(2,1)S(1)}, u32[]{:S(2)}, u32[]{:S(2)}) collective-permute-start(bf16[8,1024]{1,0:T(8,128)(2,1)S(1)} %slice.3), channel_id=1, source_target_pairs={{0,4},{4,8},{8,12},{12,16},{16,20},{20,24},{24,28},{1,5},{5,9},{9,... | collective-permute-start | bytes 49160 | tf_op jit(solution)/shard_map/ppermute | solution.py:19
  6.6 3.9 %collective-permute-start.1 = (bf16[136,1024]{1,0:T(8,128)(2,1)S(1)}, bf16[136,1024]{1,0:T(8,128)(2,1)S(1)}, u32[]{:S(2)}, u32[]{:S(2)}) collective-permute-start(bf16[136,1024]{1,0:T(8,128)(2,1)S(1)} %get-tuple-element.105), channel_id=1, source_target_pairs={{0,4},{4,0},{8,12},{12,8},{16,20},{20,16},{24,28},{28,24},{1,5},{5... | collective-permute-start | bytes 835592 | tf_op jit(solution)/shard_map/ppermute | solution.py:228
  10.5 9.4 %collective-permute-start.4 = (bf16[136,1024]{1,0:T(8,128)(2,1)S(1)}, bf16[136,1024]{1,0:T(8,128)(2,1)S(1)}, u32[]{:S(2)}, u32[]{:S(2)}) collective-permute-start(bf16[136,1024]{1,0:T(8,128)(2,1)S(1)} %shard_map.134), channel_id=1, source_target_pairs={{4,28},{12,20},{16,8},{24,0},{5,29},{13,21},{17,9},{25,1},{6,30},{... | collective-permute-start | bytes 835592 | tf_op jit(solution)/shard_map/ppermute | solution.py:577
  11.8 11.0 %collective-permute-start.3 = (bf16[136,1024]{1,0:T(8,128)(2,1)S(1)}, bf16[136,1024]{1,0:T(8,128)(2,1)S(1)}, u32[]{:S(2)}, u32[]{:S(2)}) collective-permute-start(bf16[136,1024]{1,0:T(8,128)(2,1)S(1)} %shard_map.134), channel_id=1, source_target_pairs={{4,20},{12,28},{16,0},{24,8},{5,21},{13,29},{17,1},{25,9},{6,22},{... | collective-permute-start | bytes 835592 | tf_op jit(solution)/shard_map/ppermute | solution.py:577
  13.1 9.7 %collective-permute-start.2 = (bf16[136,1024]{1,0:T(8,128)(2,1)S(1)}, bf16[136,1024]{1,0:T(8,128)(2,1)S(1)}, u32[]{:S(2)}, u32[]{:S(2)}) collective-permute-start(bf16[136,1024]{1,0:T(8,128)(2,1)S(1)} %shard_map.134), channel_id=1, source_target_pairs={{4,12},{8,0},{20,28},{24,16},{5,13},{9,1},{21,29},{25,17},{6,14},{... | collective-permute-start | bytes 835592 | tf_op jit(solution)/shard_map/ppermute | solution.py:577
  23.0 2.1 %collective-permute-start.5 = (bf16[128,1024]{1,0:T(8,128)(2,1)S(1)}, bf16[128,1024]{1,0:T(8,128)(2,1)S(1)}, u32[]{:S(2)}, u32[]{:S(2)}) collective-permute-start(bf16[128,1024]{1,0:T(8,128)(2,1)S(1)} %shard_map.136.prefix), channel_id=1, source_target_pairs={{0,4},{4,0},{8,12},{12,8},{16,20},{20,16},{24,28},{28,24},{1,5},{5... | collective-permute-start | bytes 786440 | tf_op jit(solution)/shard_map/ppermute | solution.py:228
  25.8 9.1 %collective-permute-start.6 = (bf16[48,1024]{1,0:T(8,128)(2,1)S(1)}, bf16[48,1024]{1,0:T(8,128)(2,1)S(1)}, u32[]{:S(2)}, u32[]{:S(2)}) collective-permute-start(bf16[48,1024]{1,0:T(8,128)(2,1)S(1)} %get-tuple-element.120), channel_id=1, source_target_pairs={{0,1},{1,0},{2,3},{3,2},{4,5},{5,4},{6,7},{7,6},{8,9},{9,8},{10,11... | collective-permute-start | bytes 294920 | tf_op jit(solution)/shard_map/ppermute | solution.py:228
  27.4 10.7 %collective-permute-start.7 = (bf16[48,1024]{1,0:T(8,128)(2,1)S(1)}, bf16[48,1024]{1,0:T(8,128)(2,1)S(1)}, u32[]{:S(2)}, u32[]{:S(2)}) collective-permute-start(bf16[48,1024]{1,0:T(8,128)(2,1)S(1)} %get-tuple-element.121), channel_id=1, source_target_pairs={{0,2},{1,3},{2,0},{3,1},{4,6},{5,7},{6,4},{7,5},{8,10},{9,11},{10,... | collective-permute-start | bytes 294920 | tf_op jit(solution)/shard_map/ppermute | solution.py:228
  30.0 8.1 %collective-permute-start.8 = (bf16[48,1024]{1,0:T(8,128)(2,1)S(1)}, bf16[48,1024]{1,0:T(8,128)(2,1)S(1)}, u32[]{:S(2)}, u32[]{:S(2)}) collective-permute-start(bf16[48,1024]{1,0:T(8,128)(2,1)S(1)} %get-tuple-element.122), channel_id=1, source_target_pairs={{0,3},{1,2},{2,1},{3,0},{4,7},{5,6},{6,5},{7,4},{8,11},{9,10},{10,... | collective-permute-start | bytes 294920 | tf_op jit(solution)/shard_map/ppermute | solution.py:228
  38.4 13.6 %collective-permute-start.10 = (bf16[2,48,2048]{2,1,0:T(8,128)(2,1)S(1)}, bf16[2,48,2048]{2,1,0:T(8,128)(2,1)S(1)}, u32[]{:S(2)}, u32[]{:S(2)}) collective-permute-start(bf16[2,48,2048]{2,1,0:T(8,128)(2,1)S(1)} %shard_map.139.refs_0_), channel_id=1, source_target_pairs={{0,16},{4,20},{8,24},{12,28},{16,0},{20,4},{24,8},{28,12},{1,17},{... | collective-permute-start | bytes 1179656 | tf_op jit(solution)/shard_map/ppermute | solution.py:228
  40.3 11.8 %collective-permute-start.9 = (bf16[2,48,2048]{2,1,0:T(8,128)(2,1)S(1)}, bf16[2,48,2048]{2,1,0:T(8,128)(2,1)S(1)}, u32[]{:S(2)}, u32[]{:S(2)}) collective-permute-start(bf16[2,48,2048]{2,1,0:T(8,128)(2,1)S(1)} %shard_map.139.refs_0_), channel_id=1, source_target_pairs={{0,8},{4,12},{8,0},{12,4},{16,24},{20,28},{24,16},{28,20},{1,9},{5... | collective-permute-start | bytes 1179656 | tf_op jit(solution)/shard_map/ppermute | solution.py:228
  40.6 5.1 %collective-permute-start.11 = (bf16[48,1024]{1,0:T(8,128)(2,1)S(1)}, bf16[48,1024]{1,0:T(8,128)(2,1)S(1)}, u32[]{:S(2)}, u32[]{:S(2)}) collective-permute-start(bf16[48,1024]{1,0:T(8,128)(2,1)S(1)} %get-tuple-element.124), channel_id=1, source_target_pairs={{0,1},{1,0},{2,3},{3,2},{4,5},{5,4},{6,7},{7,6},{8,9},{9,8},{10,11... | collective-permute-start | bytes 294920 | tf_op jit(solution)/shard_map/ppermute | solution.py:228
  42.3 8.9 %collective-permute-start.12 = (bf16[48,1024]{1,0:T(8,128)(2,1)S(1)}, bf16[48,1024]{1,0:T(8,128)(2,1)S(1)}, u32[]{:S(2)}, u32[]{:S(2)}) collective-permute-start(bf16[48,1024]{1,0:T(8,128)(2,1)S(1)} %get-tuple-element.125), channel_id=1, source_target_pairs={{0,2},{1,3},{2,0},{3,1},{4,6},{5,7},{6,4},{7,5},{8,10},{9,11},{10,... | collective-permute-start | bytes 294920 | tf_op jit(solution)/shard_map/ppermute | solution.py:228
  43.7 7.5 %collective-permute-start.13 = (bf16[48,1024]{1,0:T(8,128)(2,1)S(1)}, bf16[48,1024]{1,0:T(8,128)(2,1)S(1)}, u32[]{:S(2)}, u32[]{:S(2)}) collective-permute-start(bf16[48,1024]{1,0:T(8,128)(2,1)S(1)} %get-tuple-element.126), channel_id=1, source_target_pairs={{0,3},{1,2},{2,1},{3,0},{4,7},{5,6},{6,5},{7,4},{8,11},{9,10},{10,... | collective-permute-start | bytes 294920 | tf_op jit(solution)/shard_map/ppermute | solution.py:228
  51.5 2.9 %collective-permute-start.18 = (bf16[2,48,2048]{2,1,0:T(8,128)(2,1)S(1)}, bf16[2,48,2048]{2,1,0:T(8,128)(2,1)S(1)}, u32[]{:S(2)}, u32[]{:S(2)}) collective-permute-start(bf16[2,48,2048]{2,1,0:T(8,128)(2,1)S(1)} %shard_map.140.own.refs_3_), channel_id=1, source_target_pairs={{0,4},{4,0},{8,12},{12,8},{16,20},{20,16},{24,28},{28,24},{1,5},{5... | collective-permute-start | bytes 1179656 | tf_op jit(solution)/shard_map/ppermute | solution.py:228
  51.5 3.6 %collective-permute-start.15 = (bf16[2,48,2048]{2,1,0:T(8,128)(2,1)S(1)}, bf16[2,48,2048]{2,1,0:T(8,128)(2,1)S(1)}, u32[]{:S(2)}, u32[]{:S(2)}) collective-permute-start(bf16[2,48,2048]{2,1,0:T(8,128)(2,1)S(1)} %shard_map.139.refs_0_), channel_id=1, source_target_pairs={{0,4},{4,0},{8,12},{12,8},{16,20},{20,16},{24,28},{28,24},{1,5},{5... | collective-permute-start | bytes 1179656 | tf_op jit(solution)/shard_map/ppermute | solution.py:228
  52.0 3.2 %collective-permute-start.17 = (bf16[2,48,2048]{2,1,0:T(8,128)(2,1)S(1)}, bf16[2,48,2048]{2,1,0:T(8,128)(2,1)S(1)}, u32[]{:S(2)}, u32[]{:S(2)}) collective-permute-start(bf16[2,48,2048]{2,1,0:T(8,128)(2,1)S(1)} %collective-permute-done.10.along_y.refs_2_), channel_id=1, source_target_pairs={{0,4},{4,0},{8,12},{12,8},{16,20},{20,16},{24,28},{28,24},{1,5},{5... | collective-permute-start | bytes 1179656 | tf_op jit(solution)/shard_map/ppermute | solution.py:228
  52.1 3.1 %collective-permute-start.16 = (bf16[2,48,2048]{2,1,0:T(8,128)(2,1)S(1)}, bf16[2,48,2048]{2,1,0:T(8,128)(2,1)S(1)}, u32[]{:S(2)}, u32[]{:S(2)}) collective-permute-start(bf16[2,48,2048]{2,1,0:T(8,128)(2,1)S(1)} %collective-permute-done.9.along_x.refs_1_), channel_id=1, source_target_pairs={{0,4},{4,0},{8,12},{12,8},{16,20},{20,16},{24,28},{28,24},{1,5},{5... | collective-permute-start | bytes 1179656 | tf_op jit(solution)/shard_map/ppermute | solution.py:228
  52.6 15.4 %collective-permute-start.14 = (bf16[3,48,2048]{2,1,0:T(8,128)(2,1)S(1)}, bf16[3,48,2048]{2,1,0:T(8,128)(2,1)S(1)}, u32[]{:S(2)}, u32[]{:S(2)}) collective-permute-start(bf16[3,48,2048]{2,1,0:T(8,128)(2,1)S(1)} %get-tuple-element.127), channel_id=1, source_target_pairs={{0,8},{4,12},{8,0},{12,4},{16,24},{20,28},{24,16},{28,20},{1,9},{5... | collective-permute-start | bytes 1769480 | tf_op jit(solution)/shard_map/ppermute | solution.py:228
  54.4 15.0 %collective-permute-start.19 = (bf16[3,48,2048]{2,1,0:T(8,128)(2,1)S(1)}, bf16[3,48,2048]{2,1,0:T(8,128)(2,1)S(1)}, u32[]{:S(2)}, u32[]{:S(2)}) collective-permute-start(bf16[3,48,2048]{2,1,0:T(8,128)(2,1)S(1)} %get-tuple-element.130), channel_id=1, source_target_pairs={{0,16},{4,20},{8,24},{12,28},{16,0},{20,4},{24,8},{28,12},{1,17},{... | collective-permute-start | bytes 1769480 | tf_op jit(solution)/shard_map/ppermute | solution.py:228
  65.1 4.3 %collective-permute-start.20 = (bf16[2,48,2048]{2,1,0:T(8,128)(2,1)S(1)}, bf16[2,48,2048]{2,1,0:T(8,128)(2,1)S(1)}, u32[]{:S(2)}, u32[]{:S(2)}) collective-permute-start(bf16[2,48,2048]{2,1,0:T(8,128)(2,1)S(1)} %get-tuple-element.133), channel_id=1, source_target_pairs={{0,4},{4,0},{8,12},{12,8},{16,20},{20,16},{24,28},{28,24},{1,5},{5... | collective-permute-start | bytes 1179656 | tf_op jit(solution)/shard_map/ppermute | solution.py:228
  65.2 4.2 %collective-permute-start.21 = (bf16[2,48,2048]{2,1,0:T(8,128)(2,1)S(1)}, bf16[2,48,2048]{2,1,0:T(8,128)(2,1)S(1)}, u32[]{:S(2)}, u32[]{:S(2)}) collective-permute-start(bf16[2,48,2048]{2,1,0:T(8,128)(2,1)S(1)} %get-tuple-element.134), channel_id=1, source_target_pairs={{0,4},{4,0},{8,12},{12,8},{16,20},{20,16},{24,28},{28,24},{1,5},{5... | collective-permute-start | bytes 1179656 | tf_op jit(solution)/shard_map/ppermute | solution.py:228
  65.7 3.8 %collective-permute-start.22 = (bf16[2,48,2048]{2,1,0:T(8,128)(2,1)S(1)}, bf16[2,48,2048]{2,1,0:T(8,128)(2,1)S(1)}, u32[]{:S(2)}, u32[]{:S(2)}) collective-permute-start(bf16[2,48,2048]{2,1,0:T(8,128)(2,1)S(1)} %get-tuple-element.135), channel_id=1, source_target_pairs={{0,4},{4,0},{8,12},{12,8},{16,20},{20,16},{24,28},{28,24},{1,5},{5... | collective-permute-start | bytes 1179656 | tf_op jit(solution)/shard_map/ppermute | solution.py:228
  69.8 2.3 %collective-permute-start.23 = (bf16[2,48,2048]{2,1,0:T(8,128)(2,1)S(1)}, bf16[2,48,2048]{2,1,0:T(8,128)(2,1)S(1)}, u32[]{:S(2)}, u32[]{:S(2)}) collective-permute-start(bf16[2,48,2048]{2,1,0:T(8,128)(2,1)S(1)} %get-tuple-element.136.refs_0_), channel_id=1, source_target_pairs={{0,4},{4,0},{8,12},{12,8},{16,20},{20,16},{24,28},{28,24},{1,5},{5... | collective-permute-start | bytes 1179656 | tf_op jit(solution)/shard_map/ppermute | solution.py:228
  69.9 2.3 %collective-permute-start.24 = (bf16[2,48,2048]{2,1,0:T(8,128)(2,1)S(1)}, bf16[2,48,2048]{2,1,0:T(8,128)(2,1)S(1)}, u32[]{:S(2)}, u32[]{:S(2)}) collective-permute-start(bf16[2,48,2048]{2,1,0:T(8,128)(2,1)S(1)} %get-tuple-element.137.refs_1_), channel_id=1, source_target_pairs={{0,4},{4,0},{8,12},{12,8},{16,20},{20,16},{24,28},{28,24},{1,5},{5... | collective-permute-start | bytes 1179656 | tf_op jit(solution)/shard_map/ppermute | solution.py:228
  70.4 2.3 %collective-permute-start.25 = (bf16[2,48,2048]{2,1,0:T(8,128)(2,1)S(1)}, bf16[2,48,2048]{2,1,0:T(8,128)(2,1)S(1)}, u32[]{:S(2)}, u32[]{:S(2)}) collective-permute-start(bf16[2,48,2048]{2,1,0:T(8,128)(2,1)S(1)} %get-tuple-element.138.refs_2_), channel_id=1, source_target_pairs={{0,4},{4,0},{8,12},{12,8},{16,20},{20,16},{24,28},{28,24},{1,5},{5... | collective-permute-start | bytes 1179656 | tf_op jit(solution)/shard_map/ppermute | solution.py:228
  70.5 11.5 %collective-permute-start.26 = (bf16[2,48,2048]{2,1,0:T(8,128)(2,1)S(1)}, bf16[2,48,2048]{2,1,0:T(8,128)(2,1)S(1)}, u32[]{:S(2)}, u32[]{:S(2)}) collective-permute-start(bf16[2,48,2048]{2,1,0:T(8,128)(2,1)S(1)} %get-tuple-element.140), channel_id=1, source_target_pairs={{0,8},{4,12},{8,0},{12,4},{16,24},{20,28},{24,16},{28,20},{1,9},{5... | collective-permute-start | bytes 1179656 | tf_op jit(solution)/shard_map/ppermute | solution.py:228
  71.3 11.2 %collective-permute-start.27 = (bf16[2,48,2048]{2,1,0:T(8,128)(2,1)S(1)}, bf16[2,48,2048]{2,1,0:T(8,128)(2,1)S(1)}, u32[]{:S(2)}, u32[]{:S(2)}) collective-permute-start(bf16[2,48,2048]{2,1,0:T(8,128)(2,1)S(1)} %get-tuple-element.142), channel_id=1, source_target_pairs={{0,16},{4,20},{8,24},{12,28},{16,0},{20,4},{24,8},{28,12},{1,17},{... | collective-permute-start | bytes 1179656 | tf_op jit(solution)/shard_map/ppermute | solution.py:228
  72.1 10.5 %collective-permute-start.29 = (bf16[2,48,2048]{2,1,0:T(8,128)(2,1)S(1)}, bf16[2,48,2048]{2,1,0:T(8,128)(2,1)S(1)}, u32[]{:S(2)}, u32[]{:S(2)}) collective-permute-start(bf16[2,48,2048]{2,1,0:T(8,128)(2,1)S(1)} %get-tuple-element.148), channel_id=1, source_target_pairs={{0,4},{4,0},{8,12},{12,8},{16,20},{20,16},{24,28},{28,24},{1,5},{5... | collective-permute-start | bytes 1179656 | tf_op jit(solution)/shard_map/ppermute | solution.py:228
  80.4 2.2 %collective-permute-start.28 = (bf16[2,48,2048]{2,1,0:T(8,128)(2,1)S(1)}, bf16[2,48,2048]{2,1,0:T(8,128)(2,1)S(1)}, u32[]{:S(2)}, u32[]{:S(2)}) collective-permute-start(bf16[2,48,2048]{2,1,0:T(8,128)(2,1)S(1)} %get-tuple-element.144), channel_id=1, source_target_pairs={{0,4},{4,0},{8,12},{12,8},{16,20},{20,16},{24,28},{28,24},{1,5},{5... | collective-permute-start | bytes 1179656 | tf_op jit(solution)/shard_map/ppermute | solution.py:228
  80.6 2.1 %collective-permute-start.30 = (bf16[2,48,2048]{2,1,0:T(8,128)(2,1)S(1)}, bf16[2,48,2048]{2,1,0:T(8,128)(2,1)S(1)}, u32[]{:S(2)}, u32[]{:S(2)}) collective-permute-start(bf16[2,48,2048]{2,1,0:T(8,128)(2,1)S(1)} %get-tuple-element.149), channel_id=1, source_target_pairs={{0,4},{4,0},{8,12},{12,8},{16,20},{20,16},{24,28},{28,24},{1,5},{5... | collective-permute-start | bytes 1179656 | tf_op jit(solution)/shard_map/ppermute | solution.py:228
  81.9 1.7 %collective-permute-start.31 = (bf16[2,48,2048]{2,1,0:T(8,128)(2,1)S(1)}, bf16[2,48,2048]{2,1,0:T(8,128)(2,1)S(1)}, u32[]{:S(2)}, u32[]{:S(2)}) collective-permute-start(bf16[2,48,2048]{2,1,0:T(8,128)(2,1)S(1)} %get-tuple-element.150), channel_id=1, source_target_pairs={{0,4},{4,0},{8,12},{12,8},{16,20},{20,16},{24,28},{28,24},{1,5},{5... | collective-permute-start | bytes 1179656 | tf_op jit(solution)/shard_map/ppermute | solution.py:228
  82.6 3.2 %collective-permute-start.34 = (bf16[2,48,2048]{2,1,0:T(8,128)(2,1)S(1)}, bf16[2,48,2048]{2,1,0:T(8,128)(2,1)S(1)}, u32[]{:S(2)}, u32[]{:S(2)}) collective-permute-start(bf16[2,48,2048]{2,1,0:T(8,128)(2,1)S(1)} %shard_map.145.refs_0_), channel_id=1, source_target_pairs={{0,4},{4,0},{8,12},{12,8},{16,20},{20,16},{24,28},{28,24},{1,5},{5... | collective-permute-start | bytes 1179656 | tf_op jit(solution)/shard_map/ppermute | solution.py:228
  84.0 11.2 %collective-permute-start.32 = (bf16[2,48,2048]{2,1,0:T(8,128)(2,1)S(1)}, bf16[2,48,2048]{2,1,0:T(8,128)(2,1)S(1)}, u32[]{:S(2)}, u32[]{:S(2)}) collective-permute-start(bf16[2,48,2048]{2,1,0:T(8,128)(2,1)S(1)} %get-tuple-element.153), channel_id=1, source_target_pairs={{0,8},{4,12},{8,0},{12,4},{16,24},{20,28},{24,16},{28,20},{1,9},{5... | collective-permute-start | bytes 1179656 | tf_op jit(solution)/shard_map/ppermute | solution.py:228
  85.0 10.9 %collective-permute-start.33 = (bf16[2,48,2048]{2,1,0:T(8,128)(2,1)S(1)}, bf16[2,48,2048]{2,1,0:T(8,128)(2,1)S(1)}, u32[]{:S(2)}, u32[]{:S(2)}) collective-permute-start(bf16[2,48,2048]{2,1,0:T(8,128)(2,1)S(1)} %get-tuple-element.154), channel_id=1, source_target_pairs={{0,16},{4,20},{8,24},{12,28},{16,0},{20,4},{24,8},{28,12},{1,17},{... | collective-permute-start | bytes 1179656 | tf_op jit(solution)/shard_map/ppermute | solution.py:228
  89.9 1.5 %collective-permute-start.35 = (bf16[48,2048]{1,0:T(8,128)(2,1)S(1)}, bf16[48,2048]{1,0:T(8,128)(2,1)S(1)}, u32[]{:S(2)}, u32[]{:S(2)}) collective-permute-start(bf16[48,2048]{1,0:T(8,128)(2,1)S(1)} %get-tuple-element.159), channel_id=1, source_target_pairs={{0,4},{4,0},{8,12},{12,8},{16,20},{20,16},{24,28},{28,24},{1,5},{5... | collective-permute-start | bytes 589832 | tf_op jit(solution)/shard_map/ppermute | solution.py:228
  90.0 1.7 %collective-permute-start.36 = (bf16[48,2048]{1,0:T(8,128)(2,1)S(1)}, bf16[48,2048]{1,0:T(8,128)(2,1)S(1)}, u32[]{:S(2)}, u32[]{:S(2)}) collective-permute-start(bf16[48,2048]{1,0:T(8,128)(2,1)S(1)} %get-tuple-element.160), channel_id=1, source_target_pairs={{0,4},{4,0},{8,12},{12,8},{16,20},{20,16},{24,28},{28,24},{1,5},{5... | collective-permute-start | bytes 589832 | tf_op jit(solution)/shard_map/ppermute | solution.py:228
  96.0 10.1 %collective-permute-start.37 = (bf16[2,48,2048]{2,1,0:T(8,128)(2,1)S(1)}, bf16[2,48,2048]{2,1,0:T(8,128)(2,1)S(1)}, u32[]{:S(2)}, u32[]{:S(2)}) collective-permute-start(bf16[2,48,2048]{2,1,0:T(8,128)(2,1)S(1)} %get-tuple-element.161), channel_id=1, source_target_pairs={{0,8},{4,12},{8,0},{12,4},{16,24},{20,28},{24,16},{28,20},{1,9},{5... | collective-permute-start | bytes 1179656 | tf_op jit(solution)/shard_map/ppermute | solution.py:228
  97.2 9.7 %collective-permute-start.38 = (bf16[2,48,2048]{2,1,0:T(8,128)(2,1)S(1)}, bf16[2,48,2048]{2,1,0:T(8,128)(2,1)S(1)}, u32[]{:S(2)}, u32[]{:S(2)}) collective-permute-start(bf16[2,48,2048]{2,1,0:T(8,128)(2,1)S(1)} %get-tuple-element.162), channel_id=1, source_target_pairs={{0,16},{4,20},{8,24},{12,28},{16,0},{20,4},{24,8},{28,12},{1,17},{... | collective-permute-start | bytes 1179656 | tf_op jit(solution)/shard_map/ppermute | solution.py:228
  107.0 7.9 %collective-permute-start.40 = (bf16[48,2048]{1,0:T(8,128)(2,1)S(1)}, bf16[48,2048]{1,0:T(8,128)(2,1)S(1)}, u32[]{:S(2)}, u32[]{:S(2)}) collective-permute-start(bf16[48,2048]{1,0:T(8,128)(2,1)S(1)} %get-tuple-element.171), channel_id=1, source_target_pairs={{0,16},{4,20},{8,24},{12,28},{16,0},{20,4},{24,8},{28,12},{1,17},{... | collective-permute-start | bytes 589832 | tf_op jit(solution)/shard_map/ppermute | solution.py:228
  107.9 7.0 %collective-permute-start.39 = (bf16[48,2048]{1,0:T(8,128)(2,1)S(1)}, bf16[48,2048]{1,0:T(8,128)(2,1)S(1)}, u32[]{:S(2)}, u32[]{:S(2)}) collective-permute-start(bf16[48,2048]{1,0:T(8,128)(2,1)S(1)} %get-tuple-element.165), channel_id=1, source_target_pairs={{0,8},{4,12},{8,0},{12,4},{16,24},{20,28},{24,16},{28,20},{1,9},{5... | collective-permute-start | bytes 589832 | tf_op jit(solution)/shard_map/ppermute | solution.py:228
  109.4 8.8 %collective-permute-start.44 = (bf16[48,1024]{1,0:T(8,128)(2,1)S(1)}, bf16[48,1024]{1,0:T(8,128)(2,1)S(1)}, u32[]{:S(2)}, u32[]{:S(2)}) collective-permute-start(bf16[48,1024]{1,0:T(8,128)(2,1)S(1)} %get-tuple-element.177), channel_id=1, source_target_pairs={{0,1},{1,0},{2,3},{3,2},{4,5},{5,4},{6,7},{7,6},{8,9},{9,8},{10,11... | collective-permute-start | bytes 294920 | tf_op jit(solution)/shard_map/ppermute | solution.py:228
  112.5 13.0 %collective-permute-start.45 = (bf16[48,1024]{1,0:T(8,128)(2,1)S(1)}, bf16[48,1024]{1,0:T(8,128)(2,1)S(1)}, u32[]{:S(2)}, u32[]{:S(2)}) collective-permute-start(bf16[48,1024]{1,0:T(8,128)(2,1)S(1)} %get-tuple-element.178), channel_id=1, source_target_pairs={{0,2},{1,3},{2,0},{3,1},{4,6},{5,7},{6,4},{7,5},{8,10},{9,11},{10,... | collective-permute-start | bytes 294920 | tf_op jit(solution)/shard_map/ppermute | solution.py:228
  113.5 12.0 %collective-permute-start.46 = (bf16[48,1024]{1,0:T(8,128)(2,1)S(1)}, bf16[48,1024]{1,0:T(8,128)(2,1)S(1)}, u32[]{:S(2)}, u32[]{:S(2)}) collective-permute-start(bf16[48,1024]{1,0:T(8,128)(2,1)S(1)} %get-tuple-element.179), channel_id=1, source_target_pairs={{0,3},{1,2},{2,1},{3,0},{4,7},{5,6},{6,5},{7,4},{8,11},{9,10},{10,... | collective-permute-start | bytes 294920 | tf_op jit(solution)/shard_map/ppermute | solution.py:228
  115.2 10.8 %collective-permute-start.41 = (bf16[48,1024]{1,0:T(8,128)(2,1)S(1)}, bf16[48,1024]{1,0:T(8,128)(2,1)S(1)}, u32[]{:S(2)}, u32[]{:S(2)}) collective-permute-start(bf16[48,1024]{1,0:T(8,128)(2,1)S(1)} %get-tuple-element.173), channel_id=1, source_target_pairs={{0,1},{1,0},{2,3},{3,2},{4,5},{5,4},{6,7},{7,6},{8,9},{9,8},{10,11... | collective-permute-start | bytes 294920 | tf_op jit(solution)/shard_map/ppermute | solution.py:228
  116.4 12.4 %collective-permute-start.42 = (bf16[48,1024]{1,0:T(8,128)(2,1)S(1)}, bf16[48,1024]{1,0:T(8,128)(2,1)S(1)}, u32[]{:S(2)}, u32[]{:S(2)}) collective-permute-start(bf16[48,1024]{1,0:T(8,128)(2,1)S(1)} %get-tuple-element.174), channel_id=1, source_target_pairs={{0,2},{1,3},{2,0},{3,1},{4,6},{5,7},{6,4},{7,5},{8,10},{9,11},{10,... | collective-permute-start | bytes 294920 | tf_op jit(solution)/shard_map/ppermute | solution.py:228
  118.2 10.5 %collective-permute-start.43 = (bf16[48,1024]{1,0:T(8,128)(2,1)S(1)}, bf16[48,1024]{1,0:T(8,128)(2,1)S(1)}, u32[]{:S(2)}, u32[]{:S(2)}) collective-permute-start(bf16[48,1024]{1,0:T(8,128)(2,1)S(1)} %get-tuple-element.175), channel_id=1, source_target_pairs={{0,3},{1,2},{2,1},{3,0},{4,7},{5,6},{6,5},{7,4},{8,11},{9,10},{10,... | collective-permute-start | bytes 294920 | tf_op jit(solution)/shard_map/ppermute | solution.py:228

commit v4 on v3

--- a/solution.py
+++ b/solution.py
@@ -379,23 +379,33 @@
     return names, fast_dot(names.astype(BF16), tri).astype(jnp.int32)
 
 
-def carry_kernel(core, mine, shared, prefix, received, inner, grow, c, ids, *outs):
-    chunks, masks = len(outs) // N_MASKS, N_MASKS
-    states, lanes = prefix.shape
-    rows = inner.shape[0]
+def choice_kernel(mine, ids, weights, sending, keeping, shares):
+    chunks, _, slots, rows = sending.shape
+    share = rows // chunks
+    chosen = ids[...]
+    names, counts = choices(chosen, mine[0], N_MASKS, rows, chunks)
+    chunk_of = iota((slots, rows), 1) // share
+    slot = iota((slots, rows), 0)
+    fills = [counts[m : m + 1, :] - 1 == slot for m in range(N_MASKS)]
+    for m in range(N_MASKS):
+        row = fills[m] & (names[m : m + 1, :] > 0)
+        for chunk in range(chunks):
+            sending[chunk, m] = (row & (chunk_of == chunk)).astype(BF16)
+    for k in range(TOPK):
+        picks = [(fills[m] & (chosen[k : k + 1, :] == mine[0] ^ m)).astype(F32) for m in range(N_MASKS)]
+        pick = jnp.concatenate(picks, axis=0).T.astype(BF16)
+        for chunk in range(chunks):
+            keeping[chunk, k] = pick[chunk * share : (chunk + 1) * share]
+    shares[...] = jnp.concatenate([weights[...], jnp.zeros((8 - TOPK, rows), F32)], axis=0).T
+
+
+def carry_kernel(core, shared, prefix, received, inner, grow, c, sending, *outs):
     own = carried(prefix, received)
     carry = jnp.where(core[0] != 0, own, shared[...].astype(F32))
     out = inner[...] + grow[...] * fast_dot(c[...], carry.astype(BF16))
     out = out.astype(BF16)
-    names, counts = choices(ids[...], mine[0], masks, rows, chunks)
-    slots = outs[0].shape[0]
-    chunk_of = iota((slots, rows), 1) // (rows // chunks)
-    slot = iota((slots, rows), 0)
-    for chunk in range(chunks):
-        for mask in range(masks):
-            row = (counts[mask : mask + 1, :] - 1 == slot) & (names[mask : mask + 1, :] > 0)
-            pick = (row & (chunk_of == chunk)).astype(BF16)
-            outs[chunk * masks + mask][...] = fast_dot(pick, out).astype(BF16)
+    for n, picked in enumerate(outs):
+        picked[...] = fast_dot(sending[n // N_MASKS, n % N_MASKS], out).astype(BF16)
 
 
 def carried(prefix, received):
@@ -539,26 +549,15 @@
         out[...] = total[at // per_half, :, pl.ds(to, width)]
 
 
-def combine_kernel(chunk, mine, ids, weights, *refs):
+def combine_kernel(chunk, keeping, shares, *refs):
     parts, out = refs[:N_MASKS], refs[-1]
     earlier = refs[N_MASKS:-1]
-    slots = parts[0].shape[0]
-    rows = ids.shape[1]
-    share = rows // CHUNKS
+    share = keeping.shape[2]
     here = slice(chunk * share, (chunk + 1) * share)
-    chosen = ids[...]
-    names, counts = choices(chosen, mine[0], N_MASKS, rows, CHUNKS)
-    slot = iota((slots, rows), 0)
     values = jnp.concatenate([part[...] for part in parts], axis=0)
-    columns = jnp.concatenate([weights[...], jnp.zeros((8 - TOPK, rows), F32)], axis=0).T
     result = jnp.zeros((share, values.shape[1]), F32)
     for k in range(TOPK):
-        picks = []
-        for mask in range(N_MASKS):
-            row = (counts[mask : mask + 1, :] - 1 == slot) & (chosen[k : k + 1, :] == mine[0] ^ mask)
-            picks.append(row.astype(F32))
-        pick = jnp.concatenate(picks, axis=0).T[here].astype(BF16)
-        result = result + columns[here, k : k + 1] * fast_dot(pick, values)
+        result = result + shares[here, k : k + 1] * fast_dot(keeping[chunk, k], values)
     result = result.astype(BF16)
     if earlier:
         out[:share] = earlier[0][...]
@@ -637,16 +636,28 @@
         mix_kernel, [shape_of((rows, lanes), BF16), payload, payload], smem=1
     )(core, conv, rim, taps, b, fade, backward, through)
     received = swap(sent, "ctx", 1)
-    inner, grad_inner = call(inner_kernel, [block, block])(mixed, b, c, decay, grad, skip)
-    chip_sum = call(pair_kernel, payload)(received, after(kept, inner))
+    chip_sum = call(pair_kernel, payload)(received, kept)
     up = load(after(up_weight[0], chip_sum), 1)
+    inner, grad_inner = call(inner_kernel, [block, block])(
+        after(mixed, up), b, c, decay, grad, skip
+    )
     near, middle, far = (directed(chip_sum, mask) for mask in (2, 4, 6))
+    share = rows // CHUNKS
+    sending, keeping, shares = call(
+        choice_kernel,
+        [
+            shape_of((CHUNKS, N_MASKS, slots, rows), BF16),
+            shape_of((CHUNKS, TOPK, share, N_MASKS * slots), BF16),
+            shape_of((rows, 8), F32),
+        ],
+        smem=1,
+    )(mine, after(ids, up, inner), weights)
     prefix = call(reach_kernel, shape_of((states, lanes), BF16), smem=1)(
-        after(flip, up), near, middle, far
+        after(flip, sending), near, middle, far
     )
     shared = swap(prefix, "ctx", 1)
-    picked = call(carry_kernel, [shape_of((slots, lanes), BF16)] * (CHUNKS * experts), smem=2)(
-        core, mine, shared, prefix, received, inner, grow, c, ids
+    picked = call(carry_kernel, [shape_of((slots, lanes), BF16)] * (CHUNKS * experts), smem=1)(
+        core, shared, prefix, received, inner, grow, c, sending
     )
     down = load(after(down_weight[0], picked[0]), 1)
     masks = (2, 3, 1)
@@ -678,16 +689,19 @@
         return [parts[0]] + [arrived[m] for m in range(1, experts)]
 
     onward = shape_of((3, slots, half), BF16)
-    share = rows // CHUNKS
     first1, *others1 = to_experts(0)
     own1 = normed([after(first1, down), *others1])
     x1, y1 = along(own1, own1)
-    own2 = normed(to_experts(1))
-    from_x, from_y = along(*call(onward_kernel, [onward, onward])(x1, y1, own2))
+    arrived2 = to_experts(1)
+    own2 = normed(arrived2)
+    twin_own1 = twin(after(own1, arrived2[1]))
+    to_x, to_y = call(onward_kernel, [onward, onward])(x1, y1, after(own2, twin_own1))
+    from_x, from_y = along(to_x, to_y)
     double = shape_of((2, slots, half), BF16)
     sums = [row_block, double, double, half_block, half_block]
-    now = [own1, x1, y1, own2]
-    (*odd1, odd_own2), (*even1, even_own2) = expert_rows(now, [twin(block) for block in now], up, down)
+    now = [own1, after(x1, to_x), after(y1, to_x), own2]
+    twins = [twin_own1] + [twin(block) for block in now[1:]]
+    (*odd1, odd_own2), (*even1, even_own2) = expert_rows(now, twins, up, down)
     far1, x2, y2, own_sum1, to_x, to_y, rest_x1, rest_y1 = call(arrive_kernel, [row_block] * 3 + sums)(
         after(from_x, even1[0]), from_y, *even1, *(twin(block) for block in odd1)
     )
@@ -707,19 +721,19 @@
         from_x4, from_y4, rest_x1, rest_y1, even_far2, *(twin(part) for part in odd_far2)
     )
     from_x5, from_y5 = along(to_x, to_y)
-    next_x, next_y = call(relay_kernel, [half_block, half_block])(from_x5, from_y5, rest_x2, rest_y2)
+    grad_conv = call(grad_kernel, block, smem=1)(
+        core, shared, after(prefix, to_x), received, grad_inner, fade, b
+    )
+    next_x, next_y = call(relay_kernel, [half_block, half_block])(from_x5, from_y5, after(rest_x2, grad_conv), rest_y2)
     done1 = results(0, own_sum1, from_x3, from_y3, after(from_x5, next_x), from_y5)
     last_x, last_y = along(next_x, next_y)
     back1 = back(done1)
-    grad_conv = call(grad_kernel, block, smem=1)(
-        core, shared, after(prefix, done1[0]), received, grad_inner, fade, b
-    )
-    done2 = results(slice(None), after(own_sum2, grad_conv), from_x4, from_y4, last_x, last_y)
-    combined = call(
-        lambda *refs: combine_kernel(0, *refs), shape_of((share, lanes), BF16), smem=1
-    )(mine, after(ids, done2[0]), weights, *back1)
-    moe_out = call(lambda *refs: combine_kernel(1, *refs), shape_of((rows, lanes), BF16), smem=1)(
-        mine, ids, weights, *back(done2), combined
+    done2 = results(slice(None), own_sum2, from_x4, from_y4, last_x, last_y)
+    combined = call(lambda *refs: combine_kernel(0, *refs), shape_of((share, lanes), BF16))(
+        after(keeping, done2[0]), shares, *back1
+    )
+    moe_out = call(lambda *refs: combine_kernel(1, *refs), shape_of((rows, lanes), BF16))(
+        keeping, shares, *back(done2), combined
     )
     return (moe_out, grad_conv)
 

time: 130 us -> 129 us (level)
  waiting for transfers between devices: 44.2 us -> 41.6 us
  starting transfers between devices: 43.6 us -> 45.1 us
    ppermute x43, starting transfers between devices: 37.2 us -> 38.9 us  [swap(): return lax.ppermute(x, axis, [(i, i ^ mask) for i in range(size)])]
    ppermute x43, waiting for transfers between devices: 40.5 us -> 39.1 us  [swap(): return lax.ppermute(x, axis, [(i, i ^ mask) for i in range(size)])]
    pallas_call x21 -> x22, Pallas kernels: 29.3 us -> 29 us  [run(): pl.pallas_call(body, out_shape=outs, in_specs=specs, out_specs=jax.tree.m...]
  transfers between devices with their start and end apart: 47 -> 47, of which waited for: 22 -> 21; matrix products, arithmetic and copies ran while one was open for 0% -> 0% of each run, Pallas kernels for 28% -> 29%
where the time goes in v4:
time: 129 us
  starting transfers between devices  45.1 us (35%)
  waiting for transfers between devices  41.6 us (32%)
  Pallas kernels  40.4 us (31%)
    ppermute x43, waiting for transfers between devices, swap(): return lax.ppermute(x, axis, [(i, i ^ mask) for i in range(size)])  39.1 us
    ppermute x43, starting transfers between devices, swap(): return lax.ppermute(x, axis, [(i, i ^ mask) for i in range(size)])  38.9 us
    pallas_call x22, Pallas kernels, run(): pl.pallas_call(body, out_shape=outs, in_specs=specs, out_specs=jax.tree.m...  29 us
    pallas_call x2, Pallas kernels, load(): pl.pallas_call(load_kernel, out_shape=pltpu.VMEM(source.shape, source.dty...  9.17 us
    ppermute x3, starting transfers between devices, directed(): return lax.ppermute(x, 'ctx', route)  3.88 us
  transfers between devices with their start and end apart: 47, of which 21 were waited for; matrix products, arithmetic and copies ran while one was open for 0% of the time, Pallas kernels for 29%

profile of v4, /device:TPU:0, one launch (start us, length us, event | category | flops | bytes accessed | tf_op | source)
XLA Modules:
  0.0 128.7 jit_solution(12424003850090460555)
XLA Ops:
  0.6 0.7 slice.3
  1.4 2.3 %collective-permute-start = (bf16[8,1024]{1,0:T(8,128)(2,1)S(1)}, bf16[8,1024]{1,0:T(8,128)(2,1)S(1)}, u32[]{:S(2)}, u32[]{:S(2)}) collective-permute-start(bf16[8,1024]{1,0:T(8,128)(2,1)S(1)} %slice.3), channel_id=1, source_target_pairs={{0,4},{4,8},{8,12},{12,16},{16,20},{20,24},{24,28},{1,5},{5,9},{9,... | collective-permute-start | bytes 49160 | tf_op jit(solution)/shard_map/ppermute | solution.py:19
  3.7 2.2 %shard_map.131 = (f32[16,128]{1,0:T(8,128)S(1)}, bf16[128,128]{1,0:T(8,128)(2,1)S(1)}, bf16[128,1024]{1,0:T(8,128)(2,1)S(1)}, bf16[128,128]{1,0:T(8,128)(2,1)S(1...) custom-call(f32[16,128]{1,0:T(8,128)} %refs_0_, ...), custom_call_target="tpu_custom_call" | custom-call | flops 1 | bytes 1 | tf_op jit(solution)/shard_map/pallas_call | solution.py:624
  6.6 2.7 %collective-permute-start.1 = (bf16[136,1024]{1,0:T(8,128)(2,1)S(1)}, bf16[136,1024]{1,0:T(8,128)(2,1)S(1)}, u32[]{:S(2)}, u32[]{:S(2)}) collective-permute-start(bf16[136,1024]{1,0:T(8,128)(2,1)S(1)} %get-tuple-element.111), channel_id=1, source_target_pairs={{0,4},{4,0},{8,12},{12,8},{16,20},{20,16},{24,28},{28,24},{1,5},{5... | collective-permute-start | bytes 835592 | tf_op jit(solution)/shard_map/ppermute | solution.py:228
  9.3 1.2 collective-permute-done.1.received
  10.5 1.3 %collective-permute-start.4 = (bf16[136,1024]{1,0:T(8,128)(2,1)S(1)}, bf16[136,1024]{1,0:T(8,128)(2,1)S(1)}, u32[]{:S(2)}, u32[]{:S(2)}) collective-permute-start(bf16[136,1024]{1,0:T(8,128)(2,1)S(1)} %shard_map.133), channel_id=1, source_target_pairs={{4,28},{12,20},{16,8},{24,0},{5,29},{13,21},{17,9},{25,1},{6,30},{... | collective-permute-start | bytes 835592 | tf_op jit(solution)/shard_map/ppermute | solution.py:576
  11.8 1.3 %collective-permute-start.3 = (bf16[136,1024]{1,0:T(8,128)(2,1)S(1)}, bf16[136,1024]{1,0:T(8,128)(2,1)S(1)}, u32[]{:S(2)}, u32[]{:S(2)}) collective-permute-start(bf16[136,1024]{1,0:T(8,128)(2,1)S(1)} %shard_map.133), channel_id=1, source_target_pairs={{4,20},{12,28},{16,0},{24,8},{5,21},{13,29},{17,1},{25,9},{6,22},{... | collective-permute-start | bytes 835592 | tf_op jit(solution)/shard_map/ppermute | solution.py:576
  13.1 1.3 %collective-permute-start.2 = (bf16[136,1024]{1,0:T(8,128)(2,1)S(1)}, bf16[136,1024]{1,0:T(8,128)(2,1)S(1)}, u32[]{:S(2)}, u32[]{:S(2)}) collective-permute-start(bf16[136,1024]{1,0:T(8,128)(2,1)S(1)} %shard_map.133), channel_id=1, source_target_pairs={{4,12},{8,0},{20,28},{24,16},{5,13},{9,1},{21,29},{25,17},{6,14},{... | collective-permute-start | bytes 835592 | tf_op jit(solution)/shard_map/ppermute | solution.py:576
  14.4 4.6 %shard_map.134.refs_8_.refs_6_.refs_2_ = bf16[4096,1536]{1,0:T(8,128)(2,1)S(1)} custom-call(bf16[4096,1536]{1,0:T(8,128)(2,1)} %bitcast.9), custom_call_target="tpu_custom_call" | custom-call | flops 1 | bytes 1 | tf_op jit(solution)/shard_map/pallas_call | solution.py:298
  19.0 1.1 shard_map.135
  20.4 2.5 %collective-permute-done.3.middle = bf16[136,1024]{1,0:T(8,128)(2,1)S(1)} collective-permute-done((bf16[136,1024]{1,0:T(8,128)(2,1)S(1)}, bf16[136,1024]{1,0:T(8,128)(2,1)S(1)}, u32[]{:S(2)}, u32[]{:S(2)}) %collective-permute-start.3) | collective-permute-done | bytes 278560 | tf_op jit(solution)/shard_map/ppermute | solution.py:576
  23.0 2.1 %collective-permute-start.5 = (bf16[128,1024]{1,0:T(8,128)(2,1)S(1)}, bf16[128,1024]{1,0:T(8,128)(2,1)S(1)}, u32[]{:S(2)}, u32[]{:S(2)}) collective-permute-start(bf16[128,1024]{1,0:T(8,128)(2,1)S(1)} %shard_map.137.prefix), channel_id=1, source_target_pairs={{0,4},{4,0},{8,12},{12,8},{16,20},{20,16},{24,28},{28,24},{1,5},{5... | collective-permute-start | bytes 786440 | tf_op jit(solution)/shard_map/ppermute | solution.py:228
  25.1 1.2 collective-permute-done.5.shared
  27.0 1.7 %collective-permute-start.6 = (bf16[48,1024]{1,0:T(8,128)(2,1)S(1)}, bf16[48,1024]{1,0:T(8,128)(2,1)S(1)}, u32[]{:S(2)}, u32[]{:S(2)}) collective-permute-start(bf16[48,1024]{1,0:T(8,128)(2,1)S(1)} %get-tuple-element.132), channel_id=1, source_target_pairs={{0,1},{1,0},{2,3},{3,2},{4,5},{5,4},{6,7},{7,6},{8,9},{9,8},{10,11... | collective-permute-start | bytes 294920 | tf_op jit(solution)/shard_map/ppermute | solution.py:228
  28.6 2.6 %collective-permute-start.7 = (bf16[48,1024]{1,0:T(8,128)(2,1)S(1)}, bf16[48,1024]{1,0:T(8,128)(2,1)S(1)}, u32[]{:S(2)}, u32[]{:S(2)}) collective-permute-start(bf16[48,1024]{1,0:T(8,128)(2,1)S(1)} %get-tuple-element.133), channel_id=1, source_target_pairs={{0,2},{1,3},{2,0},{3,1},{4,6},{5,7},{6,4},{7,5},{8,10},{9,11},{10,... | collective-permute-start | bytes 294920 | tf_op jit(solution)/shard_map/ppermute | solution.py:228
  31.4 0.7 collective-permute-start.11
  32.1 4.6 %shard_map.139.refs_9_.refs_7_.refs_3_ = bf16[1536,4096]{1,0:T(8,128)(2,1)S(1)} custom-call(bf16[1536,4096]{1,0:T(8,128)(2,1)} %bitcast.10), custom_call_target="tpu_custom_call" | custom-call | flops 1 | bytes 1 | tf_op jit(solution)/shard_map/pallas_call | solution.py:298
  36.7 2.6 %collective-permute-done.7.refs_2_ = bf16[48,1024]{1,0:T(8,128)(2,1)S(1)} collective-permute-done((bf16[48,1024]{1,0:T(8,128)(2,1)S(1)}, bf16[48,1024]{1,0:T(8,128)(2,1)S(1)}, u32[]{:S(2)}, u32[]{:S(2)}) %collective-permute-start.7) | collective-permute-done | bytes 98336 | tf_op jit(solution)/shard_map/ppermute | solution.py:228
  39.7 0.7 collective-permute-start.10
  40.4 1.5 %collective-permute-start.9 = (bf16[2,48,2048]{2,1,0:T(8,128)(2,1)S(1)}, bf16[2,48,2048]{2,1,0:T(8,128)(2,1)S(1)}, u32[]{:S(2)}, u32[]{:S(2)}) collective-permute-start(bf16[2,48,2048]{2,1,0:T(8,128)(2,1)S(1)} %shard_map.140.refs_0_), channel_id=1, source_target_pairs={{0,8},{4,12},{8,0},{12,4},{16,24},{20,28},{24,16},{28,20},{1,9},{5... | collective-permute-start | bytes 1179656 | tf_op jit(solution)/shard_map/ppermute | solution.py:228
  41.9 2.7 %collective-permute-start.12 = (bf16[48,1024]{1,0:T(8,128)(2,1)S(1)}, bf16[48,1024]{1,0:T(8,128)(2,1)S(1)}, u32[]{:S(2)}, u32[]{:S(2)}) collective-permute-start(bf16[48,1024]{1,0:T(8,128)(2,1)S(1)} %get-tuple-element.137), channel_id=1, source_target_pairs={{0,2},{1,3},{2,0},{3,1},{4,6},{5,7},{6,4},{7,5},{8,10},{9,11},{10,... | collective-permute-start | bytes 294920 | tf_op jit(solution)/shard_map/ppermute | solution.py:228
  44.6 1.4 %collective-permute-start.13 = (bf16[48,1024]{1,0:T(8,128)(2,1)S(1)}, bf16[48,1024]{1,0:T(8,128)(2,1)S(1)}, u32[]{:S(2)}, u32[]{:S(2)}) collective-permute-start(bf16[48,1024]{1,0:T(8,128)(2,1)S(1)} %get-tuple-element.138), channel_id=1, source_target_pairs={{0,3},{1,2},{2,1},{3,0},{4,7},{5,6},{6,5},{7,4},{8,11},{9,10},{10,... | collective-permute-start | bytes 294920 | tf_op jit(solution)/shard_map/ppermute | solution.py:228
  45.9 6.6 %collective-permute-done.12.refs_2_ = bf16[48,1024]{1,0:T(8,128)(2,1)S(1)} collective-permute-done((bf16[48,1024]{1,0:T(8,128)(2,1)S(1)}, bf16[48,1024]{1,0:T(8,128)(2,1)S(1)}, u32[]{:S(2)}, u32[]{:S(2)}) %collective-permute-start.12) | collective-permute-done | bytes 98336 | tf_op jit(solution)/shard_map/ppermute | solution.py:228
  54.1 1.4 %collective-permute-start.19 = (bf16[3,48,2048]{2,1,0:T(8,128)(2,1)S(1)}, bf16[3,48,2048]{2,1,0:T(8,128)(2,1)S(1)}, u32[]{:S(2)}, u32[]{:S(2)}) collective-permute-start(bf16[3,48,2048]{2,1,0:T(8,128)(2,1)S(1)} %get-tuple-element.146), channel_id=1, source_target_pairs={{0,16},{4,20},{8,24},{12,28},{16,0},{20,4},{24,8},{28,12},{1,17},{... | collective-permute-start | bytes 1769480 | tf_op jit(solution)/shard_map/ppermute | solution.py:228
  55.7 9.9 %shard_map.143 = (bf16[2,48,2048]{2,1,0:T(8,128)(2,1)S(1)}, bf16[2,48,2048]{2,1,0:T(8,128)(2,1)S(1)}, bf16[2,48,2048]{2,1,0:T(8,128)(2,1)S(1)}, bf16[2,48,2048]{...) custom-call(bf16[2,48,2048]{2,1,0:T(8,128)(2,1)S(1)} %shard_map.140., ...), custom_call_target="tpu_custom_call" | custom-call | flops 1 | bytes 1 | tf_op jit(solution)/shard_map/pallas_call | solution.py:213
  66.3 3.0 %collective-permute-done.15.from_x = bf16[3,48,2048]{2,1,0:T(8,128)(2,1)S(1)} collective-permute-done((bf16[3,48,2048]{2,1,0:T(8,128)(2,1)S(1)}, bf16[3,48,2048]{2,1,0:T(8,128)(2,1)S(1)}, u32[]{:S(2)}, u32[]{:S(2)}) %collective-permute-start.15) | collective-permute-done | bytes 589856 | tf_op jit(solution)/shard_map/ppermute | solution.py:228
  70.6 1.5 %collective-permute-start.26 = (bf16[2,48,2048]{2,1,0:T(8,128)(2,1)S(1)}, bf16[2,48,2048]{2,1,0:T(8,128)(2,1)S(1)}, u32[]{:S(2)}, u32[]{:S(2)}) collective-permute-start(bf16[2,48,2048]{2,1,0:T(8,128)(2,1)S(1)} %get-tuple-element.156), channel_id=1, source_target_pairs={{0,8},{4,12},{8,0},{12,4},{16,24},{20,28},{24,16},{28,20},{1,9},{5... | collective-permute-start | bytes 1179656 | tf_op jit(solution)/shard_map/ppermute | solution.py:228
  72.8 7.7 %shard_map.145 = (bf16[2,48,2048]{2,1,0:T(8,128)(2,1)S(1)}, bf16[2,48,2048]{2,1,0:T(8,128)(2,1)S(1)}, bf16[2,48,2048]{2,1,0:T(8,128)(2,1)S(1)}, bf16[2,48,2048]{...) custom-call(bf16[2,48,2048]{2,1,0:T(8,128)(2,1)S(1)} %get-tuple-element.152.refs_0_, ...), custom_call_target="tpu_custom_call" | custom-call | flops 1 | bytes 1 | tf_op jit(solution)/shard_map/pallas_call | solution.py:213
  81.1 1.0 collective-permute-done.26.from_x.refs_2_
  82.0 1.2 collective-permute-done.27.from_y.refs_3_
  84.1 1.6 %collective-permute-start.32 = (bf16[2,48,2048]{2,1,0:T(8,128)(2,1)S(1)}, bf16[2,48,2048]{2,1,0:T(8,128)(2,1)S(1)}, u32[]{:S(2)}, u32[]{:S(2)}) collective-permute-start(bf16[2,48,2048]{2,1,0:T(8,128)(2,1)S(1)} %get-tuple-element.168), channel_id=1, source_target_pairs={{0,8},{4,12},{8,0},{12,4},{16,24},{20,28},{24,16},{28,20},{1,9},{5... | collective-permute-start | bytes 1179656 | tf_op jit(solution)/shard_map/ppermute | solution.py:228
  86.0 4.1 %shard_map.148 = (bf16[48,2048]{1,0:T(8,128)(2,1)S(1)}, bf16[48,2048]{1,0:T(8,128)(2,1)S(1)}, bf16[2,48,2048]{2,1,0:T(8,128)(2,1)S(1)}) custom-call(bf16[2,48,2048]{2,1,0:T(8,128)(2,1)S(1)} %shard_map.146.refs_0_, bf16[2,48,2048]{2,1,0:T(8,128)(2,1)S(1)} %collective-permute-done.34.refs_1_, bf16[4096,1536]{1,0:T(8,128)(2,1)S(1)} %shard_map.134.refs_8_.refs_6_.refs_2_, ...), custom_call_target="tpu_custom_call" | custom-call | flops 1 | bytes 1 | tf_op jit(solution)/shard_map/pallas_call | solution.py:213
  90.7 0.9 collective-permute-done.35.first_half
  91.9 3.5 %collective-permute-done.32.from_x.refs_2_ = bf16[2,48,2048]{2,1,0:T(8,128)(2,1)S(1)} collective-permute-done((bf16[2,48,2048]{2,1,0:T(8,128)(2,1)S(1)}, bf16[2,48,2048]{2,1,0:T(8,128)(2,1)S(1)}, u32[]{:S(2)}, u32[]{:S(2)}) %collective-permute-start.32) | collective-permute-done | bytes 393248 | tf_op jit(solution)/shard_map/ppermute | solution.py:228
  95.4 1.2 collective-permute-done.33.from_y.refs_3_
  97.3 1.5 %collective-permute-start.37 = (bf16[2,48,2048]{2,1,0:T(8,128)(2,1)S(1)}, bf16[2,48,2048]{2,1,0:T(8,128)(2,1)S(1)}, u32[]{:S(2)}, u32[]{:S(2)}) collective-permute-start(bf16[2,48,2048]{2,1,0:T(8,128)(2,1)S(1)} %get-tuple-element.176), channel_id=1, source_target_pairs={{0,8},{4,12},{8,0},{12,4},{16,24},{20,28},{24,16},{28,20},{1,9},{5... | collective-permute-start | bytes 1179656 | tf_op jit(solution)/shard_map/ppermute | solution.py:228
  98.8 1.1 shard_map.150
  99.9 6.9 %collective-permute-done.38.from_y.refs_5_ = bf16[2,48,2048]{2,1,0:T(8,128)(2,1)S(1)} collective-permute-done((bf16[2,48,2048]{2,1,0:T(8,128)(2,1)S(1)}, bf16[2,48,2048]{2,1,0:T(8,128)(2,1)S(1)}, u32[]{:S(2)}, u32[]{:S(2)}) %collective-permute-start.38) | collective-permute-done | bytes 393248 | tf_op jit(solution)/shard_map/ppermute | solution.py:228
  107.3 1.4 %collective-permute-start.40 = (bf16[48,2048]{1,0:T(8,128)(2,1)S(1)}, bf16[48,2048]{1,0:T(8,128)(2,1)S(1)}, u32[]{:S(2)}, u32[]{:S(2)}) collective-permute-start(bf16[48,2048]{1,0:T(8,128)(2,1)S(1)} %get-tuple-element.184), channel_id=1, source_target_pairs={{0,16},{4,20},{8,24},{12,28},{16,0},{20,4},{24,8},{28,12},{1,17},{... | collective-permute-start | bytes 589832 | tf_op jit(solution)/shard_map/ppermute | solution.py:228
  109.6 1.8 %collective-permute-start.44 = (bf16[48,1024]{1,0:T(8,128)(2,1)S(1)}, bf16[48,1024]{1,0:T(8,128)(2,1)S(1)}, u32[]{:S(2)}, u32[]{:S(2)}) collective-permute-start(bf16[48,1024]{1,0:T(8,128)(2,1)S(1)} %get-tuple-element.193), channel_id=1, source_target_pairs={{0,1},{1,0},{2,3},{3,2},{4,5},{5,4},{6,7},{7,6},{8,9},{9,8},{10,11... | collective-permute-start | bytes 294920 | tf_op jit(solution)/shard_map/ppermute | solution.py:228
  111.4 1.4 %collective-permute-start.45 = (bf16[48,1024]{1,0:T(8,128)(2,1)S(1)}, bf16[48,1024]{1,0:T(8,128)(2,1)S(1)}, u32[]{:S(2)}, u32[]{:S(2)}) collective-permute-start(bf16[48,1024]{1,0:T(8,128)(2,1)S(1)} %get-tuple-element.194), channel_id=1, source_target_pairs={{0,2},{1,3},{2,0},{3,1},{4,6},{5,7},{6,4},{7,5},{8,10},{9,11},{10,... | collective-permute-start | bytes 294920 | tf_op jit(solution)/shard_map/ppermute | solution.py:228
  112.8 1.2 collective-permute-start.46
  114.7 1.8 %collective-permute-start.41 = (bf16[48,1024]{1,0:T(8,128)(2,1)S(1)}, bf16[48,1024]{1,0:T(8,128)(2,1)S(1)}, u32[]{:S(2)}, u32[]{:S(2)}) collective-permute-start(bf16[48,1024]{1,0:T(8,128)(2,1)S(1)} %get-tuple-element.186), channel_id=1, source_target_pairs={{0,1},{1,0},{2,3},{3,2},{4,5},{5,4},{6,7},{7,6},{8,9},{9,8},{10,11... | collective-permute-start | bytes 294920 | tf_op jit(solution)/shard_map/ppermute | solution.py:228
  116.5 1.4 %collective-permute-start.42 = (bf16[48,1024]{1,0:T(8,128)(2,1)S(1)}, bf16[48,1024]{1,0:T(8,128)(2,1)S(1)}, u32[]{:S(2)}, u32[]{:S(2)}) collective-permute-start(bf16[48,1024]{1,0:T(8,128)(2,1)S(1)} %get-tuple-element.187), channel_id=1, source_target_pairs={{0,2},{1,3},{2,0},{3,1},{4,6},{5,7},{6,4},{7,5},{8,10},{9,11},{10,... | collective-permute-start | bytes 294920 | tf_op jit(solution)/shard_map/ppermute | solution.py:228
  117.9 2.1 %collective-permute-start.43 = (bf16[48,1024]{1,0:T(8,128)(2,1)S(1)}, bf16[48,1024]{1,0:T(8,128)(2,1)S(1)}, u32[]{:S(2)}, u32[]{:S(2)}) collective-permute-start(bf16[48,1024]{1,0:T(8,128)(2,1)S(1)} %get-tuple-element.188), channel_id=1, source_target_pairs={{0,3},{1,2},{2,1},{3,0},{4,7},{5,6},{6,5},{7,4},{8,11},{9,10},{10,... | collective-permute-start | bytes 294920 | tf_op jit(solution)/shard_map/ppermute | solution.py:228
  120.0 2.3 %collective-permute-done.45.refs_4_ = bf16[48,1024]{1,0:T(8,128)(2,1)S(1)} collective-permute-done((bf16[48,1024]{1,0:T(8,128)(2,1)S(1)}, bf16[48,1024]{1,0:T(8,128)(2,1)S(1)}, u32[]{:S(2)}, u32[]{:S(2)}) %collective-permute-start.45) | collective-permute-done | bytes 98336 | tf_op jit(solution)/shard_map/ppermute | solution.py:228
  122.5 5.2 %collective-permute-done.42.refs_4_ = bf16[48,1024]{1,0:T(8,128)(2,1)S(1)} collective-permute-done((bf16[48,1024]{1,0:T(8,128)(2,1)S(1)}, bf16[48,1024]{1,0:T(8,128)(2,1)S(1)}, u32[]{:S(2)}, u32[]{:S(2)}) %collective-permute-start.42) | collective-permute-done | bytes 98336 | tf_op jit(solution)/shard_map/ppermute | solution.py:228
  127.8 1.0 shard_map.155
  (72 shorter events, 12.4 us)
Async XLA Ops:
  1.4 4.5 %collective-permute-start = (bf16[8,1024]{1,0:T(8,128)(2,1)S(1)}, bf16[8,1024]{1,0:T(8,128)(2,1)S(1)}, u32[]{:S(2)}, u32[]{:S(2)}) collective-permute-start(bf16[8,1024]{1,0:T(8,128)(2,1)S(1)} %slice.3), channel_id=1, source_target_pairs={{0,4},{4,8},{8,12},{12,16},{16,20},{20,24},{24,28},{1,5},{5,9},{9,... | collective-permute-start | bytes 49160 | tf_op jit(solution)/shard_map/ppermute | solution.py:19
  6.6 3.9 %collective-permute-start.1 = (bf16[136,1024]{1,0:T(8,128)(2,1)S(1)}, bf16[136,1024]{1,0:T(8,128)(2,1)S(1)}, u32[]{:S(2)}, u32[]{:S(2)}) collective-permute-start(bf16[136,1024]{1,0:T(8,128)(2,1)S(1)} %get-tuple-element.111), channel_id=1, source_target_pairs={{0,4},{4,0},{8,12},{12,8},{16,20},{20,16},{24,28},{28,24},{1,5},{5... | collective-permute-start | bytes 835592 | tf_op jit(solution)/shard_map/ppermute | solution.py:228
  10.5 9.8 %collective-permute-start.4 = (bf16[136,1024]{1,0:T(8,128)(2,1)S(1)}, bf16[136,1024]{1,0:T(8,128)(2,1)S(1)}, u32[]{:S(2)}, u32[]{:S(2)}) collective-permute-start(bf16[136,1024]{1,0:T(8,128)(2,1)S(1)} %shard_map.133), channel_id=1, source_target_pairs={{4,28},{12,20},{16,8},{24,0},{5,29},{13,21},{17,9},{25,1},{6,30},{... | collective-permute-start | bytes 835592 | tf_op jit(solution)/shard_map/ppermute | solution.py:576
  11.8 11.0 %collective-permute-start.3 = (bf16[136,1024]{1,0:T(8,128)(2,1)S(1)}, bf16[136,1024]{1,0:T(8,128)(2,1)S(1)}, u32[]{:S(2)}, u32[]{:S(2)}) collective-permute-start(bf16[136,1024]{1,0:T(8,128)(2,1)S(1)} %shard_map.133), channel_id=1, source_target_pairs={{4,20},{12,28},{16,0},{24,8},{5,21},{13,29},{17,1},{25,9},{6,22},{... | collective-permute-start | bytes 835592 | tf_op jit(solution)/shard_map/ppermute | solution.py:576
  13.1 9.7 %collective-permute-start.2 = (bf16[136,1024]{1,0:T(8,128)(2,1)S(1)}, bf16[136,1024]{1,0:T(8,128)(2,1)S(1)}, u32[]{:S(2)}, u32[]{:S(2)}) collective-permute-start(bf16[136,1024]{1,0:T(8,128)(2,1)S(1)} %shard_map.133), channel_id=1, source_target_pairs={{4,12},{8,0},{20,28},{24,16},{5,13},{9,1},{21,29},{25,17},{6,14},{... | collective-permute-start | bytes 835592 | tf_op jit(solution)/shard_map/ppermute | solution.py:576
  23.0 3.2 %collective-permute-start.5 = (bf16[128,1024]{1,0:T(8,128)(2,1)S(1)}, bf16[128,1024]{1,0:T(8,128)(2,1)S(1)}, u32[]{:S(2)}, u32[]{:S(2)}) collective-permute-start(bf16[128,1024]{1,0:T(8,128)(2,1)S(1)} %shard_map.137.prefix), channel_id=1, source_target_pairs={{0,4},{4,0},{8,12},{12,8},{16,20},{20,16},{24,28},{28,24},{1,5},{5... | collective-permute-start | bytes 786440 | tf_op jit(solution)/shard_map/ppermute | solution.py:228
  27.0 9.7 %collective-permute-start.6 = (bf16[48,1024]{1,0:T(8,128)(2,1)S(1)}, bf16[48,1024]{1,0:T(8,128)(2,1)S(1)}, u32[]{:S(2)}, u32[]{:S(2)}) collective-permute-start(bf16[48,1024]{1,0:T(8,128)(2,1)S(1)} %get-tuple-element.132), channel_id=1, source_target_pairs={{0,1},{1,0},{2,3},{3,2},{4,5},{5,4},{6,7},{7,6},{8,9},{9,8},{10,11... | collective-permute-start | bytes 294920 | tf_op jit(solution)/shard_map/ppermute | solution.py:228
  28.6 10.7 %collective-permute-start.7 = (bf16[48,1024]{1,0:T(8,128)(2,1)S(1)}, bf16[48,1024]{1,0:T(8,128)(2,1)S(1)}, u32[]{:S(2)}, u32[]{:S(2)}) collective-permute-start(bf16[48,1024]{1,0:T(8,128)(2,1)S(1)} %get-tuple-element.133), channel_id=1, source_target_pairs={{0,2},{1,3},{2,0},{3,1},{4,6},{5,7},{6,4},{7,5},{8,10},{9,11},{10,... | collective-permute-start | bytes 294920 | tf_op jit(solution)/shard_map/ppermute | solution.py:228
  31.2 8.1 %collective-permute-start.8 = (bf16[48,1024]{1,0:T(8,128)(2,1)S(1)}, bf16[48,1024]{1,0:T(8,128)(2,1)S(1)}, u32[]{:S(2)}, u32[]{:S(2)}) collective-permute-start(bf16[48,1024]{1,0:T(8,128)(2,1)S(1)} %get-tuple-element.134), channel_id=1, source_target_pairs={{0,3},{1,2},{2,1},{3,0},{4,7},{5,6},{6,5},{7,4},{8,11},{9,10},{10,... | collective-permute-start | bytes 294920 | tf_op jit(solution)/shard_map/ppermute | solution.py:228
  31.4 8.1 %collective-permute-start.11 = (bf16[48,1024]{1,0:T(8,128)(2,1)S(1)}, bf16[48,1024]{1,0:T(8,128)(2,1)S(1)}, u32[]{:S(2)}, u32[]{:S(2)}) collective-permute-start(bf16[48,1024]{1,0:T(8,128)(2,1)S(1)} %get-tuple-element.136), channel_id=1, source_target_pairs={{0,1},{1,0},{2,3},{3,2},{4,5},{5,4},{6,7},{7,6},{8,9},{9,8},{10,11... | collective-permute-start | bytes 294920 | tf_op jit(solution)/shard_map/ppermute | solution.py:228
  39.6 13.3 %collective-permute-start.14 = (bf16[2,48,2048]{2,1,0:T(8,128)(2,1)S(1)}, bf16[2,48,2048]{2,1,0:T(8,128)(2,1)S(1)}, u32[]{:S(2)}, u32[]{:S(2)}) collective-permute-start(bf16[2,48,2048]{2,1,0:T(8,128)(2,1)S(1)} %shard_map.140.refs_0_), channel_id=1, source_target_pairs={{0,4},{4,0},{8,12},{12,8},{16,20},{20,16},{24,28},{28,24},{1,5},{5... | collective-permute-start | bytes 1179656 | tf_op jit(solution)/shard_map/ppermute | solution.py:228
  39.7 13.2 %collective-permute-start.10 = (bf16[2,48,2048]{2,1,0:T(8,128)(2,1)S(1)}, bf16[2,48,2048]{2,1,0:T(8,128)(2,1)S(1)}, u32[]{:S(2)}, u32[]{:S(2)}) collective-permute-start(bf16[2,48,2048]{2,1,0:T(8,128)(2,1)S(1)} %shard_map.140.refs_0_), channel_id=1, source_target_pairs={{0,16},{4,20},{8,24},{12,28},{16,0},{20,4},{24,8},{28,12},{1,17},{... | collective-permute-start | bytes 1179656 | tf_op jit(solution)/shard_map/ppermute | solution.py:228
  40.4 12.5 %collective-permute-start.9 = (bf16[2,48,2048]{2,1,0:T(8,128)(2,1)S(1)}, bf16[2,48,2048]{2,1,0:T(8,128)(2,1)S(1)}, u32[]{:S(2)}, u32[]{:S(2)}) collective-permute-start(bf16[2,48,2048]{2,1,0:T(8,128)(2,1)S(1)} %shard_map.140.refs_0_), channel_id=1, source_target_pairs={{0,8},{4,12},{8,0},{12,4},{16,24},{20,28},{24,16},{28,20},{1,9},{5... | collective-permute-start | bytes 1179656 | tf_op jit(solution)/shard_map/ppermute | solution.py:228
  41.9 10.7 %collective-permute-start.12 = (bf16[48,1024]{1,0:T(8,128)(2,1)S(1)}, bf16[48,1024]{1,0:T(8,128)(2,1)S(1)}, u32[]{:S(2)}, u32[]{:S(2)}) collective-permute-start(bf16[48,1024]{1,0:T(8,128)(2,1)S(1)} %get-tuple-element.137), channel_id=1, source_target_pairs={{0,2},{1,3},{2,0},{3,1},{4,6},{5,7},{6,4},{7,5},{8,10},{9,11},{10,... | collective-permute-start | bytes 294920 | tf_op jit(solution)/shard_map/ppermute | solution.py:228
  44.6 8.0 %collective-permute-start.13 = (bf16[48,1024]{1,0:T(8,128)(2,1)S(1)}, bf16[48,1024]{1,0:T(8,128)(2,1)S(1)}, u32[]{:S(2)}, u32[]{:S(2)}) collective-permute-start(bf16[48,1024]{1,0:T(8,128)(2,1)S(1)} %get-tuple-element.138), channel_id=1, source_target_pairs={{0,3},{1,2},{2,1},{3,0},{4,7},{5,6},{6,5},{7,4},{8,11},{9,10},{10,... | collective-permute-start | bytes 294920 | tf_op jit(solution)/shard_map/ppermute | solution.py:228
  52.8 2.8 %collective-permute-start.18 = (bf16[2,48,2048]{2,1,0:T(8,128)(2,1)S(1)}, bf16[2,48,2048]{2,1,0:T(8,128)(2,1)S(1)}, u32[]{:S(2)}, u32[]{:S(2)}) collective-permute-start(bf16[2,48,2048]{2,1,0:T(8,128)(2,1)S(1)} %shard_map.141.own.refs_3_), channel_id=1, source_target_pairs={{0,4},{4,0},{8,12},{12,8},{16,20},{20,16},{24,28},{28,24},{1,5},{5... | collective-permute-start | bytes 1179656 | tf_op jit(solution)/shard_map/ppermute | solution.py:228
  53.0 2.6 %collective-permute-start.16 = (bf16[2,48,2048]{2,1,0:T(8,128)(2,1)S(1)}, bf16[2,48,2048]{2,1,0:T(8,128)(2,1)S(1)}, u32[]{:S(2)}, u32[]{:S(2)}) collective-permute-start(bf16[2,48,2048]{2,1,0:T(8,128)(2,1)S(1)} %collective-permute-done.9.along_x.refs_1_), channel_id=1, source_target_pairs={{0,4},{4,0},{8,12},{12,8},{16,20},{20,16},{24,28},{28,24},{1,5},{5... | collective-permute-start | bytes 1179656 | tf_op jit(solution)/shard_map/ppermute | solution.py:228
  53.5 2.2 %collective-permute-start.17 = (bf16[2,48,2048]{2,1,0:T(8,128)(2,1)S(1)}, bf16[2,48,2048]{2,1,0:T(8,128)(2,1)S(1)}, u32[]{:S(2)}, u32[]{:S(2)}) collective-permute-start(bf16[2,48,2048]{2,1,0:T(8,128)(2,1)S(1)} %collective-permute-done.10.along_y.refs_2_), channel_id=1, source_target_pairs={{0,4},{4,0},{8,12},{12,8},{16,20},{20,16},{24,28},{28,24},{1,5},{5... | collective-permute-start | bytes 1179656 | tf_op jit(solution)/shard_map/ppermute | solution.py:228
  53.6 15.7 %collective-permute-start.15 = (bf16[3,48,2048]{2,1,0:T(8,128)(2,1)S(1)}, bf16[3,48,2048]{2,1,0:T(8,128)(2,1)S(1)}, u32[]{:S(2)}, u32[]{:S(2)}) collective-permute-start(bf16[3,48,2048]{2,1,0:T(8,128)(2,1)S(1)} %get-tuple-element.141), channel_id=1, source_target_pairs={{0,8},{4,12},{8,0},{12,4},{16,24},{20,28},{24,16},{28,20},{1,9},{5... | collective-permute-start | bytes 1769480 | tf_op jit(solution)/shard_map/ppermute | solution.py:228
  54.1 15.4 %collective-permute-start.19 = (bf16[3,48,2048]{2,1,0:T(8,128)(2,1)S(1)}, bf16[3,48,2048]{2,1,0:T(8,128)(2,1)S(1)}, u32[]{:S(2)}, u32[]{:S(2)}) collective-permute-start(bf16[3,48,2048]{2,1,0:T(8,128)(2,1)S(1)} %get-tuple-element.146), channel_id=1, source_target_pairs={{0,16},{4,20},{8,24},{12,28},{16,0},{20,4},{24,8},{28,12},{1,17},{... | collective-permute-start | bytes 1769480 | tf_op jit(solution)/shard_map/ppermute | solution.py:228
  65.6 4.0 %collective-permute-start.20 = (bf16[2,48,2048]{2,1,0:T(8,128)(2,1)S(1)}, bf16[2,48,2048]{2,1,0:T(8,128)(2,1)S(1)}, u32[]{:S(2)}, u32[]{:S(2)}) collective-permute-start(bf16[2,48,2048]{2,1,0:T(8,128)(2,1)S(1)} %get-tuple-element.149), channel_id=1, source_target_pairs={{0,4},{4,0},{8,12},{12,8},{16,20},{20,16},{24,28},{28,24},{1,5},{5... | collective-permute-start | bytes 1179656 | tf_op jit(solution)/shard_map/ppermute | solution.py:228
  65.8 3.8 %collective-permute-start.21 = (bf16[2,48,2048]{2,1,0:T(8,128)(2,1)S(1)}, bf16[2,48,2048]{2,1,0:T(8,128)(2,1)S(1)}, u32[]{:S(2)}, u32[]{:S(2)}) collective-permute-start(bf16[2,48,2048]{2,1,0:T(8,128)(2,1)S(1)} %get-tuple-element.150), channel_id=1, source_target_pairs={{0,4},{4,0},{8,12},{12,8},{16,20},{20,16},{24,28},{28,24},{1,5},{5... | collective-permute-start | bytes 1179656 | tf_op jit(solution)/shard_map/ppermute | solution.py:228
  66.2 3.4 %collective-permute-start.22 = (bf16[2,48,2048]{2,1,0:T(8,128)(2,1)S(1)}, bf16[2,48,2048]{2,1,0:T(8,128)(2,1)S(1)}, u32[]{:S(2)}, u32[]{:S(2)}) collective-permute-start(bf16[2,48,2048]{2,1,0:T(8,128)(2,1)S(1)} %get-tuple-element.151), channel_id=1, source_target_pairs={{0,4},{4,0},{8,12},{12,8},{16,20},{20,16},{24,28},{28,24},{1,5},{5... | collective-permute-start | bytes 1179656 | tf_op jit(solution)/shard_map/ppermute | solution.py:228
  69.9 2.4 %collective-permute-start.23 = (bf16[2,48,2048]{2,1,0:T(8,128)(2,1)S(1)}, bf16[2,48,2048]{2,1,0:T(8,128)(2,1)S(1)}, u32[]{:S(2)}, u32[]{:S(2)}) collective-permute-start(bf16[2,48,2048]{2,1,0:T(8,128)(2,1)S(1)} %get-tuple-element.152.refs_0_), channel_id=1, source_target_pairs={{0,4},{4,0},{8,12},{12,8},{16,20},{20,16},{24,28},{28,24},{1,5},{5... | collective-permute-start | bytes 1179656 | tf_op jit(solution)/shard_map/ppermute | solution.py:228
  70.0 2.4 %collective-permute-start.24 = (bf16[2,48,2048]{2,1,0:T(8,128)(2,1)S(1)}, bf16[2,48,2048]{2,1,0:T(8,128)(2,1)S(1)}, u32[]{:S(2)}, u32[]{:S(2)}) collective-permute-start(bf16[2,48,2048]{2,1,0:T(8,128)(2,1)S(1)} %get-tuple-element.153.refs_1_), channel_id=1, source_target_pairs={{0,4},{4,0},{8,12},{12,8},{16,20},{20,16},{24,28},{28,24},{1,5},{5... | collective-permute-start | bytes 1179656 | tf_op jit(solution)/shard_map/ppermute | solution.py:228
  70.5 2.3 %collective-permute-start.25 = (bf16[2,48,2048]{2,1,0:T(8,128)(2,1)S(1)}, bf16[2,48,2048]{2,1,0:T(8,128)(2,1)S(1)}, u32[]{:S(2)}, u32[]{:S(2)}) collective-permute-start(bf16[2,48,2048]{2,1,0:T(8,128)(2,1)S(1)} %get-tuple-element.154.refs_2_), channel_id=1, source_target_pairs={{0,4},{4,0},{8,12},{12,8},{16,20},{20,16},{24,28},{28,24},{1,5},{5... | collective-permute-start | bytes 1179656 | tf_op jit(solution)/shard_map/ppermute | solution.py:228
  70.6 11.5 %collective-permute-start.26 = (bf16[2,48,2048]{2,1,0:T(8,128)(2,1)S(1)}, bf16[2,48,2048]{2,1,0:T(8,128)(2,1)S(1)}, u32[]{:S(2)}, u32[]{:S(2)}) collective-permute-start(bf16[2,48,2048]{2,1,0:T(8,128)(2,1)S(1)} %get-tuple-element.156), channel_id=1, source_target_pairs={{0,8},{4,12},{8,0},{12,4},{16,24},{20,28},{24,16},{28,20},{1,9},{5... | collective-permute-start | bytes 1179656 | tf_op jit(solution)/shard_map/ppermute | solution.py:228
  72.1 11.2 %collective-permute-start.27 = (bf16[2,48,2048]{2,1,0:T(8,128)(2,1)S(1)}, bf16[2,48,2048]{2,1,0:T(8,128)(2,1)S(1)}, u32[]{:S(2)}, u32[]{:S(2)}) collective-permute-start(bf16[2,48,2048]{2,1,0:T(8,128)(2,1)S(1)} %get-tuple-element.158), channel_id=1, source_target_pairs={{0,16},{4,20},{8,24},{12,28},{16,0},{20,4},{24,8},{28,12},{1,17},{... | collective-permute-start | bytes 1179656 | tf_op jit(solution)/shard_map/ppermute | solution.py:228
  72.4 11.0 %collective-permute-start.29 = (bf16[2,48,2048]{2,1,0:T(8,128)(2,1)S(1)}, bf16[2,48,2048]{2,1,0:T(8,128)(2,1)S(1)}, u32[]{:S(2)}, u32[]{:S(2)}) collective-permute-start(bf16[2,48,2048]{2,1,0:T(8,128)(2,1)S(1)} %get-tuple-element.164), channel_id=1, source_target_pairs={{0,4},{4,0},{8,12},{12,8},{16,20},{20,16},{24,28},{28,24},{1,5},{5... | collective-permute-start | bytes 1179656 | tf_op jit(solution)/shard_map/ppermute | solution.py:228
  80.5 2.9 %collective-permute-start.28 = (bf16[2,48,2048]{2,1,0:T(8,128)(2,1)S(1)}, bf16[2,48,2048]{2,1,0:T(8,128)(2,1)S(1)}, u32[]{:S(2)}, u32[]{:S(2)}) collective-permute-start(bf16[2,48,2048]{2,1,0:T(8,128)(2,1)S(1)} %get-tuple-element.160), channel_id=1, source_target_pairs={{0,4},{4,0},{8,12},{12,8},{16,20},{20,16},{24,28},{28,24},{1,5},{5... | collective-permute-start | bytes 1179656 | tf_op jit(solution)/shard_map/ppermute | solution.py:228
  80.7 2.7 %collective-permute-start.30 = (bf16[2,48,2048]{2,1,0:T(8,128)(2,1)S(1)}, bf16[2,48,2048]{2,1,0:T(8,128)(2,1)S(1)}, u32[]{:S(2)}, u32[]{:S(2)}) collective-permute-start(bf16[2,48,2048]{2,1,0:T(8,128)(2,1)S(1)} %get-tuple-element.165), channel_id=1, source_target_pairs={{0,4},{4,0},{8,12},{12,8},{16,20},{20,16},{24,28},{28,24},{1,5},{5... | collective-permute-start | bytes 1179656 | tf_op jit(solution)/shard_map/ppermute | solution.py:228
  82.0 1.7 %collective-permute-start.31 = (bf16[2,48,2048]{2,1,0:T(8,128)(2,1)S(1)}, bf16[2,48,2048]{2,1,0:T(8,128)(2,1)S(1)}, u32[]{:S(2)}, u32[]{:S(2)}) collective-permute-start(bf16[2,48,2048]{2,1,0:T(8,128)(2,1)S(1)} %get-tuple-element.166), channel_id=1, source_target_pairs={{0,4},{4,0},{8,12},{12,8},{16,20},{20,16},{24,28},{28,24},{1,5},{5... | collective-permute-start | bytes 1179656 | tf_op jit(solution)/shard_map/ppermute | solution.py:228
  83.3 2.7 %collective-permute-start.34 = (bf16[2,48,2048]{2,1,0:T(8,128)(2,1)S(1)}, bf16[2,48,2048]{2,1,0:T(8,128)(2,1)S(1)}, u32[]{:S(2)}, u32[]{:S(2)}) collective-permute-start(bf16[2,48,2048]{2,1,0:T(8,128)(2,1)S(1)} %shard_map.146.refs_0_), channel_id=1, source_target_pairs={{0,4},{4,0},{8,12},{12,8},{16,20},{20,16},{24,28},{28,24},{1,5},{5... | collective-permute-start | bytes 1179656 | tf_op jit(solution)/shard_map/ppermute | solution.py:228
  84.1 11.2 %collective-permute-start.32 = (bf16[2,48,2048]{2,1,0:T(8,128)(2,1)S(1)}, bf16[2,48,2048]{2,1,0:T(8,128)(2,1)S(1)}, u32[]{:S(2)}, u32[]{:S(2)}) collective-permute-start(bf16[2,48,2048]{2,1,0:T(8,128)(2,1)S(1)} %get-tuple-element.168), channel_id=1, source_target_pairs={{0,8},{4,12},{8,0},{12,4},{16,24},{20,28},{24,16},{28,20},{1,9},{5... | collective-permute-start | bytes 1179656 | tf_op jit(solution)/shard_map/ppermute | solution.py:228
  85.7 10.9 %collective-permute-start.33 = (bf16[2,48,2048]{2,1,0:T(8,128)(2,1)S(1)}, bf16[2,48,2048]{2,1,0:T(8,128)(2,1)S(1)}, u32[]{:S(2)}, u32[]{:S(2)}) collective-permute-start(bf16[2,48,2048]{2,1,0:T(8,128)(2,1)S(1)} %get-tuple-element.169), channel_id=1, source_target_pairs={{0,16},{4,20},{8,24},{12,28},{16,0},{20,4},{24,8},{28,12},{1,17},{... | collective-permute-start | bytes 1179656 | tf_op jit(solution)/shard_map/ppermute | solution.py:228
  90.1 1.5 %collective-permute-start.35 = (bf16[48,2048]{1,0:T(8,128)(2,1)S(1)}, bf16[48,2048]{1,0:T(8,128)(2,1)S(1)}, u32[]{:S(2)}, u32[]{:S(2)}) collective-permute-start(bf16[48,2048]{1,0:T(8,128)(2,1)S(1)} %get-tuple-element.174), channel_id=1, source_target_pairs={{0,4},{4,0},{8,12},{12,8},{16,20},{20,16},{24,28},{28,24},{1,5},{5... | collective-permute-start | bytes 589832 | tf_op jit(solution)/shard_map/ppermute | solution.py:228
  90.2 1.7 %collective-permute-start.36 = (bf16[48,2048]{1,0:T(8,128)(2,1)S(1)}, bf16[48,2048]{1,0:T(8,128)(2,1)S(1)}, u32[]{:S(2)}, u32[]{:S(2)}) collective-permute-start(bf16[48,2048]{1,0:T(8,128)(2,1)S(1)} %get-tuple-element.175), channel_id=1, source_target_pairs={{0,4},{4,0},{8,12},{12,8},{16,20},{20,16},{24,28},{28,24},{1,5},{5... | collective-permute-start | bytes 589832 | tf_op jit(solution)/shard_map/ppermute | solution.py:228
  96.7 10.1 %collective-permute-start.38 = (bf16[2,48,2048]{2,1,0:T(8,128)(2,1)S(1)}, bf16[2,48,2048]{2,1,0:T(8,128)(2,1)S(1)}, u32[]{:S(2)}, u32[]{:S(2)}) collective-permute-start(bf16[2,48,2048]{2,1,0:T(8,128)(2,1)S(1)} %get-tuple-element.177), channel_id=1, source_target_pairs={{0,16},{4,20},{8,24},{12,28},{16,0},{20,4},{24,8},{28,12},{1,17},{... | collective-permute-start | bytes 1179656 | tf_op jit(solution)/shard_map/ppermute | solution.py:228
  97.3 9.9 %collective-permute-start.37 = (bf16[2,48,2048]{2,1,0:T(8,128)(2,1)S(1)}, bf16[2,48,2048]{2,1,0:T(8,128)(2,1)S(1)}, u32[]{:S(2)}, u32[]{:S(2)}) collective-permute-start(bf16[2,48,2048]{2,1,0:T(8,128)(2,1)S(1)} %get-tuple-element.176), channel_id=1, source_target_pairs={{0,8},{4,12},{8,0},{12,4},{16,24},{20,28},{24,16},{28,20},{1,9},{5... | collective-permute-start | bytes 1179656 | tf_op jit(solution)/shard_map/ppermute | solution.py:228
  107.3 6.7 %collective-permute-start.40 = (bf16[48,2048]{1,0:T(8,128)(2,1)S(1)}, bf16[48,2048]{1,0:T(8,128)(2,1)S(1)}, u32[]{:S(2)}, u32[]{:S(2)}) collective-permute-start(bf16[48,2048]{1,0:T(8,128)(2,1)S(1)} %get-tuple-element.184), channel_id=1, source_target_pairs={{0,16},{4,20},{8,24},{12,28},{16,0},{20,4},{24,8},{28,12},{1,17},{... | collective-permute-start | bytes 589832 | tf_op jit(solution)/shard_map/ppermute | solution.py:228
  108.7 5.7 %collective-permute-start.39 = (bf16[48,2048]{1,0:T(8,128)(2,1)S(1)}, bf16[48,2048]{1,0:T(8,128)(2,1)S(1)}, u32[]{:S(2)}, u32[]{:S(2)}) collective-permute-start(bf16[48,2048]{1,0:T(8,128)(2,1)S(1)} %get-tuple-element.183), channel_id=1, source_target_pairs={{0,8},{4,12},{8,0},{12,4},{16,24},{20,28},{24,16},{28,20},{1,9},{5... | collective-permute-start | bytes 589832 | tf_op jit(solution)/shard_map/ppermute | solution.py:228
  109.6 8.3 %collective-permute-start.44 = (bf16[48,1024]{1,0:T(8,128)(2,1)S(1)}, bf16[48,1024]{1,0:T(8,128)(2,1)S(1)}, u32[]{:S(2)}, u32[]{:S(2)}) collective-permute-start(bf16[48,1024]{1,0:T(8,128)(2,1)S(1)} %get-tuple-element.193), channel_id=1, source_target_pairs={{0,1},{1,0},{2,3},{3,2},{4,5},{5,4},{6,7},{7,6},{8,9},{9,8},{10,11... | collective-permute-start | bytes 294920 | tf_op jit(solution)/shard_map/ppermute | solution.py:228
  111.4 10.8 %collective-permute-start.45 = (bf16[48,1024]{1,0:T(8,128)(2,1)S(1)}, bf16[48,1024]{1,0:T(8,128)(2,1)S(1)}, u32[]{:S(2)}, u32[]{:S(2)}) collective-permute-start(bf16[48,1024]{1,0:T(8,128)(2,1)S(1)} %get-tuple-element.194), channel_id=1, source_target_pairs={{0,2},{1,3},{2,0},{3,1},{4,6},{5,7},{6,4},{7,5},{8,10},{9,11},{10,... | collective-permute-start | bytes 294920 | tf_op jit(solution)/shard_map/ppermute | solution.py:228
  112.8 9.4 %collective-permute-start.46 = (bf16[48,1024]{1,0:T(8,128)(2,1)S(1)}, bf16[48,1024]{1,0:T(8,128)(2,1)S(1)}, u32[]{:S(2)}, u32[]{:S(2)}) collective-permute-start(bf16[48,1024]{1,0:T(8,128)(2,1)S(1)} %get-tuple-element.195), channel_id=1, source_target_pairs={{0,3},{1,2},{2,1},{3,0},{4,7},{5,6},{6,5},{7,4},{8,11},{9,10},{10,... | collective-permute-start | bytes 294920 | tf_op jit(solution)/shard_map/ppermute | solution.py:228
  114.7 7.9 %collective-permute-start.41 = (bf16[48,1024]{1,0:T(8,128)(2,1)S(1)}, bf16[48,1024]{1,0:T(8,128)(2,1)S(1)}, u32[]{:S(2)}, u32[]{:S(2)}) collective-permute-start(bf16[48,1024]{1,0:T(8,128)(2,1)S(1)} %get-tuple-element.186), channel_id=1, source_target_pairs={{0,1},{1,0},{2,3},{3,2},{4,5},{5,4},{6,7},{7,6},{8,9},{9,8},{10,11... | collective-permute-start | bytes 294920 | tf_op jit(solution)/shard_map/ppermute | solution.py:228
  116.5 11.3 %collective-permute-start.42 = (bf16[48,1024]{1,0:T(8,128)(2,1)S(1)}, bf16[48,1024]{1,0:T(8,128)(2,1)S(1)}, u32[]{:S(2)}, u32[]{:S(2)}) collective-permute-start(bf16[48,1024]{1,0:T(8,128)(2,1)S(1)} %get-tuple-element.187), channel_id=1, source_target_pairs={{0,2},{1,3},{2,0},{3,1},{4,6},{5,7},{6,4},{7,5},{8,10},{9,11},{10,... | collective-permute-start | bytes 294920 | tf_op jit(solution)/shard_map/ppermute | solution.py:228
  117.9 9.8 %collective-permute-start.43 = (bf16[48,1024]{1,0:T(8,128)(2,1)S(1)}, bf16[48,1024]{1,0:T(8,128)(2,1)S(1)}, u32[]{:S(2)}, u32[]{:S(2)}) collective-permute-start(bf16[48,1024]{1,0:T(8,128)(2,1)S(1)} %get-tuple-element.188), channel_id=1, source_target_pairs={{0,3},{1,2},{2,1},{3,0},{4,7},{5,6},{6,5},{7,4},{8,11},{9,10},{10,... | collective-permute-start | bytes 294920 | tf_op jit(solution)/shard_map/ppermute | solution.py:228

commit v5 on v4

--- a/solution.py
+++ b/solution.py
@@ -660,7 +660,7 @@
         core, shared, prefix, received, inner, grow, c, sending
     )
     down = load(after(down_weight[0], picked[0]), 1)
-    masks = (2, 3, 1)
+    masks = (3, 2, 1)
 
     def to_experts(chunk):
         parts = picked[chunk * experts : (chunk + 1) * experts]

time: 129 us -> 129 us (level)
  no operation moved by 1% of the time
where the time goes in v5:
time: 129 us
  starting transfers between devices  45.1 us (35%)
  waiting for transfers between devices  41.6 us (32%)
  Pallas kernels  40.4 us (31%)
    ppermute x43, waiting for transfers between devices, swap(): return lax.ppermute(x, axis, [(i, i ^ mask) for i in range(size)])  39.1 us
    ppermute x43, starting transfers between devices, swap(): return lax.ppermute(x, axis, [(i, i ^ mask) for i in range(size)])  38.9 us
    pallas_call x22, Pallas kernels, run(): pl.pallas_call(body, out_shape=outs, in_specs=specs, out_specs=jax.tree.m...  29 us
    pallas_call x2, Pallas kernels, load(): pl.pallas_call(load_kernel, out_shape=pltpu.VMEM(source.shape, source.dty...  9.17 us
    ppermute x3, starting transfers between devices, directed(): return lax.ppermute(x, 'ctx', route)  3.88 us
  transfers between devices with their start and end apart: 47, of which 21 were waited for; matrix products, arithmetic and copies ran while one was open for 0% of the time, Pallas kernels for 29%

profile of v5, /device:TPU:0, one launch (start us, length us, event | category | flops | bytes accessed | tf_op | source)
XLA Modules:
  0.0 128.7 jit_solution(12424003850090460555)
XLA Ops:
  0.6 0.7 slice.3
  1.4 2.3 %collective-permute-start = (bf16[8,1024]{1,0:T(8,128)(2,1)S(1)}, bf16[8,1024]{1,0:T(8,128)(2,1)S(1)}, u32[]{:S(2)}, u32[]{:S(2)}) collective-permute-start(bf16[8,1024]{1,0:T(8,128)(2,1)S(1)} %slice.3), channel_id=1, source_target_pairs={{0,4},{4,8},{8,12},{12,16},{16,20},{20,24},{24,28},{1,5},{5,9},{9,... | collective-permute-start | bytes 49160 | tf_op jit(solution)/shard_map/ppermute | solution.py:19
  3.7 2.2 %shard_map.131 = (f32[16,128]{1,0:T(8,128)S(1)}, bf16[128,128]{1,0:T(8,128)(2,1)S(1)}, bf16[128,1024]{1,0:T(8,128)(2,1)S(1)}, bf16[128,128]{1,0:T(8,128)(2,1)S(1...) custom-call(f32[16,128]{1,0:T(8,128)} %refs_0_, ...), custom_call_target="tpu_custom_call" | custom-call | flops 1 | bytes 1 | tf_op jit(solution)/shard_map/pallas_call | solution.py:624
  6.6 2.7 %collective-permute-start.1 = (bf16[136,1024]{1,0:T(8,128)(2,1)S(1)}, bf16[136,1024]{1,0:T(8,128)(2,1)S(1)}, u32[]{:S(2)}, u32[]{:S(2)}) collective-permute-start(bf16[136,1024]{1,0:T(8,128)(2,1)S(1)} %get-tuple-element.111), channel_id=1, source_target_pairs={{0,4},{4,0},{8,12},{12,8},{16,20},{20,16},{24,28},{28,24},{1,5},{5... | collective-permute-start | bytes 835592 | tf_op jit(solution)/shard_map/ppermute | solution.py:228
  9.3 1.2 collective-permute-done.1.received
  10.5 1.3 %collective-permute-start.4 = (bf16[136,1024]{1,0:T(8,128)(2,1)S(1)}, bf16[136,1024]{1,0:T(8,128)(2,1)S(1)}, u32[]{:S(2)}, u32[]{:S(2)}) collective-permute-start(bf16[136,1024]{1,0:T(8,128)(2,1)S(1)} %shard_map.133), channel_id=1, source_target_pairs={{4,28},{12,20},{16,8},{24,0},{5,29},{13,21},{17,9},{25,1},{6,30},{... | collective-permute-start | bytes 835592 | tf_op jit(solution)/shard_map/ppermute | solution.py:576
  11.8 1.3 %collective-permute-start.3 = (bf16[136,1024]{1,0:T(8,128)(2,1)S(1)}, bf16[136,1024]{1,0:T(8,128)(2,1)S(1)}, u32[]{:S(2)}, u32[]{:S(2)}) collective-permute-start(bf16[136,1024]{1,0:T(8,128)(2,1)S(1)} %shard_map.133), channel_id=1, source_target_pairs={{4,20},{12,28},{16,0},{24,8},{5,21},{13,29},{17,1},{25,9},{6,22},{... | collective-permute-start | bytes 835592 | tf_op jit(solution)/shard_map/ppermute | solution.py:576
  13.1 1.3 %collective-permute-start.2 = (bf16[136,1024]{1,0:T(8,128)(2,1)S(1)}, bf16[136,1024]{1,0:T(8,128)(2,1)S(1)}, u32[]{:S(2)}, u32[]{:S(2)}) collective-permute-start(bf16[136,1024]{1,0:T(8,128)(2,1)S(1)} %shard_map.133), channel_id=1, source_target_pairs={{4,12},{8,0},{20,28},{24,16},{5,13},{9,1},{21,29},{25,17},{6,14},{... | collective-permute-start | bytes 835592 | tf_op jit(solution)/shard_map/ppermute | solution.py:576
  14.4 4.6 %shard_map.134.refs_8_.refs_6_.refs_2_ = bf16[4096,1536]{1,0:T(8,128)(2,1)S(1)} custom-call(bf16[4096,1536]{1,0:T(8,128)(2,1)} %bitcast.9), custom_call_target="tpu_custom_call" | custom-call | flops 1 | bytes 1 | tf_op jit(solution)/shard_map/pallas_call | solution.py:298
  19.0 1.1 shard_map.135
  20.4 2.5 %collective-permute-done.3.middle = bf16[136,1024]{1,0:T(8,128)(2,1)S(1)} collective-permute-done((bf16[136,1024]{1,0:T(8,128)(2,1)S(1)}, bf16[136,1024]{1,0:T(8,128)(2,1)S(1)}, u32[]{:S(2)}, u32[]{:S(2)}) %collective-permute-start.3) | collective-permute-done | bytes 278560 | tf_op jit(solution)/shard_map/ppermute | solution.py:576
  23.0 2.1 %collective-permute-start.5 = (bf16[128,1024]{1,0:T(8,128)(2,1)S(1)}, bf16[128,1024]{1,0:T(8,128)(2,1)S(1)}, u32[]{:S(2)}, u32[]{:S(2)}) collective-permute-start(bf16[128,1024]{1,0:T(8,128)(2,1)S(1)} %shard_map.137.prefix), channel_id=1, source_target_pairs={{0,4},{4,0},{8,12},{12,8},{16,20},{20,16},{24,28},{28,24},{1,5},{5... | collective-permute-start | bytes 786440 | tf_op jit(solution)/shard_map/ppermute | solution.py:228
  25.1 1.2 collective-permute-done.5.shared
  27.0 1.7 %collective-permute-start.6 = (bf16[48,1024]{1,0:T(8,128)(2,1)S(1)}, bf16[48,1024]{1,0:T(8,128)(2,1)S(1)}, u32[]{:S(2)}, u32[]{:S(2)}) collective-permute-start(bf16[48,1024]{1,0:T(8,128)(2,1)S(1)} %get-tuple-element.132), channel_id=1, source_target_pairs={{0,1},{1,0},{2,3},{3,2},{4,5},{5,4},{6,7},{7,6},{8,9},{9,8},{10,11... | collective-permute-start | bytes 294920 | tf_op jit(solution)/shard_map/ppermute | solution.py:228
  28.6 2.6 %collective-permute-start.7 = (bf16[48,1024]{1,0:T(8,128)(2,1)S(1)}, bf16[48,1024]{1,0:T(8,128)(2,1)S(1)}, u32[]{:S(2)}, u32[]{:S(2)}) collective-permute-start(bf16[48,1024]{1,0:T(8,128)(2,1)S(1)} %get-tuple-element.133), channel_id=1, source_target_pairs={{0,2},{1,3},{2,0},{3,1},{4,6},{5,7},{6,4},{7,5},{8,10},{9,11},{10,... | collective-permute-start | bytes 294920 | tf_op jit(solution)/shard_map/ppermute | solution.py:228
  31.4 0.7 collective-permute-start.11
  32.1 4.6 %shard_map.139.refs_9_.refs_7_.refs_3_ = bf16[1536,4096]{1,0:T(8,128)(2,1)S(1)} custom-call(bf16[1536,4096]{1,0:T(8,128)(2,1)} %bitcast.10), custom_call_target="tpu_custom_call" | custom-call | flops 1 | bytes 1 | tf_op jit(solution)/shard_map/pallas_call | solution.py:298
  36.7 2.6 %collective-permute-done.7.refs_2_ = bf16[48,1024]{1,0:T(8,128)(2,1)S(1)} collective-permute-done((bf16[48,1024]{1,0:T(8,128)(2,1)S(1)}, bf16[48,1024]{1,0:T(8,128)(2,1)S(1)}, u32[]{:S(2)}, u32[]{:S(2)}) %collective-permute-start.7) | collective-permute-done | bytes 98336 | tf_op jit(solution)/shard_map/ppermute | solution.py:228
  39.7 0.7 collective-permute-start.10
  40.4 1.5 %collective-permute-start.9 = (bf16[2,48,2048]{2,1,0:T(8,128)(2,1)S(1)}, bf16[2,48,2048]{2,1,0:T(8,128)(2,1)S(1)}, u32[]{:S(2)}, u32[]{:S(2)}) collective-permute-start(bf16[2,48,2048]{2,1,0:T(8,128)(2,1)S(1)} %shard_map.140.refs_0_), channel_id=1, source_target_pairs={{0,8},{4,12},{8,0},{12,4},{16,24},{20,28},{24,16},{28,20},{1,9},{5... | collective-permute-start | bytes 1179656 | tf_op jit(solution)/shard_map/ppermute | solution.py:228
  41.9 2.7 %collective-permute-start.12 = (bf16[48,1024]{1,0:T(8,128)(2,1)S(1)}, bf16[48,1024]{1,0:T(8,128)(2,1)S(1)}, u32[]{:S(2)}, u32[]{:S(2)}) collective-permute-start(bf16[48,1024]{1,0:T(8,128)(2,1)S(1)} %get-tuple-element.137), channel_id=1, source_target_pairs={{0,2},{1,3},{2,0},{3,1},{4,6},{5,7},{6,4},{7,5},{8,10},{9,11},{10,... | collective-permute-start | bytes 294920 | tf_op jit(solution)/shard_map/ppermute | solution.py:228
  44.6 1.4 %collective-permute-start.13 = (bf16[48,1024]{1,0:T(8,128)(2,1)S(1)}, bf16[48,1024]{1,0:T(8,128)(2,1)S(1)}, u32[]{:S(2)}, u32[]{:S(2)}) collective-permute-start(bf16[48,1024]{1,0:T(8,128)(2,1)S(1)} %get-tuple-element.138), channel_id=1, source_target_pairs={{0,3},{1,2},{2,1},{3,0},{4,7},{5,6},{6,5},{7,4},{8,11},{9,10},{10,... | collective-permute-start | bytes 294920 | tf_op jit(solution)/shard_map/ppermute | solution.py:228
  45.9 6.6 %collective-permute-done.12.refs_2_ = bf16[48,1024]{1,0:T(8,128)(2,1)S(1)} collective-permute-done((bf16[48,1024]{1,0:T(8,128)(2,1)S(1)}, bf16[48,1024]{1,0:T(8,128)(2,1)S(1)}, u32[]{:S(2)}, u32[]{:S(2)}) %collective-permute-start.12) | collective-permute-done | bytes 98336 | tf_op jit(solution)/shard_map/ppermute | solution.py:228
  54.1 1.4 %collective-permute-start.19 = (bf16[3,48,2048]{2,1,0:T(8,128)(2,1)S(1)}, bf16[3,48,2048]{2,1,0:T(8,128)(2,1)S(1)}, u32[]{:S(2)}, u32[]{:S(2)}) collective-permute-start(bf16[3,48,2048]{2,1,0:T(8,128)(2,1)S(1)} %get-tuple-element.146), channel_id=1, source_target_pairs={{0,16},{4,20},{8,24},{12,28},{16,0},{20,4},{24,8},{28,12},{1,17},{... | collective-permute-start | bytes 1769480 | tf_op jit(solution)/shard_map/ppermute | solution.py:228
  55.7 9.9 %shard_map.143 = (bf16[2,48,2048]{2,1,0:T(8,128)(2,1)S(1)}, bf16[2,48,2048]{2,1,0:T(8,128)(2,1)S(1)}, bf16[2,48,2048]{2,1,0:T(8,128)(2,1)S(1)}, bf16[2,48,2048]{...) custom-call(bf16[2,48,2048]{2,1,0:T(8,128)(2,1)S(1)} %shard_map.140., ...), custom_call_target="tpu_custom_call" | custom-call | flops 1 | bytes 1 | tf_op jit(solution)/shard_map/pallas_call | solution.py:213
  66.3 3.0 %collective-permute-done.15.from_x = bf16[3,48,2048]{2,1,0:T(8,128)(2,1)S(1)} collective-permute-done((bf16[3,48,2048]{2,1,0:T(8,128)(2,1)S(1)}, bf16[3,48,2048]{2,1,0:T(8,128)(2,1)S(1)}, u32[]{:S(2)}, u32[]{:S(2)}) %collective-permute-start.15) | collective-permute-done | bytes 589856 | tf_op jit(solution)/shard_map/ppermute | solution.py:228
  70.6 1.5 %collective-permute-start.26 = (bf16[2,48,2048]{2,1,0:T(8,128)(2,1)S(1)}, bf16[2,48,2048]{2,1,0:T(8,128)(2,1)S(1)}, u32[]{:S(2)}, u32[]{:S(2)}) collective-permute-start(bf16[2,48,2048]{2,1,0:T(8,128)(2,1)S(1)} %get-tuple-element.156), channel_id=1, source_target_pairs={{0,8},{4,12},{8,0},{12,4},{16,24},{20,28},{24,16},{28,20},{1,9},{5... | collective-permute-start | bytes 1179656 | tf_op jit(solution)/shard_map/ppermute | solution.py:228
  72.8 7.7 %shard_map.145 = (bf16[2,48,2048]{2,1,0:T(8,128)(2,1)S(1)}, bf16[2,48,2048]{2,1,0:T(8,128)(2,1)S(1)}, bf16[2,48,2048]{2,1,0:T(8,128)(2,1)S(1)}, bf16[2,48,2048]{...) custom-call(bf16[2,48,2048]{2,1,0:T(8,128)(2,1)S(1)} %get-tuple-element.152.refs_0_, ...), custom_call_target="tpu_custom_call" | custom-call | flops 1 | bytes 1 | tf_op jit(solution)/shard_map/pallas_call | solution.py:213
  81.1 1.0 collective-permute-done.26.from_x.refs_2_
  82.0 1.2 collective-permute-done.27.from_y.refs_3_
  84.1 1.6 %collective-permute-start.32 = (bf16[2,48,2048]{2,1,0:T(8,128)(2,1)S(1)}, bf16[2,48,2048]{2,1,0:T(8,128)(2,1)S(1)}, u32[]{:S(2)}, u32[]{:S(2)}) collective-permute-start(bf16[2,48,2048]{2,1,0:T(8,128)(2,1)S(1)} %get-tuple-element.168), channel_id=1, source_target_pairs={{0,8},{4,12},{8,0},{12,4},{16,24},{20,28},{24,16},{28,20},{1,9},{5... | collective-permute-start | bytes 1179656 | tf_op jit(solution)/shard_map/ppermute | solution.py:228
  86.0 4.1 %shard_map.148 = (bf16[48,2048]{1,0:T(8,128)(2,1)S(1)}, bf16[48,2048]{1,0:T(8,128)(2,1)S(1)}, bf16[2,48,2048]{2,1,0:T(8,128)(2,1)S(1)}) custom-call(bf16[2,48,2048]{2,1,0:T(8,128)(2,1)S(1)} %shard_map.146.refs_0_, bf16[2,48,2048]{2,1,0:T(8,128)(2,1)S(1)} %collective-permute-done.34.refs_1_, bf16[4096,1536]{1,0:T(8,128)(2,1)S(1)} %shard_map.134.refs_8_.refs_6_.refs_2_, ...), custom_call_target="tpu_custom_call" | custom-call | flops 1 | bytes 1 | tf_op jit(solution)/shard_map/pallas_call | solution.py:213
  90.7 0.9 collective-permute-done.35.first_half
  91.9 3.5 %collective-permute-done.32.from_x.refs_2_ = bf16[2,48,2048]{2,1,0:T(8,128)(2,1)S(1)} collective-permute-done((bf16[2,48,2048]{2,1,0:T(8,128)(2,1)S(1)}, bf16[2,48,2048]{2,1,0:T(8,128)(2,1)S(1)}, u32[]{:S(2)}, u32[]{:S(2)}) %collective-permute-start.32) | collective-permute-done | bytes 393248 | tf_op jit(solution)/shard_map/ppermute | solution.py:228
  95.4 1.2 collective-permute-done.33.from_y.refs_3_
  97.3 1.5 %collective-permute-start.37 = (bf16[2,48,2048]{2,1,0:T(8,128)(2,1)S(1)}, bf16[2,48,2048]{2,1,0:T(8,128)(2,1)S(1)}, u32[]{:S(2)}, u32[]{:S(2)}) collective-permute-start(bf16[2,48,2048]{2,1,0:T(8,128)(2,1)S(1)} %get-tuple-element.176), channel_id=1, source_target_pairs={{0,8},{4,12},{8,0},{12,4},{16,24},{20,28},{24,16},{28,20},{1,9},{5... | collective-permute-start | bytes 1179656 | tf_op jit(solution)/shard_map/ppermute | solution.py:228
  98.8 1.1 shard_map.150
  99.9 6.9 %collective-permute-done.38.from_y.refs_5_ = bf16[2,48,2048]{2,1,0:T(8,128)(2,1)S(1)} collective-permute-done((bf16[2,48,2048]{2,1,0:T(8,128)(2,1)S(1)}, bf16[2,48,2048]{2,1,0:T(8,128)(2,1)S(1)}, u32[]{:S(2)}, u32[]{:S(2)}) %collective-permute-start.38) | collective-permute-done | bytes 393248 | tf_op jit(solution)/shard_map/ppermute | solution.py:228
  107.3 1.4 %collective-permute-start.40 = (bf16[48,2048]{1,0:T(8,128)(2,1)S(1)}, bf16[48,2048]{1,0:T(8,128)(2,1)S(1)}, u32[]{:S(2)}, u32[]{:S(2)}) collective-permute-start(bf16[48,2048]{1,0:T(8,128)(2,1)S(1)} %get-tuple-element.184), channel_id=1, source_target_pairs={{0,16},{4,20},{8,24},{12,28},{16,0},{20,4},{24,8},{28,12},{1,17},{... | collective-permute-start | bytes 589832 | tf_op jit(solution)/shard_map/ppermute | solution.py:228
  109.6 1.8 %collective-permute-start.44 = (bf16[48,1024]{1,0:T(8,128)(2,1)S(1)}, bf16[48,1024]{1,0:T(8,128)(2,1)S(1)}, u32[]{:S(2)}, u32[]{:S(2)}) collective-permute-start(bf16[48,1024]{1,0:T(8,128)(2,1)S(1)} %get-tuple-element.193), channel_id=1, source_target_pairs={{0,1},{1,0},{2,3},{3,2},{4,5},{5,4},{6,7},{7,6},{8,9},{9,8},{10,11... | collective-permute-start | bytes 294920 | tf_op jit(solution)/shard_map/ppermute | solution.py:228
  111.4 1.4 %collective-permute-start.45 = (bf16[48,1024]{1,0:T(8,128)(2,1)S(1)}, bf16[48,1024]{1,0:T(8,128)(2,1)S(1)}, u32[]{:S(2)}, u32[]{:S(2)}) collective-permute-start(bf16[48,1024]{1,0:T(8,128)(2,1)S(1)} %get-tuple-element.194), channel_id=1, source_target_pairs={{0,2},{1,3},{2,0},{3,1},{4,6},{5,7},{6,4},{7,5},{8,10},{9,11},{10,... | collective-permute-start | bytes 294920 | tf_op jit(solution)/shard_map/ppermute | solution.py:228
  112.8 1.2 collective-permute-start.46
  114.7 1.8 %collective-permute-start.41 = (bf16[48,1024]{1,0:T(8,128)(2,1)S(1)}, bf16[48,1024]{1,0:T(8,128)(2,1)S(1)}, u32[]{:S(2)}, u32[]{:S(2)}) collective-permute-start(bf16[48,1024]{1,0:T(8,128)(2,1)S(1)} %get-tuple-element.186), channel_id=1, source_target_pairs={{0,1},{1,0},{2,3},{3,2},{4,5},{5,4},{6,7},{7,6},{8,9},{9,8},{10,11... | collective-permute-start | bytes 294920 | tf_op jit(solution)/shard_map/ppermute | solution.py:228
  116.5 1.4 %collective-permute-start.42 = (bf16[48,1024]{1,0:T(8,128)(2,1)S(1)}, bf16[48,1024]{1,0:T(8,128)(2,1)S(1)}, u32[]{:S(2)}, u32[]{:S(2)}) collective-permute-start(bf16[48,1024]{1,0:T(8,128)(2,1)S(1)} %get-tuple-element.187), channel_id=1, source_target_pairs={{0,2},{1,3},{2,0},{3,1},{4,6},{5,7},{6,4},{7,5},{8,10},{9,11},{10,... | collective-permute-start | bytes 294920 | tf_op jit(solution)/shard_map/ppermute | solution.py:228
  117.9 2.1 %collective-permute-start.43 = (bf16[48,1024]{1,0:T(8,128)(2,1)S(1)}, bf16[48,1024]{1,0:T(8,128)(2,1)S(1)}, u32[]{:S(2)}, u32[]{:S(2)}) collective-permute-start(bf16[48,1024]{1,0:T(8,128)(2,1)S(1)} %get-tuple-element.188), channel_id=1, source_target_pairs={{0,3},{1,2},{2,1},{3,0},{4,7},{5,6},{6,5},{7,4},{8,11},{9,10},{10,... | collective-permute-start | bytes 294920 | tf_op jit(solution)/shard_map/ppermute | solution.py:228
  120.0 2.3 %collective-permute-done.45.refs_4_ = bf16[48,1024]{1,0:T(8,128)(2,1)S(1)} collective-permute-done((bf16[48,1024]{1,0:T(8,128)(2,1)S(1)}, bf16[48,1024]{1,0:T(8,128)(2,1)S(1)}, u32[]{:S(2)}, u32[]{:S(2)}) %collective-permute-start.45) | collective-permute-done | bytes 98336 | tf_op jit(solution)/shard_map/ppermute | solution.py:228
  122.5 5.2 %collective-permute-done.42.refs_4_ = bf16[48,1024]{1,0:T(8,128)(2,1)S(1)} collective-permute-done((bf16[48,1024]{1,0:T(8,128)(2,1)S(1)}, bf16[48,1024]{1,0:T(8,128)(2,1)S(1)}, u32[]{:S(2)}, u32[]{:S(2)}) %collective-permute-start.42) | collective-permute-done | bytes 98336 | tf_op jit(solution)/shard_map/ppermute | solution.py:228
  127.8 1.0 shard_map.155
  (72 shorter events, 12.4 us)
Async XLA Ops:
  1.4 4.5 %collective-permute-start = (bf16[8,1024]{1,0:T(8,128)(2,1)S(1)}, bf16[8,1024]{1,0:T(8,128)(2,1)S(1)}, u32[]{:S(2)}, u32[]{:S(2)}) collective-permute-start(bf16[8,1024]{1,0:T(8,128)(2,1)S(1)} %slice.3), channel_id=1, source_target_pairs={{0,4},{4,8},{8,12},{12,16},{16,20},{20,24},{24,28},{1,5},{5,9},{9,... | collective-permute-start | bytes 49160 | tf_op jit(solution)/shard_map/ppermute | solution.py:19
  6.6 3.9 %collective-permute-start.1 = (bf16[136,1024]{1,0:T(8,128)(2,1)S(1)}, bf16[136,1024]{1,0:T(8,128)(2,1)S(1)}, u32[]{:S(2)}, u32[]{:S(2)}) collective-permute-start(bf16[136,1024]{1,0:T(8,128)(2,1)S(1)} %get-tuple-element.111), channel_id=1, source_target_pairs={{0,4},{4,0},{8,12},{12,8},{16,20},{20,16},{24,28},{28,24},{1,5},{5... | collective-permute-start | bytes 835592 | tf_op jit(solution)/shard_map/ppermute | solution.py:228
  10.5 9.8 %collective-permute-start.4 = (bf16[136,1024]{1,0:T(8,128)(2,1)S(1)}, bf16[136,1024]{1,0:T(8,128)(2,1)S(1)}, u32[]{:S(2)}, u32[]{:S(2)}) collective-permute-start(bf16[136,1024]{1,0:T(8,128)(2,1)S(1)} %shard_map.133), channel_id=1, source_target_pairs={{4,28},{12,20},{16,8},{24,0},{5,29},{13,21},{17,9},{25,1},{6,30},{... | collective-permute-start | bytes 835592 | tf_op jit(solution)/shard_map/ppermute | solution.py:576
  11.8 11.0 %collective-permute-start.3 = (bf16[136,1024]{1,0:T(8,128)(2,1)S(1)}, bf16[136,1024]{1,0:T(8,128)(2,1)S(1)}, u32[]{:S(2)}, u32[]{:S(2)}) collective-permute-start(bf16[136,1024]{1,0:T(8,128)(2,1)S(1)} %shard_map.133), channel_id=1, source_target_pairs={{4,20},{12,28},{16,0},{24,8},{5,21},{13,29},{17,1},{25,9},{6,22},{... | collective-permute-start | bytes 835592 | tf_op jit(solution)/shard_map/ppermute | solution.py:576
  13.1 9.7 %collective-permute-start.2 = (bf16[136,1024]{1,0:T(8,128)(2,1)S(1)}, bf16[136,1024]{1,0:T(8,128)(2,1)S(1)}, u32[]{:S(2)}, u32[]{:S(2)}) collective-permute-start(bf16[136,1024]{1,0:T(8,128)(2,1)S(1)} %shard_map.133), channel_id=1, source_target_pairs={{4,12},{8,0},{20,28},{24,16},{5,13},{9,1},{21,29},{25,17},{6,14},{... | collective-permute-start | bytes 835592 | tf_op jit(solution)/shard_map/ppermute | solution.py:576
  23.0 3.2 %collective-permute-start.5 = (bf16[128,1024]{1,0:T(8,128)(2,1)S(1)}, bf16[128,1024]{1,0:T(8,128)(2,1)S(1)}, u32[]{:S(2)}, u32[]{:S(2)}) collective-permute-start(bf16[128,1024]{1,0:T(8,128)(2,1)S(1)} %shard_map.137.prefix), channel_id=1, source_target_pairs={{0,4},{4,0},{8,12},{12,8},{16,20},{20,16},{24,28},{28,24},{1,5},{5... | collective-permute-start | bytes 786440 | tf_op jit(solution)/shard_map/ppermute | solution.py:228
  27.0 9.7 %collective-permute-start.6 = (bf16[48,1024]{1,0:T(8,128)(2,1)S(1)}, bf16[48,1024]{1,0:T(8,128)(2,1)S(1)}, u32[]{:S(2)}, u32[]{:S(2)}) collective-permute-start(bf16[48,1024]{1,0:T(8,128)(2,1)S(1)} %get-tuple-element.132), channel_id=1, source_target_pairs={{0,1},{1,0},{2,3},{3,2},{4,5},{5,4},{6,7},{7,6},{8,9},{9,8},{10,11... | collective-permute-start | bytes 294920 | tf_op jit(solution)/shard_map/ppermute | solution.py:228
  28.6 10.7 %collective-permute-start.7 = (bf16[48,1024]{1,0:T(8,128)(2,1)S(1)}, bf16[48,1024]{1,0:T(8,128)(2,1)S(1)}, u32[]{:S(2)}, u32[]{:S(2)}) collective-permute-start(bf16[48,1024]{1,0:T(8,128)(2,1)S(1)} %get-tuple-element.133), channel_id=1, source_target_pairs={{0,2},{1,3},{2,0},{3,1},{4,6},{5,7},{6,4},{7,5},{8,10},{9,11},{10,... | collective-permute-start | bytes 294920 | tf_op jit(solution)/shard_map/ppermute | solution.py:228
  31.2 8.1 %collective-permute-start.8 = (bf16[48,1024]{1,0:T(8,128)(2,1)S(1)}, bf16[48,1024]{1,0:T(8,128)(2,1)S(1)}, u32[]{:S(2)}, u32[]{:S(2)}) collective-permute-start(bf16[48,1024]{1,0:T(8,128)(2,1)S(1)} %get-tuple-element.134), channel_id=1, source_target_pairs={{0,3},{1,2},{2,1},{3,0},{4,7},{5,6},{6,5},{7,4},{8,11},{9,10},{10,... | collective-permute-start | bytes 294920 | tf_op jit(solution)/shard_map/ppermute | solution.py:228
  31.4 8.1 %collective-permute-start.11 = (bf16[48,1024]{1,0:T(8,128)(2,1)S(1)}, bf16[48,1024]{1,0:T(8,128)(2,1)S(1)}, u32[]{:S(2)}, u32[]{:S(2)}) collective-permute-start(bf16[48,1024]{1,0:T(8,128)(2,1)S(1)} %get-tuple-element.136), channel_id=1, source_target_pairs={{0,1},{1,0},{2,3},{3,2},{4,5},{5,4},{6,7},{7,6},{8,9},{9,8},{10,11... | collective-permute-start | bytes 294920 | tf_op jit(solution)/shard_map/ppermute | solution.py:228
  39.6 13.3 %collective-permute-start.14 = (bf16[2,48,2048]{2,1,0:T(8,128)(2,1)S(1)}, bf16[2,48,2048]{2,1,0:T(8,128)(2,1)S(1)}, u32[]{:S(2)}, u32[]{:S(2)}) collective-permute-start(bf16[2,48,2048]{2,1,0:T(8,128)(2,1)S(1)} %shard_map.140.refs_0_), channel_id=1, source_target_pairs={{0,4},{4,0},{8,12},{12,8},{16,20},{20,16},{24,28},{28,24},{1,5},{5... | collective-permute-start | bytes 1179656 | tf_op jit(solution)/shard_map/ppermute | solution.py:228
  39.7 13.2 %collective-permute-start.10 = (bf16[2,48,2048]{2,1,0:T(8,128)(2,1)S(1)}, bf16[2,48,2048]{2,1,0:T(8,128)(2,1)S(1)}, u32[]{:S(2)}, u32[]{:S(2)}) collective-permute-start(bf16[2,48,2048]{2,1,0:T(8,128)(2,1)S(1)} %shard_map.140.refs_0_), channel_id=1, source_target_pairs={{0,16},{4,20},{8,24},{12,28},{16,0},{20,4},{24,8},{28,12},{1,17},{... | collective-permute-start | bytes 1179656 | tf_op jit(solution)/shard_map/ppermute | solution.py:228
  40.4 12.5 %collective-permute-start.9 = (bf16[2,48,2048]{2,1,0:T(8,128)(2,1)S(1)}, bf16[2,48,2048]{2,1,0:T(8,128)(2,1)S(1)}, u32[]{:S(2)}, u32[]{:S(2)}) collective-permute-start(bf16[2,48,2048]{2,1,0:T(8,128)(2,1)S(1)} %shard_map.140.refs_0_), channel_id=1, source_target_pairs={{0,8},{4,12},{8,0},{12,4},{16,24},{20,28},{24,16},{28,20},{1,9},{5... | collective-permute-start | bytes 1179656 | tf_op jit(solution)/shard_map/ppermute | solution.py:228
  41.9 10.7 %collective-permute-start.12 = (bf16[48,1024]{1,0:T(8,128)(2,1)S(1)}, bf16[48,1024]{1,0:T(8,128)(2,1)S(1)}, u32[]{:S(2)}, u32[]{:S(2)}) collective-permute-start(bf16[48,1024]{1,0:T(8,128)(2,1)S(1)} %get-tuple-element.137), channel_id=1, source_target_pairs={{0,2},{1,3},{2,0},{3,1},{4,6},{5,7},{6,4},{7,5},{8,10},{9,11},{10,... | collective-permute-start | bytes 294920 | tf_op jit(solution)/shard_map/ppermute | solution.py:228
  44.6 8.0 %collective-permute-start.13 = (bf16[48,1024]{1,0:T(8,128)(2,1)S(1)}, bf16[48,1024]{1,0:T(8,128)(2,1)S(1)}, u32[]{:S(2)}, u32[]{:S(2)}) collective-permute-start(bf16[48,1024]{1,0:T(8,128)(2,1)S(1)} %get-tuple-element.138), channel_id=1, source_target_pairs={{0,3},{1,2},{2,1},{3,0},{4,7},{5,6},{6,5},{7,4},{8,11},{9,10},{10,... | collective-permute-start | bytes 294920 | tf_op jit(solution)/shard_map/ppermute | solution.py:228
  52.8 2.8 %collective-permute-start.18 = (bf16[2,48,2048]{2,1,0:T(8,128)(2,1)S(1)}, bf16[2,48,2048]{2,1,0:T(8,128)(2,1)S(1)}, u32[]{:S(2)}, u32[]{:S(2)}) collective-permute-start(bf16[2,48,2048]{2,1,0:T(8,128)(2,1)S(1)} %shard_map.141.own.refs_3_), channel_id=1, source_target_pairs={{0,4},{4,0},{8,12},{12,8},{16,20},{20,16},{24,28},{28,24},{1,5},{5... | collective-permute-start | bytes 1179656 | tf_op jit(solution)/shard_map/ppermute | solution.py:228
  53.0 2.6 %collective-permute-start.16 = (bf16[2,48,2048]{2,1,0:T(8,128)(2,1)S(1)}, bf16[2,48,2048]{2,1,0:T(8,128)(2,1)S(1)}, u32[]{:S(2)}, u32[]{:S(2)}) collective-permute-start(bf16[2,48,2048]{2,1,0:T(8,128)(2,1)S(1)} %collective-permute-done.9.along_x.refs_1_), channel_id=1, source_target_pairs={{0,4},{4,0},{8,12},{12,8},{16,20},{20,16},{24,28},{28,24},{1,5},{5... | collective-permute-start | bytes 1179656 | tf_op jit(solution)/shard_map/ppermute | solution.py:228
  53.5 2.2 %collective-permute-start.17 = (bf16[2,48,2048]{2,1,0:T(8,128)(2,1)S(1)}, bf16[2,48,2048]{2,1,0:T(8,128)(2,1)S(1)}, u32[]{:S(2)}, u32[]{:S(2)}) collective-permute-start(bf16[2,48,2048]{2,1,0:T(8,128)(2,1)S(1)} %collective-permute-done.10.along_y.refs_2_), channel_id=1, source_target_pairs={{0,4},{4,0},{8,12},{12,8},{16,20},{20,16},{24,28},{28,24},{1,5},{5... | collective-permute-start | bytes 1179656 | tf_op jit(solution)/shard_map/ppermute | solution.py:228
  53.6 15.7 %collective-permute-start.15 = (bf16[3,48,2048]{2,1,0:T(8,128)(2,1)S(1)}, bf16[3,48,2048]{2,1,0:T(8,128)(2,1)S(1)}, u32[]{:S(2)}, u32[]{:S(2)}) collective-permute-start(bf16[3,48,2048]{2,1,0:T(8,128)(2,1)S(1)} %get-tuple-element.141), channel_id=1, source_target_pairs={{0,8},{4,12},{8,0},{12,4},{16,24},{20,28},{24,16},{28,20},{1,9},{5... | collective-permute-start | bytes 1769480 | tf_op jit(solution)/shard_map/ppermute | solution.py:228
  54.1 15.4 %collective-permute-start.19 = (bf16[3,48,2048]{2,1,0:T(8,128)(2,1)S(1)}, bf16[3,48,2048]{2,1,0:T(8,128)(2,1)S(1)}, u32[]{:S(2)}, u32[]{:S(2)}) collective-permute-start(bf16[3,48,2048]{2,1,0:T(8,128)(2,1)S(1)} %get-tuple-element.146), channel_id=1, source_target_pairs={{0,16},{4,20},{8,24},{12,28},{16,0},{20,4},{24,8},{28,12},{1,17},{... | collective-permute-start | bytes 1769480 | tf_op jit(solution)/shard_map/ppermute | solution.py:228
  65.6 4.0 %collective-permute-start.20 = (bf16[2,48,2048]{2,1,0:T(8,128)(2,1)S(1)}, bf16[2,48,2048]{2,1,0:T(8,128)(2,1)S(1)}, u32[]{:S(2)}, u32[]{:S(2)}) collective-permute-start(bf16[2,48,2048]{2,1,0:T(8,128)(2,1)S(1)} %get-tuple-element.149), channel_id=1, source_target_pairs={{0,4},{4,0},{8,12},{12,8},{16,20},{20,16},{24,28},{28,24},{1,5},{5... | collective-permute-start | bytes 1179656 | tf_op jit(solution)/shard_map/ppermute | solution.py:228
  65.8 3.8 %collective-permute-start.21 = (bf16[2,48,2048]{2,1,0:T(8,128)(2,1)S(1)}, bf16[2,48,2048]{2,1,0:T(8,128)(2,1)S(1)}, u32[]{:S(2)}, u32[]{:S(2)}) collective-permute-start(bf16[2,48,2048]{2,1,0:T(8,128)(2,1)S(1)} %get-tuple-element.150), channel_id=1, source_target_pairs={{0,4},{4,0},{8,12},{12,8},{16,20},{20,16},{24,28},{28,24},{1,5},{5... | collective-permute-start | bytes 1179656 | tf_op jit(solution)/shard_map/ppermute | solution.py:228
  66.2 3.4 %collective-permute-start.22 = (bf16[2,48,2048]{2,1,0:T(8,128)(2,1)S(1)}, bf16[2,48,2048]{2,1,0:T(8,128)(2,1)S(1)}, u32[]{:S(2)}, u32[]{:S(2)}) collective-permute-start(bf16[2,48,2048]{2,1,0:T(8,128)(2,1)S(1)} %get-tuple-element.151), channel_id=1, source_target_pairs={{0,4},{4,0},{8,12},{12,8},{16,20},{20,16},{24,28},{28,24},{1,5},{5... | collective-permute-start | bytes 1179656 | tf_op jit(solution)/shard_map/ppermute | solution.py:228
  69.9 2.4 %collective-permute-start.23 = (bf16[2,48,2048]{2,1,0:T(8,128)(2,1)S(1)}, bf16[2,48,2048]{2,1,0:T(8,128)(2,1)S(1)}, u32[]{:S(2)}, u32[]{:S(2)}) collective-permute-start(bf16[2,48,2048]{2,1,0:T(8,128)(2,1)S(1)} %get-tuple-element.152.refs_0_), channel_id=1, source_target_pairs={{0,4},{4,0},{8,12},{12,8},{16,20},{20,16},{24,28},{28,24},{1,5},{5... | collective-permute-start | bytes 1179656 | tf_op jit(solution)/shard_map/ppermute | solution.py:228
  70.0 2.4 %collective-permute-start.24 = (bf16[2,48,2048]{2,1,0:T(8,128)(2,1)S(1)}, bf16[2,48,2048]{2,1,0:T(8,128)(2,1)S(1)}, u32[]{:S(2)}, u32[]{:S(2)}) collective-permute-start(bf16[2,48,2048]{2,1,0:T(8,128)(2,1)S(1)} %get-tuple-element.153.refs_1_), channel_id=1, source_target_pairs={{0,4},{4,0},{8,12},{12,8},{16,20},{20,16},{24,28},{28,24},{1,5},{5... | collective-permute-start | bytes 1179656 | tf_op jit(solution)/shard_map/ppermute | solution.py:228
  70.5 2.3 %collective-permute-start.25 = (bf16[2,48,2048]{2,1,0:T(8,128)(2,1)S(1)}, bf16[2,48,2048]{2,1,0:T(8,128)(2,1)S(1)}, u32[]{:S(2)}, u32[]{:S(2)}) collective-permute-start(bf16[2,48,2048]{2,1,0:T(8,128)(2,1)S(1)} %get-tuple-element.154.refs_2_), channel_id=1, source_target_pairs={{0,4},{4,0},{8,12},{12,8},{16,20},{20,16},{24,28},{28,24},{1,5},{5... | collective-permute-start | bytes 1179656 | tf_op jit(solution)/shard_map/ppermute | solution.py:228
  70.6 11.5 %collective-permute-start.26 = (bf16[2,48,2048]{2,1,0:T(8,128)(2,1)S(1)}, bf16[2,48,2048]{2,1,0:T(8,128)(2,1)S(1)}, u32[]{:S(2)}, u32[]{:S(2)}) collective-permute-start(bf16[2,48,2048]{2,1,0:T(8,128)(2,1)S(1)} %get-tuple-element.156), channel_id=1, source_target_pairs={{0,8},{4,12},{8,0},{12,4},{16,24},{20,28},{24,16},{28,20},{1,9},{5... | collective-permute-start | bytes 1179656 | tf_op jit(solution)/shard_map/ppermute | solution.py:228
  72.1 11.2 %collective-permute-start.27 = (bf16[2,48,2048]{2,1,0:T(8,128)(2,1)S(1)}, bf16[2,48,2048]{2,1,0:T(8,128)(2,1)S(1)}, u32[]{:S(2)}, u32[]{:S(2)}) collective-permute-start(bf16[2,48,2048]{2,1,0:T(8,128)(2,1)S(1)} %get-tuple-element.158), channel_id=1, source_target_pairs={{0,16},{4,20},{8,24},{12,28},{16,0},{20,4},{24,8},{28,12},{1,17},{... | collective-permute-start | bytes 1179656 | tf_op jit(solution)/shard_map/ppermute | solution.py:228
  72.4 11.0 %collective-permute-start.29 = (bf16[2,48,2048]{2,1,0:T(8,128)(2,1)S(1)}, bf16[2,48,2048]{2,1,0:T(8,128)(2,1)S(1)}, u32[]{:S(2)}, u32[]{:S(2)}) collective-permute-start(bf16[2,48,2048]{2,1,0:T(8,128)(2,1)S(1)} %get-tuple-element.164), channel_id=1, source_target_pairs={{0,4},{4,0},{8,12},{12,8},{16,20},{20,16},{24,28},{28,24},{1,5},{5... | collective-permute-start | bytes 1179656 | tf_op jit(solution)/shard_map/ppermute | solution.py:228
  80.5 2.9 %collective-permute-start.28 = (bf16[2,48,2048]{2,1,0:T(8,128)(2,1)S(1)}, bf16[2,48,2048]{2,1,0:T(8,128)(2,1)S(1)}, u32[]{:S(2)}, u32[]{:S(2)}) collective-permute-start(bf16[2,48,2048]{2,1,0:T(8,128)(2,1)S(1)} %get-tuple-element.160), channel_id=1, source_target_pairs={{0,4},{4,0},{8,12},{12,8},{16,20},{20,16},{24,28},{28,24},{1,5},{5... | collective-permute-start | bytes 1179656 | tf_op jit(solution)/shard_map/ppermute | solution.py:228
  80.7 2.7 %collective-permute-start.30 = (bf16[2,48,2048]{2,1,0:T(8,128)(2,1)S(1)}, bf16[2,48,2048]{2,1,0:T(8,128)(2,1)S(1)}, u32[]{:S(2)}, u32[]{:S(2)}) collective-permute-start(bf16[2,48,2048]{2,1,0:T(8,128)(2,1)S(1)} %get-tuple-element.165), channel_id=1, source_target_pairs={{0,4},{4,0},{8,12},{12,8},{16,20},{20,16},{24,28},{28,24},{1,5},{5... | collective-permute-start | bytes 1179656 | tf_op jit(solution)/shard_map/ppermute | solution.py:228
  82.0 1.7 %collective-permute-start.31 = (bf16[2,48,2048]{2,1,0:T(8,128)(2,1)S(1)}, bf16[2,48,2048]{2,1,0:T(8,128)(2,1)S(1)}, u32[]{:S(2)}, u32[]{:S(2)}) collective-permute-start(bf16[2,48,2048]{2,1,0:T(8,128)(2,1)S(1)} %get-tuple-element.166), channel_id=1, source_target_pairs={{0,4},{4,0},{8,12},{12,8},{16,20},{20,16},{24,28},{28,24},{1,5},{5... | collective-permute-start | bytes 1179656 | tf_op jit(solution)/shard_map/ppermute | solution.py:228
  83.3 2.7 %collective-permute-start.34 = (bf16[2,48,2048]{2,1,0:T(8,128)(2,1)S(1)}, bf16[2,48,2048]{2,1,0:T(8,128)(2,1)S(1)}, u32[]{:S(2)}, u32[]{:S(2)}) collective-permute-start(bf16[2,48,2048]{2,1,0:T(8,128)(2,1)S(1)} %shard_map.146.refs_0_), channel_id=1, source_target_pairs={{0,4},{4,0},{8,12},{12,8},{16,20},{20,16},{24,28},{28,24},{1,5},{5... | collective-permute-start | bytes 1179656 | tf_op jit(solution)/shard_map/ppermute | solution.py:228
  84.1 11.2 %collective-permute-start.32 = (bf16[2,48,2048]{2,1,0:T(8,128)(2,1)S(1)}, bf16[2,48,2048]{2,1,0:T(8,128)(2,1)S(1)}, u32[]{:S(2)}, u32[]{:S(2)}) collective-permute-start(bf16[2,48,2048]{2,1,0:T(8,128)(2,1)S(1)} %get-tuple-element.168), channel_id=1, source_target_pairs={{0,8},{4,12},{8,0},{12,4},{16,24},{20,28},{24,16},{28,20},{1,9},{5... | collective-permute-start | bytes 1179656 | tf_op jit(solution)/shard_map/ppermute | solution.py:228
  85.7 10.9 %collective-permute-start.33 = (bf16[2,48,2048]{2,1,0:T(8,128)(2,1)S(1)}, bf16[2,48,2048]{2,1,0:T(8,128)(2,1)S(1)}, u32[]{:S(2)}, u32[]{:S(2)}) collective-permute-start(bf16[2,48,2048]{2,1,0:T(8,128)(2,1)S(1)} %get-tuple-element.169), channel_id=1, source_target_pairs={{0,16},{4,20},{8,24},{12,28},{16,0},{20,4},{24,8},{28,12},{1,17},{... | collective-permute-start | bytes 1179656 | tf_op jit(solution)/shard_map/ppermute | solution.py:228
  90.1 1.5 %collective-permute-start.35 = (bf16[48,2048]{1,0:T(8,128)(2,1)S(1)}, bf16[48,2048]{1,0:T(8,128)(2,1)S(1)}, u32[]{:S(2)}, u32[]{:S(2)}) collective-permute-start(bf16[48,2048]{1,0:T(8,128)(2,1)S(1)} %get-tuple-element.174), channel_id=1, source_target_pairs={{0,4},{4,0},{8,12},{12,8},{16,20},{20,16},{24,28},{28,24},{1,5},{5... | collective-permute-start | bytes 589832 | tf_op jit(solution)/shard_map/ppermute | solution.py:228
  90.2 1.7 %collective-permute-start.36 = (bf16[48,2048]{1,0:T(8,128)(2,1)S(1)}, bf16[48,2048]{1,0:T(8,128)(2,1)S(1)}, u32[]{:S(2)}, u32[]{:S(2)}) collective-permute-start(bf16[48,2048]{1,0:T(8,128)(2,1)S(1)} %get-tuple-element.175), channel_id=1, source_target_pairs={{0,4},{4,0},{8,12},{12,8},{16,20},{20,16},{24,28},{28,24},{1,5},{5... | collective-permute-start | bytes 589832 | tf_op jit(solution)/shard_map/ppermute | solution.py:228
  96.7 10.1 %collective-permute-start.38 = (bf16[2,48,2048]{2,1,0:T(8,128)(2,1)S(1)}, bf16[2,48,2048]{2,1,0:T(8,128)(2,1)S(1)}, u32[]{:S(2)}, u32[]{:S(2)}) collective-permute-start(bf16[2,48,2048]{2,1,0:T(8,128)(2,1)S(1)} %get-tuple-element.177), channel_id=1, source_target_pairs={{0,16},{4,20},{8,24},{12,28},{16,0},{20,4},{24,8},{28,12},{1,17},{... | collective-permute-start | bytes 1179656 | tf_op jit(solution)/shard_map/ppermute | solution.py:228
  97.3 9.9 %collective-permute-start.37 = (bf16[2,48,2048]{2,1,0:T(8,128)(2,1)S(1)}, bf16[2,48,2048]{2,1,0:T(8,128)(2,1)S(1)}, u32[]{:S(2)}, u32[]{:S(2)}) collective-permute-start(bf16[2,48,2048]{2,1,0:T(8,128)(2,1)S(1)} %get-tuple-element.176), channel_id=1, source_target_pairs={{0,8},{4,12},{8,0},{12,4},{16,24},{20,28},{24,16},{28,20},{1,9},{5... | collective-permute-start | bytes 1179656 | tf_op jit(solution)/shard_map/ppermute | solution.py:228
  107.3 6.7 %collective-permute-start.40 = (bf16[48,2048]{1,0:T(8,128)(2,1)S(1)}, bf16[48,2048]{1,0:T(8,128)(2,1)S(1)}, u32[]{:S(2)}, u32[]{:S(2)}) collective-permute-start(bf16[48,2048]{1,0:T(8,128)(2,1)S(1)} %get-tuple-element.184), channel_id=1, source_target_pairs={{0,16},{4,20},{8,24},{12,28},{16,0},{20,4},{24,8},{28,12},{1,17},{... | collective-permute-start | bytes 589832 | tf_op jit(solution)/shard_map/ppermute | solution.py:228
  108.7 5.7 %collective-permute-start.39 = (bf16[48,2048]{1,0:T(8,128)(2,1)S(1)}, bf16[48,2048]{1,0:T(8,128)(2,1)S(1)}, u32[]{:S(2)}, u32[]{:S(2)}) collective-permute-start(bf16[48,2048]{1,0:T(8,128)(2,1)S(1)} %get-tuple-element.183), channel_id=1, source_target_pairs={{0,8},{4,12},{8,0},{12,4},{16,24},{20,28},{24,16},{28,20},{1,9},{5... | collective-permute-start | bytes 589832 | tf_op jit(solution)/shard_map/ppermute | solution.py:228
  109.6 8.3 %collective-permute-start.44 = (bf16[48,1024]{1,0:T(8,128)(2,1)S(1)}, bf16[48,1024]{1,0:T(8,128)(2,1)S(1)}, u32[]{:S(2)}, u32[]{:S(2)}) collective-permute-start(bf16[48,1024]{1,0:T(8,128)(2,1)S(1)} %get-tuple-element.193), channel_id=1, source_target_pairs={{0,1},{1,0},{2,3},{3,2},{4,5},{5,4},{6,7},{7,6},{8,9},{9,8},{10,11... | collective-permute-start | bytes 294920 | tf_op jit(solution)/shard_map/ppermute | solution.py:228
  111.4 10.8 %collective-permute-start.45 = (bf16[48,1024]{1,0:T(8,128)(2,1)S(1)}, bf16[48,1024]{1,0:T(8,128)(2,1)S(1)}, u32[]{:S(2)}, u32[]{:S(2)}) collective-permute-start(bf16[48,1024]{1,0:T(8,128)(2,1)S(1)} %get-tuple-element.194), channel_id=1, source_target_pairs={{0,2},{1,3},{2,0},{3,1},{4,6},{5,7},{6,4},{7,5},{8,10},{9,11},{10,... | collective-permute-start | bytes 294920 | tf_op jit(solution)/shard_map/ppermute | solution.py:228
  112.8 9.4 %collective-permute-start.46 = (bf16[48,1024]{1,0:T(8,128)(2,1)S(1)}, bf16[48,1024]{1,0:T(8,128)(2,1)S(1)}, u32[]{:S(2)}, u32[]{:S(2)}) collective-permute-start(bf16[48,1024]{1,0:T(8,128)(2,1)S(1)} %get-tuple-element.195), channel_id=1, source_target_pairs={{0,3},{1,2},{2,1},{3,0},{4,7},{5,6},{6,5},{7,4},{8,11},{9,10},{10,... | collective-permute-start | bytes 294920 | tf_op jit(solution)/shard_map/ppermute | solution.py:228
  114.7 7.9 %collective-permute-start.41 = (bf16[48,1024]{1,0:T(8,128)(2,1)S(1)}, bf16[48,1024]{1,0:T(8,128)(2,1)S(1)}, u32[]{:S(2)}, u32[]{:S(2)}) collective-permute-start(bf16[48,1024]{1,0:T(8,128)(2,1)S(1)} %get-tuple-element.186), channel_id=1, source_target_pairs={{0,1},{1,0},{2,3},{3,2},{4,5},{5,4},{6,7},{7,6},{8,9},{9,8},{10,11... | collective-permute-start | bytes 294920 | tf_op jit(solution)/shard_map/ppermute | solution.py:228
  116.5 11.3 %collective-permute-start.42 = (bf16[48,1024]{1,0:T(8,128)(2,1)S(1)}, bf16[48,1024]{1,0:T(8,128)(2,1)S(1)}, u32[]{:S(2)}, u32[]{:S(2)}) collective-permute-start(bf16[48,1024]{1,0:T(8,128)(2,1)S(1)} %get-tuple-element.187), channel_id=1, source_target_pairs={{0,2},{1,3},{2,0},{3,1},{4,6},{5,7},{6,4},{7,5},{8,10},{9,11},{10,... | collective-permute-start | bytes 294920 | tf_op jit(solution)/shard_map/ppermute | solution.py:228
  117.9 9.8 %collective-permute-start.43 = (bf16[48,1024]{1,0:T(8,128)(2,1)S(1)}, bf16[48,1024]{1,0:T(8,128)(2,1)S(1)}, u32[]{:S(2)}, u32[]{:S(2)}) collective-permute-start(bf16[48,1024]{1,0:T(8,128)(2,1)S(1)} %get-tuple-element.188), channel_id=1, source_target_pairs={{0,3},{1,2},{2,1},{3,0},{4,7},{5,6},{6,5},{7,4},{8,11},{9,10},{10,... | collective-permute-start | bytes 294920 | tf_op jit(solution)/shard_map/ppermute | solution.py:228
